TPU v7x, 32 devices: a whole 2x2x4 slice. The times are simulated.
32 devices in a mesh: row: 8 (over z, x), col: 4 (over y, core).
Axes of the slice: x: 2, y: 2, z: 4, core: 2. Of those that a mesh axis runs over, the one named last changes fastest.
Arguments:
- density: float32 [3, 524288], P(None, ('row', 'col')), may hold values from -6 to 6
- interp_weight: float32 [27, 524288], P(None, ('row', 'col')), may hold values from -1.2 to 1.2
- proj_weight: float32 [27, 524288], P(None, ('row', 'col')), may hold values from -1.2 to 1.2
- stencil_corner: int32 [3, 4096], P(None, ('row', 'col')), may hold values from 0 to 253, as said below
- near_tiles: bfloat16 [384, 3, 3, 128, 128], P(('row', 'col')), may hold values from -0.1875 to 0.1875
- pair_target: int32 [384], P(('row', 'col')), may hold values from 0 to 127
- pair_landing: int32 [384], P(('row', 'col')), may hold values from 0 to 127
- pair_count: int32 [32], P(('row', 'col')), may hold values from 4 to 12, as said below
Outputs:
- traction_adjoint: float32 [3, 524288], P(None, ('row', 'col'))
Inputs may be any that keep to these rules, and one draw needn't show every extreme that they name: `stencil_corner`: the stencil of a cluster held by the device with row index r and col index c lies in cells r * 32 to r * 32 + 31 of the first dimension and c * 64 to c * 64 + 63 of the second; every stencil lies inside the grid. `pair_count`: slots at or beyond a device's count are padding; the most is reached on some device in every draw.
All inputs are finite; a program needn't handle non-finite values.
Results may differ from a plain program's by a relative error of at most 0.0003.
Values sent between devices are 32-bit elements; how exact they have to be, the bound alone decides.
No kernel may reach another device: no remote copies, remote signals or barrier semaphores. Data moves between devices by JAX's collectives and lax.ppermute only.
A program may use at most 128 MiB of HBM per device.

v0:
```python
import math

import jax
import jax.numpy as jnp
from jax import lax
from jax.sharding import PartitionSpec as P

G = 256
STENCIL = 27


precise = lax.Precision.HIGHEST
screen_shift = 0.5


def padded(cells, sides, width):
    for axis, dim in sides:
        count = lax.axis_size(axis)
        head = lax.slice_in_dim(cells, 0, width, axis=dim)
        tail = lax.slice_in_dim(cells, cells.shape[dim] - width, cells.shape[dim], axis=dim)
        cells = jnp.concatenate(
            [
                lax.ppermute(tail, axis, [(i, (i + 1) % count) for i in range(count)]),
                cells,
                lax.ppermute(head, axis, [((i + 1) % count, i) for i in range(count)]),
            ],
            axis=dim,
        )
    return cells


def tables(rows_count, cols_count, length):
    row_indices = jnp.arange(rows_count, dtype=jnp.int32)
    col_indices = jnp.arange(cols_count, dtype=jnp.int32)
    product = row_indices[:, None] * col_indices[None, :] % length
    angles = product.astype(jnp.float32) * (2.0 * math.pi / length)
    return (jnp.cos(angles), jnp.sin(angles))


def complex_table(length, direction):
    cosines, sines = tables(length, length, length)
    from_real = jnp.stack([cosines, direction * sines], axis=1)
    from_imag = jnp.stack([-direction * sines, cosines], axis=1)
    return jnp.stack([from_real, from_imag], axis=0)


def wavenumbers(count, offset, length):
    indices = offset + jnp.arange(count, dtype=jnp.int32)
    wave_values = jnp.where(indices < length // 2, indices, indices - length).astype(jnp.float32)
    keep_mask = (indices != length // 2).astype(jnp.float32)
    return (wave_values, keep_mask)


def placed_along(pair, position):
    shape = [1, 1, 1, 1]
    shape[position] = -1
    return tuple((member.reshape(shape) for member in pair))


def project(spectral, xpair, ypair, zpair, factor):
    kfirst, keep_first = xpair
    ksecond, keep_second = ypair
    kthird, keep_third = zpair
    squared = kfirst * kfirst + ksecond * ksecond + kthird * kthird
    weighting = factor * keep_first * keep_second * keep_third / (squared + screen_shift)
    floor_sq = jnp.maximum(squared, 1.0)
    inner_sum = (kfirst * spectral[0] + ksecond * spectral[1] + kthird * spectral[2]) / floor_sq
    stacked = jnp.stack(
        [
            spectral[0] - kfirst * inner_sum,
            spectral[1] - ksecond * inner_sum,
            spectral[2] - kthird * inner_sum,
        ]
    )
    return stacked * weighting


def per_device(
    density,
    interp_weight,
    proj_weight,
    stencil_corner,
    near_tiles,
    pair_target,
    pair_landing,
    pair_count,
):
    clusters = stencil_corner.shape[1]
    panels = density.shape[1] // clusters
    rows_total = lax.axis_size("row")
    cols_total = lax.axis_size("col")
    row_index = lax.axis_index("row")
    col_index = lax.axis_index("col")
    slab_first = G // rows_total
    slab_second = G // cols_total
    charges = density.reshape(3, clusters, panels)
    weights_in = interp_weight.reshape(STENCIL, clusters, panels)
    weights_out = proj_weight.reshape(STENCIL, clusters, panels)
    offsets = jnp.arange(STENCIL, dtype=jnp.int32)
    local_first = stencil_corner[0] - row_index * slab_first
    local_second = stencil_corner[1] - col_index * slab_second
    cell_index = (
        (
            (local_first[:, None] + offsets // 9) * slab_second
            + local_second[:, None]
            + offsets // 3 % 3
        )
        * G
        + stencil_corner[2][:, None]
        + offsets % 3
    )
    spread = jnp.einsum("ckp,skp->cks", charges, weights_in, precision=precise)
    flat_grid = (
        jnp.zeros((3, slab_first * slab_second * G), jnp.float32)
        .at[:, cell_index.reshape(-1)]
        .add(spread.reshape(3, -1))
    )
    charge_field = flat_grid.reshape(3, slab_first, slab_second, G)
    kept_bins = G // 2
    fold_weight = jnp.where(jnp.arange(kept_bins, dtype=jnp.int32) == 0, 1.0, 2.0).astype(
        jnp.float32
    )
    forward_cos, forward_sin = tables(G, kept_bins, G)
    forward_real = jnp.stack([forward_cos, -forward_sin], axis=1)
    back_cos, back_sin = tables(kept_bins, G, G)
    back_real = jnp.stack(
        [back_cos * fold_weight[:, None], -back_sin * fold_weight[:, None]], axis=0
    )
    forward_full = complex_table(G, -1.0)
    backward_full = complex_table(G, 1.0)
    factor = 1.0 / math.sqrt(density.shape[1] * rows_total * cols_total)
    spectral = jnp.einsum("cxyz,zpk->ckxpy", charge_field, forward_real, precision=precise)
    spectral = lax.all_to_all(spectral, "col", split_axis=1, concat_axis=4, tiled=True)
    spectral = jnp.einsum("ckxpy,pyqm->ckmqx", spectral, forward_full, precision=precise)
    spectral = lax.all_to_all(spectral, "row", split_axis=2, concat_axis=4, tiled=True)
    spectral = jnp.einsum("ckmpx,pxqn->ckmqn", spectral, forward_full, precision=precise)
    bins_local = spectral.shape[1]
    second_local = spectral.shape[2]
    zpair = placed_along(wavenumbers(bins_local, col_index * bins_local, G), 0)
    ypair = placed_along(wavenumbers(second_local, row_index * second_local, G), 1)
    xpair = placed_along(wavenumbers(G, 0, G), 3)
    spectral = project(spectral, xpair, ypair, zpair, factor)
    spectral = jnp.einsum("ckmpn,pnqx->ckmqx", spectral, backward_full, precision=precise)
    spectral = lax.all_to_all(spectral, "row", split_axis=4, concat_axis=2, tiled=True)
    spectral = jnp.einsum("ckmpx,pmqy->ckxqy", spectral, backward_full, precision=precise)
    spectral = lax.all_to_all(spectral, "col", split_axis=4, concat_axis=1, tiled=True)
    potential = jnp.einsum("ckxpy,pkz->cxyz", spectral, back_real, precision=precise)
    sampled = potential.reshape(3, -1)[:, cell_index]
    far_term = jnp.einsum("cks,skp->ckp", sampled, weights_out, precision=precise)
    rounded = charges.astype(jnp.bfloat16)
    slot_total = pair_target.shape[0]
    slot_group = slot_total // 3
    live_count = pair_count[0]
    picked = rounded[:, pair_target, :]
    partial_value = jnp.einsum(
        "qabij,aqi->qbj", near_tiles, picked, preferred_element_type=jnp.float32
    )
    live_mask = jnp.arange(slot_total, dtype=jnp.int32) < live_count
    partial_value = jnp.where(
        live_mask[:, None, None], partial_value, jnp.zeros_like(partial_value)
    )
    leaving = partial_value[slot_group:].reshape(slot_group, 2, 3, panels)
    arrived = padded(leaving, (("row", 1),), 1)
    crossing = jnp.stack([arrived[:, 3], arrived[:, 0]], axis=1).reshape(2 * slot_group, 3, panels)
    incoming = jnp.concatenate([partial_value[:slot_group], crossing], axis=0)
    landing_hot = (pair_landing[:, None] == jnp.arange(clusters, dtype=jnp.int32)[None, :]).astype(
        jnp.float32
    )
    near_term = jnp.einsum("qk,qbj->bkj", landing_hot, incoming, precision=precise)
    return (far_term + near_term).reshape(3, -1)


def solution(mesh):
    in_specs = (
        P(None, ("row", "col")),
        P(None, ("row", "col")),
        P(None, ("row", "col")),
        P(None, ("row", "col")),
        P(("row", "col"), None, None, None, None),
        P(("row", "col")),
        P(("row", "col")),
        P(("row", "col")),
    )
    out_specs = P(None, ("row", "col"))
    return jax.shard_map(
        per_device, mesh=mesh, in_specs=in_specs, out_specs=out_specs, check_vma=False
    )
```

profile of v0, /device:TPU:0, one launch (start us, length us, event | category | flops | bytes accessed | tf_op | source)
XLA Modules:
  0.0 1524.1 jit_solution(8383795270087452262)
XLA Ops:
  1.0 1.3 sine_negate_fusion
  5.1 1.7 reshape.738
  7.6 2.0 copy.95
  9.7 4.2 fusion.26
  14.6 1.8 reshape.756
  16.4 4.0 broadcast_in_dim.19
  20.4 385.2 %scatter_fusion = f32[3,524288]{1,0:T(4,128)} fusion(f32[3,524288]{1,0:T(4,128)} %broadcast_in_dim.19, s32[3456]{0:T(1024)S(1)} %fusion.78, f32[3456,3]{0,1:T(4,128)} %bitcast.187), kind=kCustom, calls=%fused_computation.2 | custom fusion | flops 10368 | bytes 138240 | tf_op jit(solution)/shard_map/scatter-add | solution.py:116
  405.6 4.6 copy.96
  410.3 7.0 convolution_bitcast_fusion.1
  417.3 12.7 copy.57
  430.0 11.5 reshape.788
  441.5 5.5 all-to-all-start
  447.0 1.0 fusion.69
  448.0 1.0 broadcast_multiply_fusion
  448.9 1.4 fusion.44
  450.4 67.5 %all-to-all-done = f32[4,1,393216]{2,1,0:T(1,128)} async-done(((f32[4,1,393216]{2,1,0:T(1,128)}), f32[4,1,393216]{2,1,0:T(1,128)}, u32[]{:S(2)}, u32[]{:S(2)}) %all-to-all-start) | async-done | bytes 6291488 | tf_op jit(solution)/shard_map/all_to_all | solution.py:133
  518.5 20.9 %reduce.2 = f32[4,393216]{1,0:T(4,128)} reduce(f32[4,1,393216]{2,1,0:T(1,128)} %all-to-all-done, f32[]{:T(128)} %broadcast.874), dimensions={1}, to_apply=%all_to_all.52.reduce_sub_computation | reduce | bytes 12582916 | tf_op jit(solution)/shard_map/all_to_all | solution.py:133
  539.4 13.0 reshape.789
  552.4 17.0 %copy.59 = f32[3,32,32,2,4,64]{5,4,2,3,1,0:T(4,128)} copy(f32[3,32,32,2,4,64]{5,2,0,3,1,4:T(8,128)} %bitcast.178) | data formatting | bytes 12582912 | tf_op jit(solution)/shard_map/all_to_all | solution.py:133
  569.4 12.4 reshape.768
  581.8 13.7 convolution_bitcast_fusion
  595.5 20.4 %copy.60 = f32[3,32,256,2,32]{4,1,0,3,2:T(8,128)} copy(f32[3,32,256,2,32]{2,4,1,0,3:T(8,128)} %convolution_bitcast_fusion) | data formatting | bytes 12582912 | tf_op jit(solution)/shard_map/ckxpy,pyqm->ckmqx/transpose | solution.py:134
  615.9 16.7 %reshape.790 = f32[8,1,196608]{2,1,0:T(1,128)} reshape(f32[256,2,3,32,32]{4,3,2,1,0:T(8,128)} %bitcast.173) | data formatting | bytes 12582912
  632.6 7.1 all-to-all-start.1
  639.9 1.5 fusion.38
  641.4 136.1 %all-to-all-done.1 = f32[8,1,196608]{2,1,0:T(1,128)} async-done(((f32[8,1,196608]{2,1,0:T(1,128)}), f32[8,1,196608]{2,1,0:T(1,128)}, u32[]{:S(2)}, u32[]{:S(2)}) %all-to-all-start.1) | async-done | bytes 6291488 | tf_op jit(solution)/shard_map/all_to_all | solution.py:135
  777.6 19.5 %reduce.3 = f32[8,196608]{1,0:T(8,128)} reduce(f32[8,1,196608]{2,1,0:T(1,128)} %all-to-all-done.1, f32[]{:T(128)} %broadcast.874), dimensions={1}, to_apply=%all_to_all.56.reduce_sub_computation | reduce | bytes 12582916 | tf_op jit(solution)/shard_map/all_to_all | solution.py:135
  797.1 19.2 %reshape.791 = f32[256,2,3,32,32]{4,3,2,1,0:T(8,128)} reshape(f32[8,196608]{1,0:T(8,128)} %reduce.3) | data formatting | bytes 12582912
  816.3 25.1 %copy.121 = f32[3,32,8,32,2,32]{5,2,3,4,1,0:T(8,128)} copy(f32[3,32,8,32,2,32]{5,1,0,4,3,2:T(8,128)} %bitcast.168) | data formatting | bytes 12582912 | tf_op jit(solution)/shard_map/all_to_all | solution.py:135
  841.4 17.9 %reshape.770 = f32[3,32,32,2,256,1]{4,2,3,1,0,5:T(8,128)} reshape(f32[3,32,32,2,8,32]{5,4,2,3,1,0:T(8,128)} %bitcast.169) | data formatting | bytes 12582912 | tf_op jit(solution)/shard_map/all_to_all | solution.py:135
  859.3 13.3 fusion.16
  872.6 1.4 multiply_subtract_fusion.2
  874.1 1.0 multiply_subtract_fusion.1
  875.6 12.6 fusion.13
  888.3 30.6 %copy.63 = f32[3,32,32,2,256]{2,3,1,0,4:T(2,128)} copy(f32[3,32,32,2,256]{4,2,3,1,0:T(8,128)} %fusion.13) | data formatting | bytes 12582912 | tf_op jit(solution)/shard_map/ckmpn,pnqx->ckmqx/dot_general | solution.py:143
  918.9 27.1 %reshape.792 = f32[8,1,196608]{2,1,0:T(1,128)} reshape(f32[256,3,32,2,32]{4,3,2,1,0:T(2,128)} %bitcast.174) | data formatting | bytes 12582912
  946.0 142.3 %all_to_all.72 = f32[8,1,196608]{2,1,0:T(1,128)} all-to-all(f32[8,1,196608]{2,1,0:T(1,128)} %reshape.792), channel_id=1, replica_groups=mesh['row'=8,'col'=4] {'row'}, dimensions={0} | all-to-all | bytes 12582912 | tf_op jit(solution)/shard_map/all_to_all | solution.py:144
  1088.3 19.7 %reduce.4 = f32[8,196608]{1,0:T(8,128)} reduce(f32[8,1,196608]{2,1,0:T(1,128)} %all_to_all.72, f32[]{:T(128)} %broadcast.874), dimensions={1}, to_apply=%all_to_all.60.reduce_sub_computation | reduce | bytes 12582916 | tf_op jit(solution)/shard_map/all_to_all | solution.py:144
  1108.0 39.7 %reshape.793 = f32[256,3,32,2,32]{4,3,2,1,0:T(2,128)} reshape(f32[8,196608]{1,0:T(8,128)} %reduce.4) | data formatting | bytes 12582912
  1147.8 24.9 %copy.120 = f32[3,32,32,2,8,32]{2,4,5,3,1,0:T(8,128)} copy(f32[3,32,32,2,8,32]{2,3,1,0,5,4:T(2,128)} %bitcast.170) | data formatting | bytes 12582912 | tf_op jit(solution)/shard_map/all_to_all | solution.py:144
  1172.6 18.1 %reshape.775 = f32[3,32,256,2,32,1]{2,4,3,1,0,5:T(8,128)} reshape(f32[3,32,8,32,2,32]{3,2,5,4,1,0:T(8,128)} %bitcast.171) | data formatting | bytes 12582912 | tf_op jit(solution)/shard_map/all_to_all | solution.py:144
  1190.7 13.5 fusion.19
  1204.2 30.6 %copy.66 = f32[3,32,32,2,256]{2,3,1,0,4:T(2,128)} copy(f32[3,32,32,2,256]{4,2,3,1,0:T(8,128)} %fusion.19) | data formatting | bytes 12582912 | tf_op jit(solution)/shard_map/ckmpx,pmqy->ckxqy/dot_general | solution.py:145
  1234.9 39.9 %reshape.794 = f32[4,1,393216]{2,1,0:T(1,128)} reshape(f32[256,3,32,2,32]{4,3,2,1,0:T(2,128)} %bitcast.175) | data formatting | bytes 12582912
  1274.7 5.4 all-to-all-start.3
  1280.8 1.7 bitcast_convert_fusion
  1282.5 1.5 gather_fusion.1
  1285.9 2.7 collective-permute-start
  1288.6 1.4 compare_select_fusion
  1290.1 1.6 reshape.741
  1291.7 1.3 cosine_multiply_fusion
  1294.4 2.0 copy.98
  1296.4 1.3 slice.55
  1298.5 1.0 fusion.73
  1299.5 1.8 copy.71
  1301.3 49.5 %all-to-all-done.3 = f32[4,1,393216]{2,1,0:T(1,128)} async-done(((f32[4,1,393216]{2,1,0:T(1,128)}), f32[4,1,393216]{2,1,0:T(1,128)}, u32[]{:S(2)}, u32[]{:S(2)}) %all-to-all-start.3) | async-done | bytes 6291488 | tf_op jit(solution)/shard_map/all_to_all | solution.py:146
  1350.8 21.4 %reduce.5 = f32[4,393216]{1,0:T(4,128)} reduce(f32[4,1,393216]{2,1,0:T(1,128)} %all-to-all-done.3, f32[]{:T(128)} %broadcast.874), dimensions={1}, to_apply=%all_to_all.64.reduce_sub_computation | reduce | bytes 12582916 | tf_op jit(solution)/shard_map/all_to_all | solution.py:146
  1372.2 47.1 %reshape.795 = f32[256,3,32,2,32]{4,3,2,1,0:T(2,128)} reshape(f32[4,393216]{1,0:T(4,128)} %reduce.5) | data formatting | bytes 12582912
  1419.3 36.5 %copy.94 = f32[3,32,32,2,4,64]{5,1,4,3,2,0:T(8,128)} copy(f32[3,32,32,2,4,64]{2,3,1,0,5,4:T(2,128)} %bitcast.172) | data formatting | bytes 12582912 | tf_op jit(solution)/shard_map/all_to_all | solution.py:146
  1455.8 23.1 %fusion.50 = f32[3,32,64,256,1]{3,2,4,1,0:T(8,128)S(1)} fusion(f32[3,128,32,2,64]{4,1,3,2,0:T(8,128)} %bitcast.179, f32[1,128,256]{2,1,0:T(8,128)} %get-tuple-element.23, f32[1,128,256]{2,1,0:T(8,128)} %get-tuple-element.22), kind=kOutput, calls=%fused_computation.61 | convolution fusion | flops 4831903744 | bytes 12845056 | tf_op jit(solution)/shard_map/ckxpy,pkz->cxyz/dot_general | solution.py:147
  1478.9 15.6 %copy.97 = f32[1,3,2048,256]{3,1,2,0:T(4,128)} copy(f32[1,3,2048,256]{3,2,1,0:T(8,128)S(1)} %bitcast.181) | data formatting | bytes 12582912
  1494.5 22.6 %gather_fusion = f32[3456,3]{0,1:T(4,128)} fusion(f32[3,524288]{1,0:T(4,128)} %bitcast.167, s32[4096]{0:T(1024)S(1)} %pad_clamp_fusion), kind=kCustom, calls=%fused_computation | custom fusion | bytes 96768 | tf_op jit(solution)/shard_map/gather | solution.py:148
  1517.1 1.7 reshape.744
  1518.8 5.1 fusion.35
  (60 shorter events, 10.8 us)
Async XLA Ops:
  0.0 1284.0 %copy-start = (bf16[12,3,3,128,128]{4,3,2,1,0:T(8,128)(2,1)S(1)}, bf16[12,3,3,128,128]{4,3,2,1,0:T(8,128)(2,1)}, u32[]{:S(2)}) copy-start(bf16[12,3,3,128,128]{4,3,2,1,0:T(8,128)(2,1)} %param.12) | copy-start | bytes 10616836
  3.1 0.6 copy-start.9
  3.1 0.6 copy-start.10
  3.1 0.6 copy-start.11
  6.7 3.0 copy-start.4
  405.6 4.6 copy-start.6
  405.6 4.7 copy-start.7
  441.5 76.4 %all-to-all-start = ((f32[4,1,393216]{2,1,0:T(1,128)}), f32[4,1,393216]{2,1,0:T(1,128)}, u32[]{:S(2)}, u32[]{:S(2)}) async-start(f32[4,1,393216]{2,1,0:T(1,128)} %reshape.788), calls=%async_computation | async-start | bytes 12582912 | tf_op jit(solution)/shard_map/all_to_all | solution.py:133
  632.6 145.0 %all-to-all-start.1 = ((f32[8,1,196608]{2,1,0:T(1,128)}), f32[8,1,196608]{2,1,0:T(1,128)}, u32[]{:S(2)}, u32[]{:S(2)}) async-start(f32[8,1,196608]{2,1,0:T(1,128)} %reshape.790), calls=%async_computation.1 | async-start | bytes 12582912 | tf_op jit(solution)/shard_map/all_to_all | solution.py:135
  859.3 13.3 copy-start.1
  874.1 1.1 copy-start.2
  874.1 1.2 copy-start.3
  874.1 1.5 copy-start.5
  1274.7 6.1 copy-start.13
  1274.7 76.1 %all-to-all-start.3 = ((f32[4,1,393216]{2,1,0:T(1,128)}), f32[4,1,393216]{2,1,0:T(1,128)}, u32[]{:S(2)}, u32[]{:S(2)}) async-start(f32[4,1,393216]{2,1,0:T(1,128)} %reshape.794), calls=%async_computation.3 | async-start | bytes 12582912 | tf_op jit(solution)/shard_map/all_to_all | solution.py:146
  1284.7 0.6 copy-start.8
  1285.9 11.8 collective-permute-start
  1288.6 9.1 collective-permute-start.1
  1291.7 6.8 copy-start.12
where the time goes:
time: 1540 us; the launch traced here: 1520 us
  local copies, waits for them, and re-layouts  528 us (34%)
  other arithmetic  485 us (31%)
  waiting for transfers between devices  253 us (16%)
  blocking collectives  142 us (9%)
  matrix products  94.1 us (6%)
  starting transfers between devices  20.7 us (1%)
    scatter-add x1, other arithmetic, per_device(): flat_grid = jnp.zeros((3, slab_first * slab_second * G), jnp.float32).at[...  385 us
    unnamed x40, local copies, waits for them, and re-layouts  240 us
    all_to_all x1, blocking collectives, per_device(): lax.all_to_all(spectral, 'row', split_axis=4, concat_axis=2, tiled=True)  142 us
    all_to_all x1, waiting for transfers between devices, per_device(): lax.all_to_all(spectral, 'row', split_axis=2, concat_axis=4, tiled=True)  136 us
    all_to_all x1, waiting for transfers between devices, per_device(): lax.all_to_all(spectral, 'col', split_axis=1, concat_axis=4, tiled=True)  67.5 us
    all_to_all x1, waiting for transfers between devices, per_device(): lax.all_to_all(spectral, 'col', split_axis=4, concat_axis=1, tiled=True)  49.5 us
    all_to_all x2, local copies, waits for them, and re-layouts, per_device(): lax.all_to_all(spectral, 'row', split_axis=2, concat_axis=4, tiled=True)  43 us
    all_to_all x2, local copies, waits for them, and re-layouts, per_device(): lax.all_to_all(spectral, 'row', split_axis=4, concat_axis=2, tiled=True)  42.9 us
  transfers between devices with their start and end apart: 5, of which 3 were waited for; matrix products, arithmetic and copies ran while one was open for 1% of the time, Pallas kernels for 0%

commit v1 on v0

v1 whole, which is shorter than its diff:
```python
import math

import jax
import jax.numpy as jnp
import numpy as np
from jax import lax
from jax.experimental import pallas as pl
from jax.experimental.pallas import tpu as pltpu
from jax.sharding import PartitionSpec as P

G = 256
HALF = G // 2
STENCIL = 27
SIDE = 3
AXES = ("row", "col")

precise = lax.Precision.HIGHEST
screen_shift = 0.5


def padded(cells, sides, width):
    for axis, dim in sides:
        count = lax.axis_size(axis)
        head = lax.slice_in_dim(cells, 0, width, axis=dim)
        tail = lax.slice_in_dim(cells, cells.shape[dim] - width, cells.shape[dim], axis=dim)
        cells = jnp.concatenate(
            [
                lax.ppermute(tail, axis, [(i, (i + 1) % count) for i in range(count)]),
                cells,
                lax.ppermute(head, axis, [((i + 1) % count, i) for i in range(count)]),
            ],
            axis=dim,
        )
    return cells


def near_field(charges, near_tiles, pair_target, pair_landing, pair_count):
    clusters, panels = charges.shape[1:]
    rounded = charges.astype(jnp.bfloat16)
    slot_total = pair_target.shape[0]
    slot_group = slot_total // 3
    picked = rounded[:, pair_target, :]
    partial_value = jnp.einsum(
        "qabij,aqi->qbj", near_tiles, picked, preferred_element_type=jnp.float32
    )
    live_mask = jnp.arange(slot_total, dtype=jnp.int32) < pair_count[0]
    partial_value = jnp.where(
        live_mask[:, None, None], partial_value, jnp.zeros_like(partial_value)
    )
    leaving = partial_value[slot_group:].reshape(slot_group, 2, 3, panels)
    arrived = padded(leaving, (("row", 1),), 1)
    crossing = jnp.stack([arrived[:, 3], arrived[:, 0]], axis=1).reshape(2 * slot_group, 3, panels)
    incoming = jnp.concatenate([partial_value[:slot_group], crossing], axis=0)
    landing_hot = (pair_landing[:, None] == jnp.arange(clusters, dtype=jnp.int32)[None, :]).astype(
        jnp.float32
    )
    return jnp.einsum("qk,qbj->bkj", landing_hot, incoming, precision=precise)


def half_tables():
    cells = np.arange(HALF)
    parts = []
    for parity in range(2):
        product = cells[:, None] * (2 * cells[None, :] + parity) % G
        angles = product * (2.0 * np.pi / G)
        cosines, sines = np.cos(angles), np.sin(angles)
        table = np.block([[cosines, -sines], [sines, cosines]]).astype(np.float32)
        high = table.astype(jnp.bfloat16)
        low = (table - high.astype(np.float32)).astype(jnp.bfloat16)
        parts.append(np.stack([high, low]))
    return np.stack(parts)


def split(values):
    high = values.astype(jnp.bfloat16)
    low = (values - high.astype(jnp.float32)).astype(jnp.bfloat16)
    return high, low


def dot(left, right):
    return jnp.dot(left, right, preferred_element_type=jnp.float32)


def three_pass(left_high, left_low, right_high, right_low):
    return (
        dot(left_high, right_low) + dot(left_low, right_high) + dot(left_high, right_high)
    )


def scatter_kernel(cols, stencils, phases, out, spread, hot, total):
    parts, slab, _ = out.shape
    clusters = stencils.shape[2]
    corner = pl.program_id(0) * slab

    def block(c, carry):
        first = stencils[c, 3 * STENCIL : 3 * STENCIL + 1, :] - corner.astype(jnp.float32)
        second = stencils[c, 3 * STENCIL + 1 : 3 * STENCIL + 2, :]
        rows = lax.broadcasted_iota(jnp.int32, (G, clusters), 0).astype(jnp.float32)
        first_wide = jnp.broadcast_to(first, (2 * parts, clusters)).astype(jnp.bfloat16)
        for y in range(SIDE):
            lanes = pl.ds(pl.multiple_of((c * SIDE + y) * clusters, clusters), clusters)
            hot[:, lanes] = jnp.where(rows == second + y, 1.0, 0.0).astype(jnp.bfloat16)
            tiles = []
            for x in range(SIDE):
                modes = []
                for a in range(3):
                    at = a * STENCIL + x * 9 + y * 3
                    modes.append(
                        sum(stencils[c, at + z : at + z + 1, :] * phases[c, z] for z in range(SIDE))
                    )
                modes = jnp.concatenate(modes, axis=0)
                low = modes - modes.astype(jnp.bfloat16).astype(jnp.float32)
                tiles.append(jnp.concatenate([modes, low], axis=0).astype(jnp.bfloat16))
            blank = jnp.zeros_like(tiles[0])
            for cell in range(slab):
                value = blank
                for x in range(SIDE):
                    value = jnp.where(
                        first_wide == jnp.asarray(cell - x, jnp.bfloat16), tiles[x], value
                    )
                spread[cell, :, lanes] = value
        return carry

    lax.fori_loop(0, cols, block, 0)
    result = lax.dot_general(
        spread[...].reshape(slab * 2 * parts, hot.shape[1]),
        hot[...],
        (((1,), (1,)), ((), ())),
        preferred_element_type=jnp.float32,
    )
    for side in range(2):
        total[side] = result[:, side * HALF : (side + 1) * HALF]
    for side in range(2):
        for v in range(parts):
            out[v, :, side * HALF : (side + 1) * HALF] = (
                total[side, pl.ds(v, slab, stride=2 * parts), :]
                + total[side, pl.ds(parts + v, slab, stride=2 * parts), :]
            )


def dft_kernel(signs, thirds, field, tx, txt, ty, tyt, out, lines, modes, high, low):
    pars = ty.shape[0]
    width = pars * HALF

    def stage(values, at):
        high[at], low[at] = split(values)

    for p in range(pars):
        for a in range(3):
            for part in range(2):
                stage(
                    field[a, 0, part, :, :HALF] + signs[p] * field[a, 0, part, :, HALF:],
                    (slice(a * G, (a + 1) * G), slice(part * HALF, (part + 1) * HALF)),
                )
        for a in range(3):
            rows = slice(a * G, (a + 1) * G)
            result = three_pass(high[rows], low[rows], ty[p, 0], ty[p, 1])
            for part in range(2):
                lines[a, part, :, p * HALF : (p + 1) * HALF] = result[
                    :, part * HALF : (part + 1) * HALF
                ]
    for a in range(3):
        for q in range(2):
            rows = slice((2 * a + q) % 3 * G, ((2 * a + q) % 3 + 1) * G)
            for part in range(2):
                top, bottom = lines[a, part, :HALF], lines[a, part, HALF:]
                at = rows.start + part * HALF
                stage(top - bottom if q else top + bottom, (slice(at, at + HALF), slice(0, width)))
            result = three_pass(txt[q, 0], txt[q, 1], high[rows, :width], low[rows, :width])
            for part in range(2):
                modes[a, part, q * HALF : (q + 1) * HALF] = result[
                    part * HALF : (part + 1) * HALF
                ]

    m = pl.program_id(0)
    kthird = thirds[0, m]
    scale = thirds[1, m]
    chunk = 16

    def project(i, carry):
        rows = pl.ds(pl.multiple_of(i * chunk, chunk), chunk)
        at = lax.broadcasted_iota(jnp.int32, (chunk, width), 0) + i * chunk
        bin_first = jnp.where(at < HALF, 2 * at, 2 * at - (G - 1))
        lane = lax.broadcasted_iota(jnp.int32, (chunk, width), 1)
        second = []
        for p in range(pars):
            odd = jnp.where(signs[p] < 0.0, 1, 0)
            second.append(2 * (lane[:, p * HALF : (p + 1) * HALF] - p * HALF) + odd)
        bin_second = jnp.concatenate(second, axis=1) if pars > 1 else second[0]
        kept = (bin_first != HALF) & (bin_second != HALF)
        kfirst = jnp.where(bin_first < HALF, bin_first, bin_first - G).astype(jnp.float32)
        ksecond = jnp.where(bin_second < HALF, bin_second, bin_second - G).astype(jnp.float32)
        squared = kfirst * kfirst + ksecond * ksecond + kthird * kthird
        weighting = jnp.where(kept, scale / (squared + screen_shift), 0.0)
        inverse = 1.0 / jnp.maximum(squared, 1.0)
        for part in range(2):
            u, v, w = (modes[a, part, rows, :] for a in range(3))
            inner = (kfirst * u + ksecond * v + kthird * w) * inverse
            lines[0, part, rows, :] = (u - kfirst * inner) * weighting
            lines[1, part, rows, :] = (v - ksecond * inner) * weighting
            lines[2, part, rows, :] = (w - kthird * inner) * weighting
        return carry

    lax.fori_loop(0, G // chunk, project, 0)

    for a in range(3):
        results = []
        for q in range(2):
            rows = slice((2 * a + q) % 3 * G, ((2 * a + q) % 3 + 1) * G)
            for part in range(2):
                at = rows.start + part * HALF
                stage(
                    lines[a, part, q * HALF : (q + 1) * HALF],
                    (slice(at, at + HALF), slice(0, width)),
                )
            results.append(
                three_pass(tx[q, 0], tx[q, 1], high[rows, :width], low[rows, :width])
            )
        for part in range(2):
            even, odd = (r[part * HALF : (part + 1) * HALF] for r in results)
            modes[a, part, :HALF] = even + odd
            modes[a, part, HALF:] = even - odd
    for a in range(3):
        near = far = None
        for p in range(pars):
            rows = slice((2 * a + p) % 3 * G, ((2 * a + p) % 3 + 1) * G)
            for part in range(2):
                stage(
                    modes[a, part, :, p * HALF : (p + 1) * HALF],
                    (rows, slice(part * HALF, (part + 1) * HALF)),
                )
            result = three_pass(high[rows], low[rows], tyt[p, 0], tyt[p, 1])
            near = result if near is None else near + result
            far = signs[p] * result if far is None else far + signs[p] * result
        for part in range(2):
            out[a, 0, part, :, :HALF] = near[:, part * HALF : (part + 1) * HALF]
            out[a, 0, part, :, HALF:] = far[:, part * HALF : (part + 1) * HALF]


def gather_kernel(cols, stencils, phases, field, out, lines, found):
    parts, slab, _ = field.shape
    clusters = stencils.shape[2]
    bins = parts // 3
    span = G // cols
    corner = (pl.program_id(0) * slab).astype(jnp.float32)
    for v in range(parts):
        for side in range(2):
            lines[side, pl.ds(v, slab, stride=parts), :] = field[
                v, :, side * HALF : (side + 1) * HALF
            ]
    for c in range(cols):
        first = stencils[c, 3 * STENCIL : 3 * STENCIL + 1, :] - corner
        second = stencils[c, 3 * STENCIL + 1 : 3 * STENCIL + 2, :]
        rows = lax.broadcasted_iota(jnp.int32, (2 * span, clusters), 0)
        rows = (jnp.where(rows < span, rows, rows - span) + c * span).astype(jnp.float32)
        hot = jnp.concatenate(
            [jnp.where(rows == second + y, 1.0, 0.0) for y in range(SIDE)], axis=1
        ).astype(jnp.bfloat16)
        side, start = divmod(c * span, HALF)
        values = lines[side, :, start : start + span]
        high, low = split(values)
        found[...] = dot(jnp.concatenate([high, low], axis=1), hot)
        wide = jnp.broadcast_to(first, (parts, clusters))
        for y in range(SIDE):
            lanes = slice(y * clusters, (y + 1) * clusters)
            sums = [jnp.zeros((parts, clusters), jnp.float32) for _ in range(SIDE)]
            for cell in range(slab):
                value = found[cell * parts : (cell + 1) * parts, lanes]
                for x in range(SIDE):
                    if 0 <= cell - x <= slab - SIDE:
                        sums[x] = jnp.where(wide == (cell - x), value, sums[x])
            for x in range(SIDE):
                for a in range(3):
                    mode = sums[x][a * bins : (a + 1) * bins]
                    for z in range(SIDE):
                        at = a * STENCIL + x * 9 + y * 3 + z
                        out[c, at : at + 1, :] = jnp.sum(
                            mode * phases[c, z], axis=0, keepdims=True
                        )


def per_device(
    density,
    interp_weight,
    proj_weight,
    stencil_corner,
    near_tiles,
    pair_target,
    pair_landing,
    pair_count,
):
    clusters = stencil_corner.shape[1]
    panels = density.shape[1] // clusters
    rows_total = lax.axis_size("row")
    cols_total = lax.axis_size("col")
    devices = rows_total * cols_total
    device = lax.axis_index("row") * cols_total + lax.axis_index("col")
    slab = G // rows_total
    kept_bins = G // 2
    third_parts = min(devices, kept_bins)
    second_parts = devices // third_parts
    pars = 2 // second_parts
    third_live = kept_bins // third_parts
    bins = max(4, third_live)
    parts = 3 * 2 * bins
    width = pars * HALF
    f32, bf16 = jnp.float32, jnp.bfloat16

    charges = density.reshape(3, clusters, panels)
    weights_in = interp_weight.reshape(STENCIL, clusters, panels)
    weights_out = proj_weight.reshape(STENCIL, clusters, panels)
    spread = jnp.einsum("ckp,skp->csk", charges, weights_in, precision=precise)
    packed = jnp.concatenate(
        [spread.reshape(3 * STENCIL, clusters), stencil_corner.astype(f32)], axis=0
    )
    height = 3 * STENCIL + 3
    everyone = lax.all_to_all(
        jnp.broadcast_to(packed[None], (devices, height, clusters)), AXES, 0, 0, tiled=True
    )

    step = jnp.arange(bins, dtype=jnp.int32)
    third_bins = (device // second_parts) * third_live + step
    live = (step < third_live).astype(f32)
    factor = 1.0 / math.sqrt(density.shape[1] * devices)
    fold = jnp.where(third_bins == 0, 1.0, 2.0).astype(f32)
    thirds = jnp.stack([third_bins.astype(f32), live * fold * factor])
    first_parity = device % second_parts
    signs = 1.0 - 2.0 * (first_parity + jnp.arange(pars, dtype=jnp.int32)).astype(f32)

    shape = (devices, SIDE, bins, 2, clusters)
    cells = everyone[:, 3 * STENCIL + 2].astype(jnp.int32)[:, None, None, None, :]
    cells = cells + lax.broadcasted_iota(jnp.int32, shape, 1)
    turns = cells * third_bins[:, None, None] + lax.broadcasted_iota(jnp.int32, shape, 3) * (G // 4)
    phases = jnp.cos((turns % G).astype(f32) * (2.0 * math.pi / G)) * live[:, None, None]
    phases = phases.reshape(devices, SIDE, 2 * bins, clusters)

    tables = half_tables()
    tx = jnp.asarray(tables)
    txt = jnp.asarray(np.ascontiguousarray(np.swapaxes(tables, 2, 3)))
    if pars == 2:
        ty, tyt = tx, txt
    else:
        ty = lax.dynamic_slice_in_dim(tx, first_parity, 1, axis=0)
        tyt = lax.dynamic_slice_in_dim(txt, first_parity, 1, axis=0)

    whole_row = pl.BlockSpec((cols_total, height, clusters), lambda r: (r, 0, 0))
    phase_row = pl.BlockSpec((cols_total, SIDE, 2 * bins, clusters), lambda r: (r, 0, 0, 0))
    slab_block = pl.BlockSpec((parts, slab, G), lambda r: (0, r, 0))
    lanes = cols_total * SIDE * clusters
    field = pl.pallas_call(
        lambda *refs: scatter_kernel(cols_total, *refs),
        grid=(rows_total,),
        in_specs=[whole_row, phase_row],
        out_specs=slab_block,
        out_shape=jax.ShapeDtypeStruct((parts, G, G), f32),
        scratch_shapes=[
            pltpu.VMEM((slab, 2 * parts, lanes), bf16),
            pltpu.VMEM((G, lanes), bf16),
            pltpu.VMEM((2, slab * 2 * parts, HALF), f32),
        ],
        name="scatter",
    )(everyone, phases)

    plane = pl.BlockSpec((3, 1, 2, G, G), lambda m: (0, m, 0, 0, 0))
    smem = pl.BlockSpec(memory_space=pltpu.SMEM)
    table = pl.BlockSpec((2, 2, G, G), lambda m: (0, 0, 0, 0))
    table_y = pl.BlockSpec((pars, 2, G, G), lambda m: (0, 0, 0, 0))
    field = pl.pallas_call(
        dft_kernel,
        grid=(bins,),
        in_specs=[smem, smem, plane, table, table, table_y, table_y],
        out_specs=plane,
        out_shape=jax.ShapeDtypeStruct((3, bins, 2, G, G), f32),
        scratch_shapes=[
            pltpu.VMEM((3, 2, G, width), f32),
            pltpu.VMEM((3, 2, G, width), f32),
            pltpu.VMEM((3 * G, G), bf16),
            pltpu.VMEM((3 * G, G), bf16),
        ],
        name="spectral",
    )(signs, thirds, field.reshape(3, bins, 2, G, G), tx, txt, ty, tyt)

    sampled = pl.pallas_call(
        lambda *refs: gather_kernel(cols_total, *refs),
        grid=(rows_total,),
        in_specs=[whole_row, phase_row, slab_block],
        out_specs=pl.BlockSpec((cols_total, 3 * STENCIL, clusters), lambda r: (r, 0, 0)),
        out_shape=jax.ShapeDtypeStruct((devices, 3 * STENCIL, clusters), f32),
        scratch_shapes=[
            pltpu.VMEM((2, slab * parts, HALF), f32),
            pltpu.VMEM((slab * parts, SIDE * clusters), f32),
        ],
        name="gather",
    )(everyone, phases, field.reshape(parts, G, G))
    sampled = lax.all_to_all(sampled, AXES, 0, 0, tiled=True)
    sampled = jnp.sum(sampled, axis=0).reshape(3, STENCIL, clusters)
    far_term = jnp.einsum("csk,skp->ckp", sampled, weights_out, precision=precise)
    near_term = near_field(charges, near_tiles, pair_target, pair_landing, pair_count)
    return (far_term + near_term).reshape(3, -1)


def solution(mesh):
    in_specs = (
        P(None, AXES),
        P(None, AXES),
        P(None, AXES),
        P(None, AXES),
        P(AXES, None, None, None, None),
        P(AXES),
        P(AXES),
        P(AXES),
    )
    return jax.shard_map(
        per_device, mesh=mesh, in_specs=in_specs, out_specs=P(None, AXES), check_vma=False
    )
```

time: 1540 us -> 168 us (0.11)
  local copies, waits for them, and re-layouts: 528 us -> 15.8 us
  other arithmetic: 485 us -> 8.92 us
  waiting for transfers between devices: 253 us -> 53.9 us
  blocking collectives: 142 us -> 0 us
  matrix products: 94.1 us -> 11.5 us
  Pallas kernels: 0 us -> 60 us
    scatter-add x1 -> x0, other arithmetic: 385 us -> none  [per_device(): flat_grid = jnp.zeros((3, slab_first * slab_second * G), jnp.float32).at[...]
    unnamed x40 -> x14, local copies, waits for them, and re-layouts: 240 us -> 3.26 us
    all_to_all x3 -> x2, waiting for transfers between devices: 253 us -> 35.8 us  [the longest x1 32.9 us: per_device(): lax.all_to_all(jnp.broadcast_to(packed[None], (devices, height, clusters)...]
    all_to_all x8 -> x0, local copies, waits for them, and re-layouts: 152 us -> none  [the longest x2 43 us: per_device(): lax.all_to_all(spectral, 'row', split_axis=2, concat_axis=4, tiled=True)]
    all_to_all x1 -> x0, blocking collectives: 142 us -> none  [per_device(): lax.all_to_all(spectral, 'row', split_axis=4, concat_axis=2, tiled=True)]
    dot_general x10 -> x4, matrix products: 94.1 us -> 11.5 us  [the longest x1 4.95 us: per_device(): jnp.einsum('csk,skp->ckp', sampled, weights_out, precision=precise)]
    all_to_all x4 -> x0, other arithmetic: 81.6 us -> none  [the longest x1 21.4 us: per_device(): lax.all_to_all(spectral, 'col', split_axis=4, concat_axis=1, tiled=True)]
    dot_general x3 -> x1, local copies, waits for them, and re-layouts: 63 us -> 1.76 us  [near_field(): return jnp.einsum('qk,qbj->bkj', landing_hot, incoming, precision=precise)]
  transfers between devices with their start and end apart: 5 -> 4, of which waited for: 3 -> 4; matrix products, arithmetic and copies ran while one was open for 1% -> 6% of each run, Pallas kernels for 0% -> 0%
where the time goes in v1:
time: 168 us; the launch traced here: 167 us
  Pallas kernels  60 us (36%)
  waiting for transfers between devices  53.9 us (32%)
  starting transfers between devices  15.9 us (9%)
  local copies, waits for them, and re-layouts  15.8 us (9%)
  matrix products  11.5 us (7%)
  other arithmetic  8.92 us (5%)
    all_to_all x1, waiting for transfers between devices, per_device(): lax.all_to_all(jnp.broadcast_to(packed[None], (devices, height, clusters)...  32.9 us
    pallas_call x1, Pallas kernels, per_device(): pl.pallas_call(lambda *refs: scatter_kernel(cols_total, *refs), grid=(row...  28.3 us
    pallas_call x1, Pallas kernels, per_device(): pl.pallas_call(dft_kernel, grid=(bins,), in_specs=[smem, smem, plane, tab...  19.5 us
    ppermute x1, waiting for transfers between devices, padded(): lax.ppermute(head, axis, [((i + 1) % count, i) for i in range(count)])  13.2 us
    pallas_call x1, Pallas kernels, per_device(): pl.pallas_call(lambda *refs: gather_kernel(cols_total, *refs), grid=(rows...  12.2 us
    all_to_all x1, starting transfers between devices, per_device(): lax.all_to_all(jnp.broadcast_to(packed[None], (devices, height, clusters)...  7.62 us
    dot_general x1, matrix products, per_device(): jnp.einsum('csk,skp->ckp', sampled, weights_out, precision=precise)  4.95 us
    dot_general x1, matrix products, per_device(): spread = jnp.einsum('ckp,skp->csk', charges, weights_in, precision=precise)  4.91 us
  transfers between devices with their start and end apart: 4, of which 4 were waited for; matrix products, arithmetic and copies ran while one was open for 6% of the time, Pallas kernels for 0%

profile of v1, /device:TPU:0, one launch (start us, length us, event | category | flops | bytes accessed | tf_op | source)
XLA Modules:
  0.0 166.9 jit_solution(3994836202727633010)
XLA Ops:
  0.0 0.0 copy-start
  0.0 2.1 %copy.24 = f32[4,8,128,128]{3,2,1,0:T(8,128)S(1)} copy(f32[4,8,128,128]{3,1,2,0:T(8,128)} %bitcast.42) | data formatting | bytes 4194304
  2.1 0.0 copy-start.2
  2.1 0.2 slice.27
  2.3 0.8 copy-done.2
  3.1 0.0 copy-start.3
  3.1 4.9 %fusion.6 = f32[3,27,128]{1,0,2:T(4,128)} fusion(f32[27,128,128]{2,1,0:T(8,128)S(1)} %slice.27, f32[3,16384]{1,0:T(4,128)S(1)} %copy-done.2), kind=kOutput, calls=%fused_computation.7 | convolution fusion | flops 15925248 | bytes 2007552 | tf_op jit(solution)/shard_map/ckp,skp->csk/dot_general | solution.py:312
  8.0 1.7 %copy.17 = f32[3,27,128]{2,1,0:T(8,128)} copy(f32[3,27,128]{1,0,2:T(4,128)} %fusion.6) | data formatting | bytes 82944 | tf_op jit(solution)/shard_map/ckp,skp->csk/transpose | solution.py:312
  9.7 1.4 reshape.87
  11.1 0.0 copy-done.3
  11.1 0.8 pad_maximum_fusion
  11.9 1.2 broadcast_in_dim.32
  13.1 7.6 %all-to-all-start = ((f32[32,84,128]{2,1,0:T(8,128)}), f32[32,84,128]{2,1,0:T(8,128)}, u32[]{:S(2)}, u32[]{:S(2)}) async-start(f32[32,84,128]{2,1,0:T(8,128)} %broadcast_in_dim.32), calls=%async_computation | async-start | bytes 2883584 | tf_op jit(solution)/shard_map/all_to_all | solution.py:317
  20.8 0.1 mul.64
  20.8 0.1 mul.65
  20.9 0.1 iota.47
  21.0 0.1 mul.72
  21.1 0.1 mul.73
  21.2 0.5 multiply_subtract_fusion.signs
  21.7 0.6 pad_maximum_fusion.2.thirds
  22.3 32.9 %all-to-all-done.refs_0_ = f32[32,84,128]{2,1,0:T(8,128)} async-done(((f32[32,84,128]{2,1,0:T(8,128)}), f32[32,84,128]{2,1,0:T(8,128)}, u32[]{:S(2)}, u32[]{:S(2)}) %all-to-all-start) | async-done | bytes 1376288 | tf_op jit(solution)/shard_map/all_to_all | solution.py:317
  55.2 0.9 slice_convert_fusion
  56.1 2.3 %fusion.22.refs_1_ = f32[32,3,8,128]{3,2,1,0:T(8,128)} fusion(f32[8]{0:T(128)S(1)} %mul.73, s32[8]{0:T(128)S(1)} %iota.47, s32[8]{0:T(128)S(1)} %mul.65, s32[32,128]{1,0:T(8,128)S(1)} %bitcast.45), kind=kLoop, calls=%fused_computation.18 | loop fusion | flops 1671168 | bytes 409696 | tf_op jit(solution)/shard_map/mul | solution.py:334
  58.4 28.3 %scatter.1 = f32[24,256,256]{2,1,0:T(8,128)} custom-call(f32[32,84,128]{2,1,0:T(8,128)} %all-to-all-done.refs_0_, f32[32,3,8,128]{3,2,1,0:T(8,128)} %fusion.22.refs_1_), custom_call_target="tpu_custom_call" | custom-call | tf_op jit(solution)/shard_map/scatter/pallas_call | solution.py:350
  86.7 19.5 %spectral.1 = f32[3,4,2,256,256]{4,3,2,1,0:T(8,128)} custom-call(f32[2]{0:T(128)} %multiply_subtract_fusion.signs, f32[2,4]{1,0:T(2,128)} %pad_maximum_fusion.2.thirds, f32[3,4,2,256,256]{4,3,2,1,0:T(8,128)} %bitcast.39, bf16[2,2,256,256]{3,2,1,0:T(8,128)(2,1)} %constant.71.clone.tx.ty, bf16[2,2,256,256]{3,2,1,0:T(8,128)(2,1)} %constant.72.clone.txt.tyt, ...), custom_call_target="tpu_custom_call" | custom-call | tf_op jit(solution)/shard_map/spectral/pallas_call | solution.py:368
  106.2 12.2 %gather.7 = f32[32,81,128]{2,1,0:T(8,128)} custom-call(f32[32,84,128]{2,1,0:T(8,128)} %all-to-all-done.refs_0_, f32[32,3,8,128]{3,2,1,0:T(8,128)} %fusion.22.refs_1_, f32[24,256,256]{2,1,0:T(8,128)} %bitcast.38), custom_call_target="tpu_custom_call" | custom-call | tf_op jit(solution)/shard_map/gather/pallas_call | solution.py:383
  118.4 0.0 copy-start.5
  118.4 3.7 %all-to-all-start.1 = ((f32[32,81,128]{2,1,0:T(8,128)}), f32[32,81,128]{2,1,0:T(8,128)}, u32[]{:S(2)}, u32[]{:S(2)}) async-start(f32[32,81,128]{2,1,0:T(8,128)} %gather.7), calls=%async_computation.1 | async-start | bytes 2883584 | tf_op jit(solution)/shard_map/all_to_all | solution.py:395
  122.8 0.0 copy-done.5
  122.8 1.7 bitcast_convert_fusion
  124.5 1.5 gather_fusion
  126.0 0.0 copy-start.1
  126.0 0.0 copy-done
  126.0 0.6 fusion
  126.6 0.1 bitcast_select_fusion
  126.7 4.5 %collective-permute-start = (f32[4,1,3,128]{3,1,0,2:T(1,128)S(1)}, f32[4,1,3,128]{3,1,0,2:T(1,128)S(1)}, u32[]{:S(2)}, u32[]{:S(2)}) collective-permute-start(f32[4,1,3,128]{3,1,0,2:T(1,128)S(1)} %get-tuple-element.5), channel_id=1, source_target_pairs={{4,0},{8,4},{12,8},{16,12},{20,16},{24,20},{28,24},{0,28},{5,1},{9... | collective-permute-start | bytes 18440 | tf_op jit(solution)/shard_map/ppermute | solution.py:30
  131.3 0.0 collective-permute-start.1
  131.3 0.0 copy-done.1
  131.3 0.4 copy.25
  131.7 0.0 copy-start.4
  131.7 1.3 slice.28
  133.0 13.2 %collective-permute-done = f32[4,1,3,128]{3,1,0,2:T(1,128)S(1)} collective-permute-done((f32[4,1,3,128]{3,1,0,2:T(1,128)S(1)}, f32[4,1,3,128]{3,1,0,2:T(1,128)S(1)}, u32[]{:S(2)}, u32[]{:S(2)}) %collective-permute-start) | collective-permute-done | bytes 6176 | tf_op jit(solution)/shard_map/ppermute | solution.py:30
  146.2 4.8 %collective-permute-done.1 = f32[4,1,3,128]{3,1,0,2:T(1,128)S(1)} collective-permute-done((f32[4,1,3,128]{3,1,0,2:T(1,128)S(1)}, f32[4,1,3,128]{3,1,0,2:T(1,128)S(1)}, u32[]{:S(2)}, u32[]{:S(2)}) %collective-permute-start.1) | collective-permute-done | bytes 6176 | tf_op jit(solution)/shard_map/ppermute | solution.py:28
  151.1 0.0 copy-done.4
  151.1 1.0 fusion.24
  152.1 1.8 %copy.20 = f32[3,128,128]{1,0,2:T(4,128)} copy(f32[3,128,128]{2,1,0:T(8,128)} %fusion.24) | data formatting | bytes 393216 | tf_op jit(solution)/shard_map/qk,qbj->bkj/dot_general | solution.py:57
  153.9 2.9 %all-to-all-done.1 = f32[32,81,128]{2,1,0:T(8,128)} async-done(((f32[32,81,128]{2,1,0:T(8,128)}), f32[32,81,128]{2,1,0:T(8,128)}, u32[]{:S(2)}, u32[]{:S(2)}) %all-to-all-start.1) | async-done | bytes 1327136 | tf_op jit(solution)/shard_map/all_to_all | solution.py:395
  156.8 2.1 %reduce_sum.9 = f32[81,128]{1,0:T(8,128)} reduce(f32[32,81,128]{2,1,0:T(8,128)} %all-to-all-done.1, f32[]{:T(128)} %constant.68.clone.1), dimensions={0}, to_apply=%region_0.1 | reduce | flops 321408 | bytes 1368580 | tf_op jit(solution)/shard_map/reduce_sum | solution.py:396
  158.9 1.4 reshape.90
  160.3 1.6 copy.18
  161.9 5.0 %fusion.15 = f32[3,16384]{1,0:T(4,128)} fusion(f32[3,27,128]{1,0,2:T(4,128)} %copy.18, f32[27,128,128]{2,1,0:T(8,128)} %slice.28, f32[3,128,128]{1,0,2:T(4,128)} %copy.20), kind=kOutput, calls=%fused_computation.10 | convolution fusion | flops 15974400 | bytes 2204160 | tf_op jit(solution)/shard_map/csk,skp->ckp/dot_general | solution.py:397
  (14 shorter events, 0.1 us)
Async XLA Ops:
  0.0 126.0 %copy-start = (bf16[12,3,3,128,128]{4,3,2,1,0:T(8,128)(2,1)S(1)}, bf16[12,3,3,128,128]{4,3,2,1,0:T(8,128)(2,1)}, u32[]{:S(2)}) copy-start(bf16[12,3,3,128,128]{4,3,2,1,0:T(8,128)(2,1)} %param.14) | copy-start | bytes 10616836
  2.1 1.0 copy-start.2
  3.1 8.0 %copy-start.3 = (s32[3,128]{1,0:T(4,128)S(1)}, s32[3,128]{1,0:T(4,128)}, u32[]{:S(2)}) copy-start(s32[3,128]{1,0:T(4,128)} %param.13) | copy-start | bytes 4612
  13.1 42.1 %all-to-all-start = ((f32[32,84,128]{2,1,0:T(8,128)}), f32[32,84,128]{2,1,0:T(8,128)}, u32[]{:S(2)}, u32[]{:S(2)}) async-start(f32[32,84,128]{2,1,0:T(8,128)} %broadcast_in_dim.32), calls=%async_computation | async-start | bytes 2883584 | tf_op jit(solution)/shard_map/all_to_all | solution.py:317
  118.4 4.4 %copy-start.5 = (s32[12]{0:T(128)S(1)}, s32[12]{0:T(128)}, u32[]{:S(2)}) copy-start(s32[12]{0:T(128)} %param.15) | copy-start | bytes 148
  118.4 38.4 %all-to-all-start.1 = ((f32[32,81,128]{2,1,0:T(8,128)}), f32[32,81,128]{2,1,0:T(8,128)}, u32[]{:S(2)}, u32[]{:S(2)}) async-start(f32[32,81,128]{2,1,0:T(8,128)} %gather.7), calls=%async_computation.1 | async-start | bytes 2883584 | tf_op jit(solution)/shard_map/all_to_all | solution.py:395
  126.0 5.3 %copy-start.1 = (f32[27,16384]{1,0:T(8,128)S(1)}, f32[27,16384]{1,0:T(8,128)}, u32[]{:S(2)}) copy-start(f32[27,16384]{1,0:T(8,128)} %param.12) | copy-start | bytes 5308420
  126.7 19.5 %collective-permute-start = (f32[4,1,3,128]{3,1,0,2:T(1,128)S(1)}, f32[4,1,3,128]{3,1,0,2:T(1,128)S(1)}, u32[]{:S(2)}, u32[]{:S(2)}) collective-permute-start(f32[4,1,3,128]{3,1,0,2:T(1,128)S(1)} %get-tuple-element.5), channel_id=1, source_target_pairs={{4,0},{8,4},{12,8},{16,12},{20,16},{24,20},{28,24},{0,28},{5,1},{9... | collective-permute-start | bytes 18440 | tf_op jit(solution)/shard_map/ppermute | solution.py:30
  131.3 19.8 %collective-permute-start.1 = (f32[4,1,3,128]{3,1,0,2:T(1,128)S(1)}, f32[4,1,3,128]{3,1,0,2:T(1,128)S(1)}, u32[]{:S(2)}, u32[]{:S(2)}) collective-permute-start(f32[4,1,3,128]{3,1,0,2:T(1,128)S(1)} %get-tuple-element.6), channel_id=1, source_target_pairs={{0,4},{4,8},{8,12},{12,16},{16,20},{20,24},{24,28},{28,0},{1,5},{5... | collective-permute-start | bytes 18440 | tf_op jit(solution)/shard_map/ppermute | solution.py:28
  131.7 19.4 %copy-start.4 = (s32[12]{0:T(128)S(1)}, s32[12]{0:T(128)}, u32[]{:S(2)}) copy-start(s32[12]{0:T(128)} %param.16) | copy-start | bytes 148

commit v2 on v1

--- a/solution.py
+++ b/solution.py
@@ -12,7 +12,8 @@
 HALF = G // 2
 STENCIL = 27
 SIDE = 3
-AXES = ("row", "col")
+AXES = ("row", "half", "core")
+PEERS = ("row", "half")
 
 precise = lax.Precision.HIGHEST
 screen_shift = 0.5
@@ -87,16 +88,32 @@
     )
 
 
-def scatter_kernel(cols, stencils, phases, out, spread, hot, total):
+def ordered(core, mine, other, stencils):
+    for j in range(mine.shape[0]):
+        stencils[2 * j + core] = mine[j]
+        stencils[2 * j + 1 - core] = other[j]
+
+
+def scatter_kernel(live, where, mine, other, out, phases, stencils, spread, hot, total):
     parts, slab, _ = out.shape
-    clusters = stencils.shape[2]
+    cols, _, clusters = stencils.shape
     corner = pl.program_id(0) * slab
+    ordered(where[0], mine, other, stencils)
+    bins = lax.broadcasted_iota(jnp.int32, phases.shape[2:], 0)
+    waves = bins // 2 + where[1]
+    quarter = bins % 2 * (G // 4) + HALF
+    kept = bins < 2 * live
 
     def block(c, carry):
         first = stencils[c, 3 * STENCIL : 3 * STENCIL + 1, :] - corner.astype(jnp.float32)
         second = stencils[c, 3 * STENCIL + 1 : 3 * STENCIL + 2, :]
         rows = lax.broadcasted_iota(jnp.int32, (G, clusters), 0).astype(jnp.float32)
         first_wide = jnp.broadcast_to(first, (2 * parts, clusters)).astype(jnp.bfloat16)
+        third = stencils[c, 3 * STENCIL + 2 : 3 * STENCIL + 3, :].astype(jnp.int32)
+        for z in range(SIDE):
+            turns = (((third + z) * waves + quarter) & (G - 1)) - HALF
+            turned = jnp.cos(turns.astype(jnp.float32) * (2.0 * math.pi / G))
+            phases[c, z] = jnp.where(kept, turned, 0.0)
         for y in range(SIDE):
             lanes = pl.ds(pl.multiple_of((c * SIDE + y) * clusters, clusters), clusters)
             hot[:, lanes] = jnp.where(rows == second + y, 1.0, 0.0).astype(jnp.bfloat16)
@@ -237,9 +254,10 @@
             out[a, 0, part, :, HALF:] = far[:, part * HALF : (part + 1) * HALF]
 
 
-def gather_kernel(cols, stencils, phases, field, out, lines, found):
+def gather_kernel(where, mine, other, phases, field, out, stencils, lines, found):
     parts, slab, _ = field.shape
-    clusters = stencils.shape[2]
+    cols, _, clusters = stencils.shape
+    ordered(where[0], mine, other, stencils)
     bins = parts // 3
     span = G // cols
     corner = (pl.program_id(0) * slab).astype(jnp.float32)
@@ -274,7 +292,7 @@
                     mode = sums[x][a * bins : (a + 1) * bins]
                     for z in range(SIDE):
                         at = a * STENCIL + x * 9 + y * 3 + z
-                        out[c, at : at + 1, :] = jnp.sum(
+                        out[(c + where[0]) % 2, c // 2, at : at + 1, :] = jnp.sum(
                             mode * phases[c, z], axis=0, keepdims=True
                         )
 
@@ -292,9 +310,12 @@
     clusters = stencil_corner.shape[1]
     panels = density.shape[1] // clusters
     rows_total = lax.axis_size("row")
-    cols_total = lax.axis_size("col")
+    halves = lax.axis_size("half")
+    cols_total = halves * lax.axis_size("core")
     devices = rows_total * cols_total
-    device = lax.axis_index("row") * cols_total + lax.axis_index("col")
+    core = lax.axis_index("core")
+    device = lax.axis_index("row") * cols_total + lax.axis_index("half") * 2 + core
+    swap = [(0, 1), (1, 0)]
     slab = G // rows_total
     kept_bins = G // 2
     third_parts = min(devices, kept_bins)
@@ -314,9 +335,11 @@
         [spread.reshape(3 * STENCIL, clusters), stencil_corner.astype(f32)], axis=0
     )
     height = 3 * STENCIL + 3
-    everyone = lax.all_to_all(
-        jnp.broadcast_to(packed[None], (devices, height, clusters)), AXES, 0, 0, tiled=True
-    )
+    peers = devices // 2
+    mine = lax.all_to_all(
+        jnp.broadcast_to(packed[None], (peers, height, clusters)), PEERS, 0, 0, tiled=True
+    )
+    other = lax.ppermute(mine, "core", swap)
 
     step = jnp.arange(bins, dtype=jnp.int32)
     third_bins = (device // second_parts) * third_live + step
@@ -327,12 +350,7 @@
     first_parity = device % second_parts
     signs = 1.0 - 2.0 * (first_parity + jnp.arange(pars, dtype=jnp.int32)).astype(f32)
 
-    shape = (devices, SIDE, bins, 2, clusters)
-    cells = everyone[:, 3 * STENCIL + 2].astype(jnp.int32)[:, None, None, None, :]
-    cells = cells + lax.broadcasted_iota(jnp.int32, shape, 1)
-    turns = cells * third_bins[:, None, None] + lax.broadcasted_iota(jnp.int32, shape, 3) * (G // 4)
-    phases = jnp.cos((turns % G).astype(f32) * (2.0 * math.pi / G)) * live[:, None, None]
-    phases = phases.reshape(devices, SIDE, 2 * bins, clusters)
+    where = jnp.stack([core, (device // second_parts) * third_live]).astype(jnp.int32)
 
     tables = half_tables()
     tx = jnp.asarray(tables)
@@ -343,26 +361,30 @@
         ty = lax.dynamic_slice_in_dim(tx, first_parity, 1, axis=0)
         tyt = lax.dynamic_slice_in_dim(txt, first_parity, 1, axis=0)
 
-    whole_row = pl.BlockSpec((cols_total, height, clusters), lambda r: (r, 0, 0))
+    smem = pl.BlockSpec(memory_space=pltpu.SMEM)
+    peer_row = pl.BlockSpec((halves, height, clusters), lambda r: (r, 0, 0))
     phase_row = pl.BlockSpec((cols_total, SIDE, 2 * bins, clusters), lambda r: (r, 0, 0, 0))
     slab_block = pl.BlockSpec((parts, slab, G), lambda r: (0, r, 0))
     lanes = cols_total * SIDE * clusters
-    field = pl.pallas_call(
-        lambda *refs: scatter_kernel(cols_total, *refs),
+    field, phases = pl.pallas_call(
+        lambda *refs: scatter_kernel(third_live, *refs),
         grid=(rows_total,),
-        in_specs=[whole_row, phase_row],
-        out_specs=slab_block,
-        out_shape=jax.ShapeDtypeStruct((parts, G, G), f32),
+        in_specs=[smem, peer_row, peer_row],
+        out_specs=[slab_block, phase_row],
+        out_shape=[
+            jax.ShapeDtypeStruct((parts, G, G), f32),
+            jax.ShapeDtypeStruct((devices, SIDE, 2 * bins, clusters), f32),
+        ],
         scratch_shapes=[
+            pltpu.VMEM((cols_total, height, clusters), f32),
             pltpu.VMEM((slab, 2 * parts, lanes), bf16),
             pltpu.VMEM((G, lanes), bf16),
             pltpu.VMEM((2, slab * 2 * parts, HALF), f32),
         ],
         name="scatter",
-    )(everyone, phases)
+    )(where, mine, other)
 
     plane = pl.BlockSpec((3, 1, 2, G, G), lambda m: (0, m, 0, 0, 0))
-    smem = pl.BlockSpec(memory_space=pltpu.SMEM)
     table = pl.BlockSpec((2, 2, G, G), lambda m: (0, 0, 0, 0))
     table_y = pl.BlockSpec((pars, 2, G, G), lambda m: (0, 0, 0, 0))
     field = pl.pallas_call(
@@ -381,18 +403,20 @@
     )(signs, thirds, field.reshape(3, bins, 2, G, G), tx, txt, ty, tyt)
 
     sampled = pl.pallas_call(
-        lambda *refs: gather_kernel(cols_total, *refs),
+        gather_kernel,
         grid=(rows_total,),
-        in_specs=[whole_row, phase_row, slab_block],
-        out_specs=pl.BlockSpec((cols_total, 3 * STENCIL, clusters), lambda r: (r, 0, 0)),
-        out_shape=jax.ShapeDtypeStruct((devices, 3 * STENCIL, clusters), f32),
+        in_specs=[smem, peer_row, peer_row, phase_row, slab_block],
+        out_specs=pl.BlockSpec((2, halves, 3 * STENCIL, clusters), lambda r: (0, r, 0, 0)),
+        out_shape=jax.ShapeDtypeStruct((2, peers, 3 * STENCIL, clusters), f32),
         scratch_shapes=[
+            pltpu.VMEM((cols_total, height, clusters), f32),
             pltpu.VMEM((2, slab * parts, HALF), f32),
             pltpu.VMEM((slab * parts, SIDE * clusters), f32),
         ],
         name="gather",
-    )(everyone, phases, field.reshape(parts, G, G))
-    sampled = lax.all_to_all(sampled, AXES, 0, 0, tiled=True)
+    )(where, mine, other, phases, field.reshape(parts, G, G))
+    sampled = sampled[0] + lax.ppermute(sampled[1], "core", swap)
+    sampled = lax.all_to_all(sampled, PEERS, 0, 0, tiled=True)
     sampled = jnp.sum(sampled, axis=0).reshape(3, STENCIL, clusters)
     far_term = jnp.einsum("csk,skp->ckp", sampled, weights_out, precision=precise)
     near_term = near_field(charges, near_tiles, pair_target, pair_landing, pair_count)
@@ -410,6 +434,8 @@
         P(AXES),
         P(AXES),
     )
+    rows_total, cols_total = (mesh.shape[axis] for axis in ("row", "col"))
+    split_mesh = jax.sharding.Mesh(mesh.devices.reshape(rows_total, cols_total // 2, 2), AXES)
     return jax.shard_map(
-        per_device, mesh=mesh, in_specs=in_specs, out_specs=P(None, AXES), check_vma=False
-    )
+        per_device, mesh=split_mesh, in_specs=in_specs, out_specs=P(None, AXES), check_vma=False
+    )

time: 168 us -> 153 us (0.911)
  waiting for transfers between devices: 53.9 us -> 9.82 us
  blocking collectives: 0 us -> 28.1 us
  starting transfers between devices: 15.9 us -> 9.35 us
  Pallas kernels: 60 us -> 65.7 us
  local copies, waits for them, and re-layouts: 15.8 us -> 19.8 us
  other arithmetic: 8.92 us -> 6.99 us
    all_to_all x2 -> x1, waiting for transfers between devices: 35.8 us -> 0.01 us  [per_device(): sampled = lax.all_to_all(sampled, PEERS, 0, 0, tiled=True)]
    all_to_all x0 -> x1, blocking collectives: none -> 28.1 us  [per_device(): lax.all_to_all(jnp.broadcast_to(packed[None], (peers, height, clusters)),...]
    ppermute x1, waiting for transfers between devices: 13.2 us -> 0.01 us  [padded(): lax.ppermute(head, axis, [((i + 1) % count, i) for i in range(count)])]
    all_to_all x2 -> x1, starting transfers between devices: 11.4 us -> 4.28 us  [per_device(): sampled = lax.all_to_all(sampled, PEERS, 0, 0, tiled=True)]
    pallas_call x2, Pallas kernels: 40.6 us -> 46.3 us  [the longest x1 33.8 us: per_device(): pl.pallas_call(lambda *refs: scatter_kernel(third_live, *refs), grid=(row...]
    ppermute x1, waiting for transfers between devices: 4.85 us -> 7.76 us  [padded(): lax.ppermute(tail, axis, [(i, (i + 1) % count) for i in range(count)])]
    mul x2 -> x0, other arithmetic: 2.28 us -> none  [the longest x1 2.27 us: per_device(): jnp.cos((turns % G).astype(f32) * (2.0 * math.pi / G)) * live[:, None, None]]
    ppermute x0 -> x1, local copies, waits for them, and re-layouts: none -> 2.17 us  [per_device(): other = lax.ppermute(mine, 'core', swap)]
  transfers between devices with their start and end apart: 4 -> 5, of which waited for: 4 -> 3; matrix products, arithmetic and copies ran while one was open for 6% -> 6% of each run, Pallas kernels for 0% -> 0%
where the time goes in v2:
time: 153 us; the launch traced here: 152 us
  Pallas kernels  65.7 us (43%)
  blocking collectives  28.1 us (18%)
  local copies, waits for them, and re-layouts  19.8 us (13%)
  matrix products  11.5 us (8%)
  waiting for transfers between devices  9.82 us (6%)
  starting transfers between devices  9.35 us (6%)
  other arithmetic  6.99 us (5%)
    pallas_call x1, Pallas kernels, per_device(): pl.pallas_call(lambda *refs: scatter_kernel(third_live, *refs), grid=(row...  33.8 us
    all_to_all x1, blocking collectives, per_device(): lax.all_to_all(jnp.broadcast_to(packed[None], (peers, height, clusters)),...  28.1 us
    pallas_call x1, Pallas kernels, per_device(): pl.pallas_call(dft_kernel, grid=(bins,), in_specs=[smem, smem, plane, tab...  19.4 us
    pallas_call x1, Pallas kernels, per_device(): pl.pallas_call(gather_kernel, grid=(rows_total,), in_specs=[smem, peer_ro...  12.4 us
    ppermute x1, waiting for transfers between devices, padded(): lax.ppermute(tail, axis, [(i, (i + 1) % count) for i in range(count)])  7.76 us
    dot_general x1, matrix products, per_device(): jnp.einsum('csk,skp->ckp', sampled, weights_out, precision=precise)  4.95 us
    dot_general x1, matrix products, per_device(): spread = jnp.einsum('ckp,skp->csk', charges, weights_in, precision=precise)  4.91 us
    all_to_all x1, starting transfers between devices, per_device(): sampled = lax.all_to_all(sampled, PEERS, 0, 0, tiled=True)  4.28 us
  transfers between devices with their start and end apart: 5, of which 3 were waited for; matrix products, arithmetic and copies ran while one was open for 6% of the time, Pallas kernels for 0%

profile of v2, /device:TPU:0, one launch (start us, length us, event | category | flops | bytes accessed | tf_op | source)
XLA Modules:
  0.0 152.1 jit_solution(11413646793958064553)
XLA Ops:
  0.0 0.0 copy-start
  0.0 0.8 convert_element_type.21
  0.8 2.1 %copy.34 = f32[4,8,128,128]{3,2,1,0:T(8,128)S(1)} copy(f32[4,8,128,128]{3,1,2,0:T(8,128)} %bitcast.49) | data formatting | bytes 4194304
  3.0 0.0 copy-start.4
  3.0 0.2 slice.32
  3.2 0.8 copy-done.4
  3.9 4.9 %fusion.6 = f32[3,27,128]{1,0,2:T(4,128)} fusion(f32[27,128,128]{2,1,0:T(8,128)S(1)} %slice.32, f32[3,16384]{1,0:T(4,128)S(1)} %copy-done.4), kind=kOutput, calls=%fused_computation.7 | convolution fusion | flops 15925248 | bytes 2007552 | tf_op jit(solution)/shard_map/ckp,skp->csk/dot_general | solution.py:333
  8.8 1.7 %copy.22 = f32[3,27,128]{2,1,0:T(8,128)} copy(f32[3,27,128]{1,0,2:T(4,128)} %fusion.6) | data formatting | bytes 82944 | tf_op jit(solution)/shard_map/ckp,skp->csk/transpose | solution.py:333
  10.5 1.4 reshape.67
  11.9 0.8 pad_maximum_fusion
  12.8 28.1 %all_to_all.10.refs_1_.mine = f32[16,84,128]{2,1,0:T(8,128)S(1)} all-to-all(f32[16,84,128]{2,1,0:T(8,128)S(1)} %broadcast_in_dim.31), channel_id=1, replica_groups=mesh['row'=8,'half'=2,'core'=2] {'row','half'}, dimensions={0} | all-to-all | bytes 1376256 | tf_op jit(solution)/shard_map/all_to_all | solution.py:339
  40.9 0.0 copy-start.1
  40.9 0.9 copy-done.1
  41.9 1.0 copy.23
  42.9 0.0 collective-permute-start
  42.9 0.5 multiply_subtract_fusion.signs
  43.4 0.6 pad_add_fusion.refs_0_.where
  44.0 0.6 pad_maximum_fusion.2.thirds
  44.6 0.8 collective-permute-done
  45.4 2.2 %copy.25.refs_2_.other = f32[16,84,128]{2,1,0:T(8,128)} copy(f32[16,84,128]{2,0,1:T(8,128)} %collective-permute-done) | data formatting | bytes 1376256 | tf_op jit(solution)/shard_map/ppermute | solution.py:342
  47.5 33.8 %scatter.1 = (f32[24,256,256]{2,1,0:T(8,128)}, f32[32,3,8,128]{3,2,1,0:T(8,128)}) custom-call(s32[2]{0:T(128)} %pad_add_fusion.refs_0_.where, f32[16,84,128]{2,1,0:T(8,128)} %copy-done.1, f32[16,84,128]{2,1,0:T(8,128)} %copy.25.refs_2_.other), custom_call_target="tpu_custom_call" | custom-call | tf_op jit(solution)/shard_map/scatter/pallas_call | solution.py:369
  81.4 19.4 %spectral.1 = f32[3,4,2,256,256]{4,3,2,1,0:T(8,128)} custom-call(f32[2]{0:T(128)} %multiply_subtract_fusion.signs, f32[2,4]{1,0:T(2,128)} %pad_maximum_fusion.2.thirds, f32[3,4,2,256,256]{4,3,2,1,0:T(8,128)} %bitcast.48, bf16[2,2,256,256]{3,2,1,0:T(8,128)(2,1)} %constant.60.clone.tx.ty, bf16[2,2,256,256]{3,2,1,0:T(8,128)(2,1)} %constant.61.clone.txt.tyt, ...), custom_call_target="tpu_custom_call" | custom-call | tf_op jit(solution)/shard_map/spectral/pallas_call | solution.py:390
  100.8 12.4 %gather.7 = f32[2,16,81,128]{3,2,1,0:T(8,128)} custom-call(s32[2]{0:T(128)} %pad_add_fusion.refs_0_.where, f32[16,84,128]{2,1,0:T(8,128)} %copy-done.1, f32[16,84,128]{2,1,0:T(8,128)} %copy.25.refs_2_.other, f32[32,3,8,128]{3,2,1,0:T(8,128)} %get-tuple-element.7.phases, f32[24,256,256]{2,1,0:T(8,128)} %bitcast.45), custom_call_target="tpu_custom_call" | custom-call | tf_op jit(solution)/shard_map/gather/pallas_call | solution.py:405
  113.2 0.0 copy-start.7
  113.2 0.0 copy-start.5
  113.2 0.0 copy-start.2
  113.2 1.3 slice_bitcast_fusion
  114.5 0.1 copy.26
  114.7 0.2 collective-permute-start.1
  114.9 0.0 copy-done.7
  114.9 0.0 copy-done.5
  114.9 0.7 bitcast_convert_fusion
  115.6 1.3 collective-permute-done.1
  116.8 0.0 copy-done.2
  116.8 1.1 fusion.18
  117.9 4.3 %all-to-all-start.1 = ((f32[16,81,128]{2,1,0:T(8,128)}), f32[16,81,128]{2,1,0:T(8,128)}, u32[]{:S(2)}, u32[]{:S(2)}) async-start(f32[16,81,128]{2,1,0:T(8,128)} %fusion.18), calls=%async_computation.1 | async-start | bytes 1441792 | tf_op jit(solution)/shard_map/all_to_all | solution.py:419
  122.9 1.5 gather_fusion
  124.4 0.0 copy-start.3
  124.4 0.0 copy-done
  124.4 0.6 fusion
  125.0 0.1 bitcast_select_fusion
  125.1 1.8 %collective-permute-start.3 = (f32[4,1,3,128]{3,1,0,2:T(1,128)S(1)}, f32[4,1,3,128]{3,1,0,2:T(1,128)S(1)}, u32[]{:S(2)}, u32[]{:S(2)}) collective-permute-start(f32[4,1,3,128]{3,1,0,2:T(1,128)S(1)} %get-tuple-element.10), channel_id=1, source_target_pairs={{0,4},{4,8},{8,12},{12,16},{16,20},{20,24},{24,28},{28,0},{1,5},{5... | collective-permute-start | bytes 18440 | tf_op jit(solution)/shard_map/ppermute | solution.py:29
  126.9 3.1 %collective-permute-start.2 = (f32[4,1,3,128]{3,1,0,2:T(1,128)S(1)}, f32[4,1,3,128]{3,1,0,2:T(1,128)S(1)}, u32[]{:S(2)}, u32[]{:S(2)}) collective-permute-start(f32[4,1,3,128]{3,1,0,2:T(1,128)S(1)} %get-tuple-element.9), channel_id=1, source_target_pairs={{4,0},{8,4},{12,8},{16,12},{20,16},{24,20},{28,24},{0,28},{5,1},{9... | collective-permute-start | bytes 18440 | tf_op jit(solution)/shard_map/ppermute | solution.py:31
  130.0 0.0 copy-done.3
  130.0 0.4 copy.35
  130.4 0.0 copy-start.6
  130.4 1.3 slice.33
  131.7 7.8 %collective-permute-done.3 = f32[4,1,3,128]{3,1,0,2:T(1,128)S(1)} collective-permute-done((f32[4,1,3,128]{3,1,0,2:T(1,128)S(1)}, f32[4,1,3,128]{3,1,0,2:T(1,128)S(1)}, u32[]{:S(2)}, u32[]{:S(2)}) %collective-permute-start.3) | collective-permute-done | bytes 6176 | tf_op jit(solution)/shard_map/ppermute | solution.py:29
  139.5 0.0 collective-permute-done.2
  139.5 0.0 copy-done.6
  139.5 1.0 fusion.20
  140.6 1.8 %copy.30 = f32[3,128,128]{1,0,2:T(4,128)} copy(f32[3,128,128]{2,1,0:T(8,128)} %fusion.20) | data formatting | bytes 393216 | tf_op jit(solution)/shard_map/qk,qbj->bkj/dot_general | solution.py:58
  142.3 0.0 all-to-all-done.1
  142.3 1.8 %reduce_sum.9 = f32[81,128]{1,0:T(8,128)} reduce(f32[16,81,128]{2,1,0:T(8,128)} %all-to-all-done.1, f32[]{:T(128)} %constant.57.clone.1), dimensions={0}, to_apply=%region_0.1 | reduce | flops 155520 | bytes 705028 | tf_op jit(solution)/shard_map/reduce_sum | solution.py:420
  144.1 1.4 reshape.70
  145.5 1.6 %copy.28 = f32[3,27,128]{1,0,2:T(4,128)} copy(f32[3,27,128]{2,1,0:T(8,128)} %reshape.70) | data formatting | bytes 82944 | tf_op jit(solution)/shard_map/reshape | solution.py:420
  147.2 5.0 %fusion.15 = f32[3,16384]{1,0:T(4,128)} fusion(f32[3,27,128]{1,0,2:T(4,128)} %copy.28, f32[27,128,128]{2,1,0:T(8,128)} %slice.33, f32[3,128,128]{1,0,2:T(4,128)} %copy.30), kind=kOutput, calls=%fused_computation.10 | convolution fusion | flops 15974400 | bytes 2204160 | tf_op jit(solution)/shard_map/csk,skp->ckp/dot_general | solution.py:421
  (10 shorter events, 0.1 us)
Async XLA Ops:
  0.0 124.4 %copy-start = (bf16[12,3,3,128,128]{4,3,2,1,0:T(8,128)(2,1)S(1)}, bf16[12,3,3,128,128]{4,3,2,1,0:T(8,128)(2,1)}, u32[]{:S(2)}) copy-start(bf16[12,3,3,128,128]{4,3,2,1,0:T(8,128)(2,1)} %param.14) | copy-start | bytes 10616836
  3.0 1.0 copy-start.4
  40.9 0.9 copy-start.1
  42.9 2.5 %collective-permute-start = (f32[16,84,128]{2,0,1:T(8,128)}, f32[16,84,128]{2,0,1:T(8,128)}, u32[]{:S(2)}, u32[]{:S(2)}) collective-permute-start(f32[16,84,128]{2,0,1:T(8,128)} %copy.23), channel_id=1, source_target_pairs={{0,1},{1,0},{2,3},{3,2},{4,5},{5,4},{6,7},{7,6},{8,9},{9,8},{10,11... | collective-permute-start | bytes 2064392 | tf_op jit(solution)/shard_map/ppermute | solution.py:342
  113.2 1.6 %copy-start.7 = (s32[12]{0:T(128)S(1)}, s32[12]{0:T(128)}, u32[]{:S(2)}) copy-start(s32[12]{0:T(128)} %param.15) | copy-start | bytes 148
  113.2 1.6 %copy-start.5 = (f32[3,16384]{1,0:T(4,128)S(1)}, f32[3,16384]{1,0:T(4,128)}, u32[]{:S(2)}) copy-start(f32[3,16384]{1,0:T(4,128)} %param.10) | copy-start | bytes 589828
  113.2 3.6 %copy-start.2 = (f32[2,16,81,128]{3,2,1,0:T(8,128)S(1)}, f32[2,16,81,128]{3,2,1,0:T(8,128)}, u32[]{:S(2)}) copy-start(f32[2,16,81,128]{3,2,1,0:T(8,128)} %gather.7) | copy-start | bytes 3981316
  114.7 2.2 %collective-permute-start.1 = (f32[16,81,128]{2,0,1:T(8,128)S(1)}, f32[16,81,128]{2,0,1:T(8,128)S(1)}, u32[]{:S(2)}, u32[]{:S(2)}) collective-permute-start(f32[16,81,128]{2,0,1:T(8,128)S(1)} %copy.26), channel_id=1, source_target_pairs={{0,1},{1,0},{2,3},{3,2},{4,5},{5,4},{6,7},{7,6},{8,9},{9,8},{10,11... | collective-permute-start | bytes 1990664 | tf_op jit(solution)/shard_map/ppermute | solution.py:418
  117.9 24.4 %all-to-all-start.1 = ((f32[16,81,128]{2,1,0:T(8,128)}), f32[16,81,128]{2,1,0:T(8,128)}, u32[]{:S(2)}, u32[]{:S(2)}) async-start(f32[16,81,128]{2,1,0:T(8,128)} %fusion.18), calls=%async_computation.1 | async-start | bytes 1441792 | tf_op jit(solution)/shard_map/all_to_all | solution.py:419
  124.4 5.6 %copy-start.3 = (f32[27,16384]{1,0:T(8,128)S(1)}, f32[27,16384]{1,0:T(8,128)}, u32[]{:S(2)}) copy-start(f32[27,16384]{1,0:T(8,128)} %param.12) | copy-start | bytes 5308420
  125.1 14.4 %collective-permute-start.3 = (f32[4,1,3,128]{3,1,0,2:T(1,128)S(1)}, f32[4,1,3,128]{3,1,0,2:T(1,128)S(1)}, u32[]{:S(2)}, u32[]{:S(2)}) collective-permute-start(f32[4,1,3,128]{3,1,0,2:T(1,128)S(1)} %get-tuple-element.10), channel_id=1, source_target_pairs={{0,4},{4,8},{8,12},{12,16},{16,20},{20,24},{24,28},{28,0},{1,5},{5... | collective-permute-start | bytes 18440 | tf_op jit(solution)/shard_map/ppermute | solution.py:29
  126.9 12.6 %collective-permute-start.2 = (f32[4,1,3,128]{3,1,0,2:T(1,128)S(1)}, f32[4,1,3,128]{3,1,0,2:T(1,128)S(1)}, u32[]{:S(2)}, u32[]{:S(2)}) collective-permute-start(f32[4,1,3,128]{3,1,0,2:T(1,128)S(1)} %get-tuple-element.9), channel_id=1, source_target_pairs={{4,0},{8,4},{12,8},{16,12},{20,16},{24,20},{28,24},{0,28},{5,1},{9... | collective-permute-start | bytes 18440 | tf_op jit(solution)/shard_map/ppermute | solution.py:31
  130.4 9.1 %copy-start.6 = (s32[12]{0:T(128)S(1)}, s32[12]{0:T(128)}, u32[]{:S(2)}) copy-start(s32[12]{0:T(128)} %param.16) | copy-start | bytes 148

commit v3 on v2

--- a/solution.py
+++ b/solution.py
@@ -12,6 +12,7 @@
 HALF = G // 2
 STENCIL = 27
 SIDE = 3
+FINE = 4
 AXES = ("row", "half", "core")
 PEERS = ("row", "half")
 
@@ -94,65 +95,89 @@
         stencils[2 * j + 1 - core] = other[j]
 
 
+def cosine(turns):
+    turns = turns & (G - 1)
+    turns = jnp.minimum(turns, G - turns)
+    flipped = turns > G // 4
+    angle = jnp.where(flipped, G // 2 - turns, turns).astype(jnp.float32) * (2.0 * math.pi / G)
+    square = angle * angle
+    total = jnp.full_like(square, 1.0 / math.factorial(12))
+    for order in (10, 8, 6, 4, 2, 0):
+        total = total * square + (-1.0) ** (order // 2) / math.factorial(order)
+    return jnp.where(flipped, -total, total)
+
+
 def scatter_kernel(live, where, mine, other, out, phases, stencils, spread, hot, total):
-    parts, slab, _ = out.shape
+    sides, parts, slab, lanes = out.shape
     cols, _, clusters = stencils.shape
+    span = G // cols
+    high_cells = slab // FINE
     corner = pl.program_id(0) * slab
     ordered(where[0], mine, other, stencils)
     bins = lax.broadcasted_iota(jnp.int32, phases.shape[2:], 0)
     waves = bins // 2 + where[1]
-    quarter = bins % 2 * (G // 4) + HALF
+    quarter = bins % 2 * (G // 4)
     kept = bins < 2 * live
-
-    def block(c, carry):
-        first = stencils[c, 3 * STENCIL : 3 * STENCIL + 1, :] - corner.astype(jnp.float32)
-        second = stencils[c, 3 * STENCIL + 1 : 3 * STENCIL + 2, :]
-        rows = lax.broadcasted_iota(jnp.int32, (G, clusters), 0).astype(jnp.float32)
-        first_wide = jnp.broadcast_to(first, (2 * parts, clusters)).astype(jnp.bfloat16)
-        third = stencils[c, 3 * STENCIL + 2 : 3 * STENCIL + 3, :].astype(jnp.int32)
+    bf16 = jnp.bfloat16
+    columns = lax.broadcasted_iota(jnp.int32, (FINE * span, clusters), 0)
+    columns = columns.astype(jnp.float32).astype(bf16)
+    for c in range(cols):
+        first, second, third = (
+            stencils[c, 3 * STENCIL + i : 3 * STENCIL + i + 1, :].astype(jnp.int32)
+            for i in range(3)
+        )
         for z in range(SIDE):
-            turns = (((third + z) * waves + quarter) & (G - 1)) - HALF
-            turned = jnp.cos(turns.astype(jnp.float32) * (2.0 * math.pi / G))
-            phases[c, z] = jnp.where(kept, turned, 0.0)
-        for y in range(SIDE):
-            lanes = pl.ds(pl.multiple_of((c * SIDE + y) * clusters, clusters), clusters)
-            hot[:, lanes] = jnp.where(rows == second + y, 1.0, 0.0).astype(jnp.bfloat16)
-            tiles = []
-            for x in range(SIDE):
+            phases[c, z] = jnp.where(kept, cosine((third + z) * waves + quarter), 0.0)
+        for x in range(SIDE):
+            cell = first - corner + x
+            fine = (cell & (FINE - 1)) * span + second - c * span
+            coarse = (cell // FINE).astype(jnp.float32)
+            coarse = jnp.broadcast_to(coarse, (2 * parts, clusters)).astype(bf16)
+            for y in range(SIDE):
+                at = slice((x * SIDE + y) * clusters, (x * SIDE + y + 1) * clusters)
+                target = jnp.broadcast_to((fine + y).astype(jnp.float32), columns.shape)
+                hot[c, :, at] = jnp.where(
+                    columns == target.astype(bf16), jnp.ones_like(columns), jnp.zeros_like(columns)
+                )
                 modes = []
                 for a in range(3):
-                    at = a * STENCIL + x * 9 + y * 3
+                    row = a * STENCIL + x * 9 + y * 3
                     modes.append(
-                        sum(stencils[c, at + z : at + z + 1, :] * phases[c, z] for z in range(SIDE))
+                        sum(
+                            stencils[c, row + z : row + z + 1, :] * phases[c, z]
+                            for z in range(SIDE)
+                        )
                     )
                 modes = jnp.concatenate(modes, axis=0)
-                low = modes - modes.astype(jnp.bfloat16).astype(jnp.float32)
-                tiles.append(jnp.concatenate([modes, low], axis=0).astype(jnp.bfloat16))
-            blank = jnp.zeros_like(tiles[0])
-            for cell in range(slab):
-                value = blank
-                for x in range(SIDE):
-                    value = jnp.where(
-                        first_wide == jnp.asarray(cell - x, jnp.bfloat16), tiles[x], value
+                low = modes - modes.astype(bf16).astype(jnp.float32)
+                tile = jnp.concatenate([modes, low], axis=0).astype(bf16)
+                for h in range(high_cells):
+                    spread[c, h, :, at] = jnp.where(
+                        coarse == jnp.asarray(h, bf16), tile, jnp.zeros_like(tile)
                     )
-                spread[cell, :, lanes] = value
-        return carry
-
-    lax.fori_loop(0, cols, block, 0)
-    result = lax.dot_general(
-        spread[...].reshape(slab * 2 * parts, hot.shape[1]),
-        hot[...],
-        (((1,), (1,)), ((), ())),
-        preferred_element_type=jnp.float32,
-    )
-    for side in range(2):
-        total[side] = result[:, side * HALF : (side + 1) * HALF]
-    for side in range(2):
-        for v in range(parts):
-            out[v, :, side * HALF : (side + 1) * HALF] = (
-                total[side, pl.ds(v, slab, stride=2 * parts), :]
-                + total[side, pl.ds(parts + v, slab, stride=2 * parts), :]
-            )
+        result = lax.dot_general(
+            spread[c].reshape(high_cells * 2 * parts, SIDE * SIDE * clusters),
+            hot[c],
+            (((1,), (1,)), ((), ())),
+            preferred_element_type=jnp.float32,
+        )
+        for part in range(total.shape[1]):
+            total[c, part] = result[:, part * lanes : (part + 1) * lanes]
+    across = lanes // span
+    for side in range(sides):
+        for fine in range(FINE):
+            part, start = divmod(fine * span, lanes)
+            for v in range(parts):
+                pieces = []
+                for c in range(side * across, (side + 1) * across):
+                    piece = (
+                        total[c, part, pl.ds(v, high_cells, stride=2 * parts), :]
+                        + total[c, part, pl.ds(parts + v, high_cells, stride=2 * parts), :]
+                    )
+                    pieces.append(piece[:, start : start + span])
+                out[side, v, pl.ds(fine, high_cells, stride=FINE), :] = jnp.concatenate(
+                    pieces, axis=1
+                )
 
 
 def dft_kernel(signs, thirds, field, tx, txt, ty, tyt, out, lines, modes, high, low):
@@ -166,7 +191,7 @@
         for a in range(3):
             for part in range(2):
                 stage(
-                    field[a, 0, part, :, :HALF] + signs[p] * field[a, 0, part, :, HALF:],
+                    field[0, a, 0, part] + signs[p] * field[1, a, 0, part],
                     (slice(a * G, (a + 1) * G), slice(part * HALF, (part + 1) * HALF)),
                 )
         for a in range(3):
@@ -250,12 +275,12 @@
             near = result if near is None else near + result
             far = signs[p] * result if far is None else far + signs[p] * result
         for part in range(2):
-            out[a, 0, part, :, :HALF] = near[:, part * HALF : (part + 1) * HALF]
-            out[a, 0, part, :, HALF:] = far[:, part * HALF : (part + 1) * HALF]
+            out[0, a, 0, part] = near[:, part * HALF : (part + 1) * HALF]
+            out[1, a, 0, part] = far[:, part * HALF : (part + 1) * HALF]
 
 
 def gather_kernel(where, mine, other, phases, field, out, stencils, lines, found):
-    parts, slab, _ = field.shape
+    _, parts, slab, _ = field.shape
     cols, _, clusters = stencils.shape
     ordered(where[0], mine, other, stencils)
     bins = parts // 3
@@ -263,9 +288,7 @@
     corner = (pl.program_id(0) * slab).astype(jnp.float32)
     for v in range(parts):
         for side in range(2):
-            lines[side, pl.ds(v, slab, stride=parts), :] = field[
-                v, :, side * HALF : (side + 1) * HALF
-            ]
+            lines[side, pl.ds(v, slab, stride=parts), :] = field[side, v]
     for c in range(cols):
         first = stencils[c, 3 * STENCIL : 3 * STENCIL + 1, :] - corner
         second = stencils[c, 3 * STENCIL + 1 : 3 * STENCIL + 2, :]
@@ -364,27 +387,27 @@
     smem = pl.BlockSpec(memory_space=pltpu.SMEM)
     peer_row = pl.BlockSpec((halves, height, clusters), lambda r: (r, 0, 0))
     phase_row = pl.BlockSpec((cols_total, SIDE, 2 * bins, clusters), lambda r: (r, 0, 0, 0))
-    slab_block = pl.BlockSpec((parts, slab, G), lambda r: (0, r, 0))
-    lanes = cols_total * SIDE * clusters
+    slab_block = pl.BlockSpec((2, parts, slab, HALF), lambda r: (0, 0, r, 0))
+    span = G // cols_total
     field, phases = pl.pallas_call(
         lambda *refs: scatter_kernel(third_live, *refs),
         grid=(rows_total,),
         in_specs=[smem, peer_row, peer_row],
         out_specs=[slab_block, phase_row],
         out_shape=[
-            jax.ShapeDtypeStruct((parts, G, G), f32),
+            jax.ShapeDtypeStruct((2, parts, G, HALF), f32),
             jax.ShapeDtypeStruct((devices, SIDE, 2 * bins, clusters), f32),
         ],
         scratch_shapes=[
             pltpu.VMEM((cols_total, height, clusters), f32),
-            pltpu.VMEM((slab, 2 * parts, lanes), bf16),
-            pltpu.VMEM((G, lanes), bf16),
-            pltpu.VMEM((2, slab * 2 * parts, HALF), f32),
+            pltpu.VMEM((cols_total, slab // FINE, 2 * parts, SIDE * SIDE * clusters), bf16),
+            pltpu.VMEM((cols_total, FINE * span, SIDE * SIDE * clusters), bf16),
+            pltpu.VMEM((cols_total, FINE * span // HALF, slab // FINE * 2 * parts, HALF), f32),
         ],
         name="scatter",
     )(where, mine, other)
 
-    plane = pl.BlockSpec((3, 1, 2, G, G), lambda m: (0, m, 0, 0, 0))
+    plane = pl.BlockSpec((2, 3, 1, 2, G, HALF), lambda m: (0, 0, m, 0, 0, 0))
     table = pl.BlockSpec((2, 2, G, G), lambda m: (0, 0, 0, 0))
     table_y = pl.BlockSpec((pars, 2, G, G), lambda m: (0, 0, 0, 0))
     field = pl.pallas_call(
@@ -392,7 +415,7 @@
         grid=(bins,),
         in_specs=[smem, smem, plane, table, table, table_y, table_y],
         out_specs=plane,
-        out_shape=jax.ShapeDtypeStruct((3, bins, 2, G, G), f32),
+        out_shape=jax.ShapeDtypeStruct((2, 3, bins, 2, G, HALF), f32),
         scratch_shapes=[
             pltpu.VMEM((3, 2, G, width), f32),
             pltpu.VMEM((3, 2, G, width), f32),
@@ -400,7 +423,7 @@
             pltpu.VMEM((3 * G, G), bf16),
         ],
         name="spectral",
-    )(signs, thirds, field.reshape(3, bins, 2, G, G), tx, txt, ty, tyt)
+    )(signs, thirds, field.reshape(2, 3, bins, 2, G, HALF), tx, txt, ty, tyt)
 
     sampled = pl.pallas_call(
         gather_kernel,
@@ -414,7 +437,7 @@
             pltpu.VMEM((slab * parts, SIDE * clusters), f32),
         ],
         name="gather",
-    )(where, mine, other, phases, field.reshape(parts, G, G))
+    )(where, mine, other, phases, field.reshape(2, parts, G, HALF))
     sampled = sampled[0] + lax.ppermute(sampled[1], "core", swap)
     sampled = lax.all_to_all(sampled, PEERS, 0, 0, tiled=True)
     sampled = jnp.sum(sampled, axis=0).reshape(3, STENCIL, clusters)

time: 153 us -> 141 us (0.922)
  Pallas kernels: 65.7 us -> 53.6 us
    pallas_call x1, Pallas kernels: 33.8 us -> 21.7 us  [per_device(): pl.pallas_call(lambda *refs: scatter_kernel(third_live, *refs), grid=(row...]
  transfers between devices with their start and end apart: 5 -> 5, of which waited for: 3 -> 3; matrix products, arithmetic and copies ran while one was open for 6% -> 7% of each run, Pallas kernels for 0% -> 0%
where the time goes in v3:
time: 141 us; the launch traced here: 140 us
  Pallas kernels  53.6 us (38%)
  blocking collectives  28.1 us (20%)
  local copies, waits for them, and re-layouts  19.8 us (14%)
  matrix products  11.5 us (8%)
  waiting for transfers between devices  9.82 us (7%)
  starting transfers between devices  9.35 us (7%)
  other arithmetic  6.99 us (5%)
    all_to_all x1, blocking collectives, per_device(): lax.all_to_all(jnp.broadcast_to(packed[None], (peers, height, clusters)),...  28.1 us
    pallas_call x1, Pallas kernels, per_device(): pl.pallas_call(lambda *refs: scatter_kernel(third_live, *refs), grid=(row...  21.7 us
    pallas_call x1, Pallas kernels, per_device(): pl.pallas_call(dft_kernel, grid=(bins,), in_specs=[smem, smem, plane, tab...  19.4 us
    pallas_call x1, Pallas kernels, per_device(): pl.pallas_call(gather_kernel, grid=(rows_total,), in_specs=[smem, peer_ro...  12.4 us
    ppermute x1, waiting for transfers between devices, padded(): lax.ppermute(tail, axis, [(i, (i + 1) % count) for i in range(count)])  7.76 us
    dot_general x1, matrix products, per_device(): jnp.einsum('csk,skp->ckp', sampled, weights_out, precision=precise)  4.95 us
    dot_general x1, matrix products, per_device(): spread = jnp.einsum('ckp,skp->csk', charges, weights_in, precision=precise)  4.91 us
    all_to_all x1, starting transfers between devices, per_device(): sampled = lax.all_to_all(sampled, PEERS, 0, 0, tiled=True)  4.28 us
  transfers between devices with their start and end apart: 5, of which 3 were waited for; matrix products, arithmetic and copies ran while one was open for 7% of the time, Pallas kernels for 0%

profile of v3, /device:TPU:0, one launch (start us, length us, event | category | flops | bytes accessed | tf_op | source)
XLA Modules:
  0.0 140.0 jit_solution(16401325903036089517)
XLA Ops:
  0.0 0.0 copy-start
  0.0 0.8 convert_element_type.21
  0.8 2.1 %copy.34 = f32[4,8,128,128]{3,2,1,0:T(8,128)S(1)} copy(f32[4,8,128,128]{3,1,2,0:T(8,128)} %bitcast.49) | data formatting | bytes 4194304
  3.0 0.0 copy-start.4
  3.0 0.2 slice.32
  3.2 0.8 copy-done.4
  3.9 4.9 %fusion.6 = f32[3,27,128]{1,0,2:T(4,128)} fusion(f32[27,128,128]{2,1,0:T(8,128)S(1)} %slice.32, f32[3,16384]{1,0:T(4,128)S(1)} %copy-done.4), kind=kOutput, calls=%fused_computation.7 | convolution fusion | flops 15925248 | bytes 2007552 | tf_op jit(solution)/shard_map/ckp,skp->csk/dot_general | solution.py:356
  8.8 1.7 %copy.22 = f32[3,27,128]{2,1,0:T(8,128)} copy(f32[3,27,128]{1,0,2:T(4,128)} %fusion.6) | data formatting | bytes 82944 | tf_op jit(solution)/shard_map/ckp,skp->csk/transpose | solution.py:356
  10.5 1.4 %reshape.67 = f32[81,128]{1,0:T(8,128)} reshape(f32[3,27,128]{2,1,0:T(8,128)} %copy.22) | data formatting | bytes 82944 | tf_op jit(solution)/shard_map/reshape | solution.py:358
  11.9 0.8 pad_maximum_fusion
  12.8 28.1 %all_to_all.10.refs_1_.mine = f32[16,84,128]{2,1,0:T(8,128)S(1)} all-to-all(f32[16,84,128]{2,1,0:T(8,128)S(1)} %broadcast_in_dim.31), channel_id=1, replica_groups=mesh['row'=8,'half'=2,'core'=2] {'row','half'}, dimensions={0} | all-to-all | bytes 1376256 | tf_op jit(solution)/shard_map/all_to_all | solution.py:362
  40.9 0.0 copy-start.1
  40.9 0.9 copy-done.1
  41.9 1.0 copy.23
  42.9 0.0 collective-permute-start
  42.9 0.5 multiply_subtract_fusion.signs
  43.4 0.6 pad_add_fusion.refs_0_.where
  44.0 0.6 pad_maximum_fusion.2.thirds
  44.6 0.8 collective-permute-done
  45.4 2.2 %copy.25.refs_2_.other = f32[16,84,128]{2,1,0:T(8,128)} copy(f32[16,84,128]{2,0,1:T(8,128)} %collective-permute-done) | data formatting | bytes 1376256 | tf_op jit(solution)/shard_map/ppermute | solution.py:365
  47.5 21.7 %scatter.1 = (f32[2,24,256,128]{3,2,1,0:T(8,128)}, f32[32,3,8,128]{3,2,1,0:T(8,128)}) custom-call(s32[2]{0:T(128)} %pad_add_fusion.refs_0_.where, f32[16,84,128]{2,1,0:T(8,128)} %copy-done.1, f32[16,84,128]{2,1,0:T(8,128)} %copy.25.refs_2_.other), custom_call_target="tpu_custom_call" | custom-call | tf_op jit(solution)/shard_map/scatter/pallas_call | solution.py:392
  69.2 19.4 %spectral.1 = f32[2,3,4,2,256,128]{5,4,3,2,1,0:T(8,128)} custom-call(f32[2]{0:T(128)} %multiply_subtract_fusion.signs, f32[2,4]{1,0:T(2,128)} %pad_maximum_fusion.2.thirds, f32[2,3,4,2,256,128]{5,4,3,2,1,0:T(8,128)} %bitcast.48, bf16[2,2,256,256]{3,2,1,0:T(8,128)(2,1)} %constant.60.clone.tx.ty, bf16[2,2,256,256]{3,2,1,0:T(8,128)(2,1)} %constant.61.clone.txt.tyt, ...), custom_call_target="tpu_custom_call" | custom-call | tf_op jit(solution)/shard_map/spectral/pallas_call | solution.py:413
  88.6 12.4 %gather.7 = f32[2,16,81,128]{3,2,1,0:T(8,128)} custom-call(s32[2]{0:T(128)} %pad_add_fusion.refs_0_.where, f32[16,84,128]{2,1,0:T(8,128)} %copy-done.1, f32[16,84,128]{2,1,0:T(8,128)} %copy.25.refs_2_.other, f32[32,3,8,128]{3,2,1,0:T(8,128)} %get-tuple-element.7.phases, f32[2,24,256,128]{3,2,1,0:T(8,128)} %bitcast.45), custom_call_target="tpu_custom_call" | custom-call | tf_op jit(solution)/shard_map/gather/pallas_call | solution.py:428
  101.1 0.0 copy-start.7
  101.1 0.0 copy-start.5
  101.1 0.0 copy-start.2
  101.1 1.3 slice_bitcast_fusion
  102.4 0.1 copy.26
  102.5 0.2 collective-permute-start.1
  102.7 0.0 copy-done.7
  102.7 0.0 copy-done.5
  102.7 0.7 bitcast_convert_fusion
  103.4 1.3 collective-permute-done.1
  104.7 0.0 copy-done.2
  104.7 1.1 fusion.18
  105.8 4.3 %all-to-all-start.1 = ((f32[16,81,128]{2,1,0:T(8,128)}), f32[16,81,128]{2,1,0:T(8,128)}, u32[]{:S(2)}, u32[]{:S(2)}) async-start(f32[16,81,128]{2,1,0:T(8,128)} %fusion.18), calls=%async_computation.1 | async-start | bytes 1441792 | tf_op jit(solution)/shard_map/all_to_all | solution.py:442
  110.7 1.5 %gather_fusion = bf16[12,3,128]{2,1,0:T(4,128)(2,1)S(1)} fusion(bf16[3,128,128]{2,0,1:T(4,128)(2,1)} %bitcast_convert_fusion, s32[1024]{0:T(1024)S(1)} %pad_clamp_fusion), kind=kCustom, calls=%fused_computation | custom fusion | bytes 18480 | tf_op jit(solution)/shard_map/gather | solution.py:44
  112.2 0.0 copy-start.3
  112.2 0.0 copy-done
  112.3 0.6 fusion
  112.9 0.1 bitcast_select_fusion
  113.0 1.8 %collective-permute-start.3 = (f32[4,1,3,128]{3,1,0,2:T(1,128)S(1)}, f32[4,1,3,128]{3,1,0,2:T(1,128)S(1)}, u32[]{:S(2)}, u32[]{:S(2)}) collective-permute-start(f32[4,1,3,128]{3,1,0,2:T(1,128)S(1)} %get-tuple-element.10), channel_id=1, source_target_pairs={{0,4},{4,8},{8,12},{12,16},{16,20},{20,24},{24,28},{28,0},{1,5},{5... | collective-permute-start | bytes 18440 | tf_op jit(solution)/shard_map/ppermute | solution.py:30
  114.8 3.1 %collective-permute-start.2 = (f32[4,1,3,128]{3,1,0,2:T(1,128)S(1)}, f32[4,1,3,128]{3,1,0,2:T(1,128)S(1)}, u32[]{:S(2)}, u32[]{:S(2)}) collective-permute-start(f32[4,1,3,128]{3,1,0,2:T(1,128)S(1)} %get-tuple-element.9), channel_id=1, source_target_pairs={{4,0},{8,4},{12,8},{16,12},{20,16},{24,20},{28,24},{0,28},{5,1},{9... | collective-permute-start | bytes 18440 | tf_op jit(solution)/shard_map/ppermute | solution.py:32
  117.9 0.0 copy-done.3
  117.9 0.4 copy.35
  118.2 0.0 copy-start.6
  118.3 1.3 slice.33
  119.6 7.8 %collective-permute-done.3 = f32[4,1,3,128]{3,1,0,2:T(1,128)S(1)} collective-permute-done((f32[4,1,3,128]{3,1,0,2:T(1,128)S(1)}, f32[4,1,3,128]{3,1,0,2:T(1,128)S(1)}, u32[]{:S(2)}, u32[]{:S(2)}) %collective-permute-start.3) | collective-permute-done | bytes 6176 | tf_op jit(solution)/shard_map/ppermute | solution.py:30
  127.4 0.0 collective-permute-done.2
  127.4 0.0 copy-done.6
  127.4 1.0 fusion.20
  128.4 1.8 %copy.30 = f32[3,128,128]{1,0,2:T(4,128)} copy(f32[3,128,128]{2,1,0:T(8,128)} %fusion.20) | data formatting | bytes 393216 | tf_op jit(solution)/shard_map/qk,qbj->bkj/dot_general | solution.py:59
  130.2 0.0 all-to-all-done.1
  130.2 1.8 %reduce_sum.9 = f32[81,128]{1,0:T(8,128)} reduce(f32[16,81,128]{2,1,0:T(8,128)} %all-to-all-done.1, f32[]{:T(128)} %constant.57.clone.1), dimensions={0}, to_apply=%region_0.1 | reduce | flops 155520 | bytes 705028 | tf_op jit(solution)/shard_map/reduce_sum | solution.py:443
  132.0 1.4 %reshape.70 = f32[3,27,128]{2,1,0:T(8,128)} reshape(f32[81,128]{1,0:T(8,128)} %reduce_sum.9) | data formatting | bytes 82944 | tf_op jit(solution)/shard_map/reshape | solution.py:443
  133.4 1.6 %copy.28 = f32[3,27,128]{1,0,2:T(4,128)} copy(f32[3,27,128]{2,1,0:T(8,128)} %reshape.70) | data formatting | bytes 82944 | tf_op jit(solution)/shard_map/reshape | solution.py:443
  135.0 5.0 %fusion.15 = f32[3,16384]{1,0:T(4,128)} fusion(f32[3,27,128]{1,0,2:T(4,128)} %copy.28, f32[27,128,128]{2,1,0:T(8,128)} %slice.33, f32[3,128,128]{1,0,2:T(4,128)} %copy.30), kind=kOutput, calls=%fused_computation.10 | convolution fusion | flops 15974400 | bytes 2204160 | tf_op jit(solution)/shard_map/csk,skp->ckp/dot_general | solution.py:444
  (10 shorter events, 0.1 us)
Async XLA Ops:
  0.0 112.2 %copy-start = (bf16[12,3,3,128,128]{4,3,2,1,0:T(8,128)(2,1)S(1)}, bf16[12,3,3,128,128]{4,3,2,1,0:T(8,128)(2,1)}, u32[]{:S(2)}) copy-start(bf16[12,3,3,128,128]{4,3,2,1,0:T(8,128)(2,1)} %param.14) | copy-start | bytes 10616836
  3.0 1.0 copy-start.4
  40.9 0.9 copy-start.1
  42.9 2.5 %collective-permute-start = (f32[16,84,128]{2,0,1:T(8,128)}, f32[16,84,128]{2,0,1:T(8,128)}, u32[]{:S(2)}, u32[]{:S(2)}) collective-permute-start(f32[16,84,128]{2,0,1:T(8,128)} %copy.23), channel_id=1, source_target_pairs={{0,1},{1,0},{2,3},{3,2},{4,5},{5,4},{6,7},{7,6},{8,9},{9,8},{10,11... | collective-permute-start | bytes 2064392 | tf_op jit(solution)/shard_map/ppermute | solution.py:365
  101.1 1.6 %copy-start.7 = (s32[12]{0:T(128)S(1)}, s32[12]{0:T(128)}, u32[]{:S(2)}) copy-start(s32[12]{0:T(128)} %param.15) | copy-start | bytes 148
  101.1 1.6 %copy-start.5 = (f32[3,16384]{1,0:T(4,128)S(1)}, f32[3,16384]{1,0:T(4,128)}, u32[]{:S(2)}) copy-start(f32[3,16384]{1,0:T(4,128)} %param.10) | copy-start | bytes 589828
  101.1 3.6 %copy-start.2 = (f32[2,16,81,128]{3,2,1,0:T(8,128)S(1)}, f32[2,16,81,128]{3,2,1,0:T(8,128)}, u32[]{:S(2)}) copy-start(f32[2,16,81,128]{3,2,1,0:T(8,128)} %gather.7) | copy-start | bytes 3981316
  102.5 2.2 %collective-permute-start.1 = (f32[16,81,128]{2,0,1:T(8,128)S(1)}, f32[16,81,128]{2,0,1:T(8,128)S(1)}, u32[]{:S(2)}, u32[]{:S(2)}) collective-permute-start(f32[16,81,128]{2,0,1:T(8,128)S(1)} %copy.26), channel_id=1, source_target_pairs={{0,1},{1,0},{2,3},{3,2},{4,5},{5,4},{6,7},{7,6},{8,9},{9,8},{10,11... | collective-permute-start | bytes 1990664 | tf_op jit(solution)/shard_map/ppermute | solution.py:441
  105.8 24.4 %all-to-all-start.1 = ((f32[16,81,128]{2,1,0:T(8,128)}), f32[16,81,128]{2,1,0:T(8,128)}, u32[]{:S(2)}, u32[]{:S(2)}) async-start(f32[16,81,128]{2,1,0:T(8,128)} %fusion.18), calls=%async_computation.1 | async-start | bytes 1441792 | tf_op jit(solution)/shard_map/all_to_all | solution.py:442
  112.2 5.6 %copy-start.3 = (f32[27,16384]{1,0:T(8,128)S(1)}, f32[27,16384]{1,0:T(8,128)}, u32[]{:S(2)}) copy-start(f32[27,16384]{1,0:T(8,128)} %param.12) | copy-start | bytes 5308420
  113.0 14.4 %collective-permute-start.3 = (f32[4,1,3,128]{3,1,0,2:T(1,128)S(1)}, f32[4,1,3,128]{3,1,0,2:T(1,128)S(1)}, u32[]{:S(2)}, u32[]{:S(2)}) collective-permute-start(f32[4,1,3,128]{3,1,0,2:T(1,128)S(1)} %get-tuple-element.10), channel_id=1, source_target_pairs={{0,4},{4,8},{8,12},{12,16},{16,20},{20,24},{24,28},{28,0},{1,5},{5... | collective-permute-start | bytes 18440 | tf_op jit(solution)/shard_map/ppermute | solution.py:30
  114.8 12.6 %collective-permute-start.2 = (f32[4,1,3,128]{3,1,0,2:T(1,128)S(1)}, f32[4,1,3,128]{3,1,0,2:T(1,128)S(1)}, u32[]{:S(2)}, u32[]{:S(2)}) collective-permute-start(f32[4,1,3,128]{3,1,0,2:T(1,128)S(1)} %get-tuple-element.9), channel_id=1, source_target_pairs={{4,0},{8,4},{12,8},{16,12},{20,16},{24,20},{28,24},{0,28},{5,1},{9... | collective-permute-start | bytes 18440 | tf_op jit(solution)/shard_map/ppermute | solution.py:32
  118.2 9.1 %copy-start.6 = (s32[12]{0:T(128)S(1)}, s32[12]{0:T(128)}, u32[]{:S(2)}) copy-start(s32[12]{0:T(128)} %param.16) | copy-start | bytes 148

commit v4 on v3

--- a/solution.py
+++ b/solution.py
@@ -13,31 +13,25 @@
 STENCIL = 27
 SIDE = 3
 FINE = 4
-AXES = ("row", "half", "core")
-PEERS = ("row", "half")
-
-precise = lax.Precision.HIGHEST
+ROW = ("z", "x")
+PLANE = ("x", "y")
+AXES = ("z", "x", "y", "core")
+
 screen_shift = 0.5
 
 
-def padded(cells, sides, width):
-    for axis, dim in sides:
-        count = lax.axis_size(axis)
-        head = lax.slice_in_dim(cells, 0, width, axis=dim)
-        tail = lax.slice_in_dim(cells, cells.shape[dim] - width, cells.shape[dim], axis=dim)
-        cells = jnp.concatenate(
-            [
-                lax.ppermute(tail, axis, [(i, (i + 1) % count) for i in range(count)]),
-                cells,
-                lax.ppermute(head, axis, [((i + 1) % count, i) for i in range(count)]),
-            ],
-            axis=dim,
-        )
-    return cells
-
-
-def near_field(charges, near_tiles, pair_target, pair_landing, pair_count):
-    clusters, panels = charges.shape[1:]
+def swapped(values, axes, offset):
+    count = lax.axis_size(axes)
+    return lax.ppermute(values, axes, [(i, i ^ offset) for i in range(count)])
+
+
+def row_shift(values, by):
+    count = lax.axis_size(ROW)
+    return lax.ppermute(values, ROW, [(i, (i + by) % count) for i in range(count)])
+
+
+def near_field(charges, near_tiles, pair_target, pair_count):
+    panels = charges.shape[2]
     rounded = charges.astype(jnp.bfloat16)
     slot_total = pair_target.shape[0]
     slot_group = slot_total // 3
@@ -50,13 +44,10 @@
         live_mask[:, None, None], partial_value, jnp.zeros_like(partial_value)
     )
     leaving = partial_value[slot_group:].reshape(slot_group, 2, 3, panels)
-    arrived = padded(leaving, (("row", 1),), 1)
-    crossing = jnp.stack([arrived[:, 3], arrived[:, 0]], axis=1).reshape(2 * slot_group, 3, panels)
-    incoming = jnp.concatenate([partial_value[:slot_group], crossing], axis=0)
-    landing_hot = (pair_landing[:, None] == jnp.arange(clusters, dtype=jnp.int32)[None, :]).astype(
-        jnp.float32
-    )
-    return jnp.einsum("qk,qbj->bkj", landing_hot, incoming, precision=precise)
+    crossing = jnp.stack([row_shift(leaving[:, 0], -1), row_shift(leaving[:, 1], 1)], axis=1)
+    return jnp.concatenate(
+        [partial_value[:slot_group], crossing.reshape(2 * slot_group, 3, panels)], axis=0
+    )
 
 
 def half_tables():
@@ -89,10 +80,57 @@
     )
 
 
-def ordered(core, mine, other, stencils):
-    for j in range(mine.shape[0]):
-        stencils[2 * j + core] = mine[j]
-        stencils[2 * j + 1 - core] = other[j]
+def spread_kernel(density, weights, corners, out):
+    clusters = corners.shape[1]
+    panels = density.shape[1] // clusters
+    unroll = 8
+    lane = lax.broadcasted_iota(jnp.int32, (STENCIL, clusters), 1)
+
+    def some(i, sums):
+        for j in range(unroll):
+            k = i * unroll + j
+            at = pl.ds(pl.multiple_of(k * panels, panels), panels)
+            weight = weights[:, at]
+            sums = tuple(
+                jnp.where(
+                    lane == k,
+                    jnp.sum(weight * density[a : a + 1, at], axis=1, keepdims=True),
+                    sums[a],
+                )
+                for a in range(3)
+            )
+        return sums
+
+    blank = jnp.zeros((STENCIL, clusters), jnp.float32)
+    sums = lax.fori_loop(0, clusters // unroll, some, (blank, blank, blank))
+    for a in range(3):
+        out[a * STENCIL : (a + 1) * STENCIL, :] = sums[a]
+    out[3 * STENCIL :, :] = corners[...].astype(jnp.float32)
+
+
+def final_kernel(landing, near, weights, *refs):
+    *samples, out = refs
+    clusters = samples[0].shape[1]
+    panels = weights.shape[1] // clusters
+    total = sum(sample[...] for sample in samples[1:]) + samples[0][...]
+    columns = [total[a * STENCIL : (a + 1) * STENCIL] for a in range(3)]
+    for k in range(clusters):
+        at = slice(k * panels, (k + 1) * panels)
+        weight = weights[:, at]
+        for a in range(3):
+            out[a : a + 1, at] = jnp.sum(
+                columns[a][:, k : k + 1] * weight, axis=0, keepdims=True
+            )
+    for q in range(near.shape[0]):
+        at = pl.ds(pl.multiple_of(landing[q] * panels, panels), panels)
+        out[:, at] = out[:, at] + near[q]
+
+
+def ordered(where, mine, other, stencils):
+    for j in range(mine.shape[1]):
+        y = j ^ where[4]
+        stencils[2 * y + where[0]] = mine[0, j, 0]
+        stencils[2 * y + 1 - where[0]] = other[0, j, 0]
 
 
 def cosine(turns):
@@ -113,7 +151,7 @@
     span = G // cols
     high_cells = slab // FINE
     corner = pl.program_id(0) * slab
-    ordered(where[0], mine, other, stencils)
+    ordered(where, mine, other, stencils)
     bins = lax.broadcasted_iota(jnp.int32, phases.shape[2:], 0)
     waves = bins // 2 + where[1]
     quarter = bins % 2 * (G // 4)
@@ -282,7 +320,7 @@
 def gather_kernel(where, mine, other, phases, field, out, stencils, lines, found):
     _, parts, slab, _ = field.shape
     cols, _, clusters = stencils.shape
-    ordered(where[0], mine, other, stencils)
+    ordered(where, mine, other, stencils)
     bins = parts // 3
     span = G // cols
     corner = (pl.program_id(0) * slab).astype(jnp.float32)
@@ -315,7 +353,7 @@
                     mode = sums[x][a * bins : (a + 1) * bins]
                     for z in range(SIDE):
                         at = a * STENCIL + x * 9 + y * 3 + z
-                        out[(c + where[0]) % 2, c // 2, at : at + 1, :] = jnp.sum(
+                        out[(c + where[0]) % 2, 0, (c // 2) ^ where[4], 0, at : at + 1, :] = jnp.sum(
                             mode * phases[c, z], axis=0, keepdims=True
                         )
 
@@ -332,13 +370,12 @@
 ):
     clusters = stencil_corner.shape[1]
     panels = density.shape[1] // clusters
-    rows_total = lax.axis_size("row")
-    halves = lax.axis_size("half")
-    cols_total = halves * lax.axis_size("core")
+    deep, wide, high = (lax.axis_size(axis) for axis in AXES[:3])
+    here = [lax.axis_index(axis) for axis in AXES]
+    rows_total = deep * wide
+    cols_total = high * lax.axis_size("core")
     devices = rows_total * cols_total
-    core = lax.axis_index("core")
-    device = lax.axis_index("row") * cols_total + lax.axis_index("half") * 2 + core
-    swap = [(0, 1), (1, 0)]
+    device = lax.axis_index(AXES)
     slab = G // rows_total
     kept_bins = G // 2
     third_parts = min(devices, kept_bins)
@@ -351,18 +388,16 @@
     f32, bf16 = jnp.float32, jnp.bfloat16
 
     charges = density.reshape(3, clusters, panels)
-    weights_in = interp_weight.reshape(STENCIL, clusters, panels)
-    weights_out = proj_weight.reshape(STENCIL, clusters, panels)
-    spread = jnp.einsum("ckp,skp->csk", charges, weights_in, precision=precise)
-    packed = jnp.concatenate(
-        [spread.reshape(3 * STENCIL, clusters), stencil_corner.astype(f32)], axis=0
-    )
     height = 3 * STENCIL + 3
-    peers = devices // 2
-    mine = lax.all_to_all(
-        jnp.broadcast_to(packed[None], (peers, height, clusters)), PEERS, 0, 0, tiled=True
-    )
-    other = lax.ppermute(mine, "core", swap)
+    packed = pl.pallas_call(
+        spread_kernel,
+        out_shape=jax.ShapeDtypeStruct((height, clusters), f32),
+        name="spread",
+    )(density, interp_weight, stencil_corner)
+    line = jnp.stack([packed] + [swapped(packed, "z", o) for o in range(1, deep)])
+    mine = jnp.stack([line] + [swapped(line, PLANE, o) for o in range(1, wide * high)])
+    mine = mine.reshape(wide, high, deep, height, clusters)
+    other = swapped(mine, "core", 1)
 
     step = jnp.arange(bins, dtype=jnp.int32)
     third_bins = (device // second_parts) * third_live + step
@@ -373,7 +408,8 @@
     first_parity = device % second_parts
     signs = 1.0 - 2.0 * (first_parity + jnp.arange(pars, dtype=jnp.int32)).astype(f32)
 
-    where = jnp.stack([core, (device // second_parts) * third_live]).astype(jnp.int32)
+    where = jnp.stack([here[3], (device // second_parts) * third_live, here[0], here[1], here[2]])
+    where = where.astype(jnp.int32)
 
     tables = half_tables()
     tx = jnp.asarray(tables)
@@ -385,24 +421,32 @@
         tyt = lax.dynamic_slice_in_dim(txt, first_parity, 1, axis=0)
 
     smem = pl.BlockSpec(memory_space=pltpu.SMEM)
-    peer_row = pl.BlockSpec((halves, height, clusters), lambda r: (r, 0, 0))
-    phase_row = pl.BlockSpec((cols_total, SIDE, 2 * bins, clusters), lambda r: (r, 0, 0, 0))
-    slab_block = pl.BlockSpec((2, parts, slab, HALF), lambda r: (0, 0, r, 0))
+    peer_row = pl.BlockSpec(
+        (1, high, 1, height, clusters),
+        lambda r, where: ((r % wide) ^ where[3], 0, (r // wide) ^ where[2], 0, 0),
+    )
+    phase_row = pl.BlockSpec(
+        (cols_total, SIDE, 2 * bins, clusters), lambda r, where: (r, 0, 0, 0)
+    )
+    slab_block = pl.BlockSpec((2, parts, slab, HALF), lambda r, where: (0, 0, r, 0))
     span = G // cols_total
     field, phases = pl.pallas_call(
         lambda *refs: scatter_kernel(third_live, *refs),
-        grid=(rows_total,),
-        in_specs=[smem, peer_row, peer_row],
-        out_specs=[slab_block, phase_row],
+        grid_spec=pltpu.PrefetchScalarGridSpec(
+            num_scalar_prefetch=1,
+            grid=(rows_total,),
+            in_specs=[peer_row, peer_row],
+            out_specs=[slab_block, phase_row],
+            scratch_shapes=[
+                pltpu.VMEM((cols_total, height, clusters), f32),
+                pltpu.VMEM((cols_total, slab // FINE, 2 * parts, SIDE * SIDE * clusters), bf16),
+                pltpu.VMEM((cols_total, FINE * span, SIDE * SIDE * clusters), bf16),
+                pltpu.VMEM((cols_total, FINE * span // HALF, slab // FINE * 2 * parts, HALF), f32),
+            ],
+        ),
         out_shape=[
             jax.ShapeDtypeStruct((2, parts, G, HALF), f32),
             jax.ShapeDtypeStruct((devices, SIDE, 2 * bins, clusters), f32),
-        ],
-        scratch_shapes=[
-            pltpu.VMEM((cols_total, height, clusters), f32),
-            pltpu.VMEM((cols_total, slab // FINE, 2 * parts, SIDE * SIDE * clusters), bf16),
-            pltpu.VMEM((cols_total, FINE * span, SIDE * SIDE * clusters), bf16),
-            pltpu.VMEM((cols_total, FINE * span // HALF, slab // FINE * 2 * parts, HALF), f32),
         ],
         name="scatter",
     )(where, mine, other)
@@ -427,23 +471,37 @@
 
     sampled = pl.pallas_call(
         gather_kernel,
-        grid=(rows_total,),
-        in_specs=[smem, peer_row, peer_row, phase_row, slab_block],
-        out_specs=pl.BlockSpec((2, halves, 3 * STENCIL, clusters), lambda r: (0, r, 0, 0)),
-        out_shape=jax.ShapeDtypeStruct((2, peers, 3 * STENCIL, clusters), f32),
-        scratch_shapes=[
-            pltpu.VMEM((cols_total, height, clusters), f32),
-            pltpu.VMEM((2, slab * parts, HALF), f32),
-            pltpu.VMEM((slab * parts, SIDE * clusters), f32),
-        ],
+        grid_spec=pltpu.PrefetchScalarGridSpec(
+            num_scalar_prefetch=1,
+            grid=(rows_total,),
+            in_specs=[peer_row, peer_row, phase_row, slab_block],
+            out_specs=pl.BlockSpec(
+                (2, 1, high, 1, 3 * STENCIL, clusters),
+                lambda r, where: (0, (r % wide) ^ where[3], 0, (r // wide) ^ where[2], 0, 0),
+            ),
+            scratch_shapes=[
+                pltpu.VMEM((cols_total, height, clusters), f32),
+                pltpu.VMEM((2, slab * parts, HALF), f32),
+                pltpu.VMEM((slab * parts, SIDE * clusters), f32),
+            ],
+        ),
+        out_shape=jax.ShapeDtypeStruct((2, wide, high, deep, 3 * STENCIL, clusters), f32),
         name="gather",
     )(where, mine, other, phases, field.reshape(2, parts, G, HALF))
-    sampled = sampled[0] + lax.ppermute(sampled[1], "core", swap)
-    sampled = lax.all_to_all(sampled, PEERS, 0, 0, tiled=True)
-    sampled = jnp.sum(sampled, axis=0).reshape(3, STENCIL, clusters)
-    far_term = jnp.einsum("csk,skp->ckp", sampled, weights_out, precision=precise)
-    near_term = near_field(charges, near_tiles, pair_target, pair_landing, pair_count)
-    return (far_term + near_term).reshape(3, -1)
+    sampled = sampled.reshape(2, wide * high, deep, 3 * STENCIL, clusters)
+    sampled = sampled[0] + swapped(sampled[1], "core", 1)
+    line = sampled[0] + sum(swapped(sampled[o], PLANE, o) for o in range(1, wide * high))
+    samples = [line[0]] + [swapped(line[o], "z", o) for o in range(1, deep)]
+    near = near_field(
+        density.reshape(3, clusters, panels), near_tiles, pair_target, pair_count
+    )
+    vmem = pl.BlockSpec(memory_space=pltpu.VMEM)
+    return pl.pallas_call(
+        final_kernel,
+        in_specs=[smem] + [vmem] * (2 + deep),
+        out_shape=jax.ShapeDtypeStruct(density.shape, f32),
+        name="final",
+    )(pair_landing, near, proj_weight, *samples)
 
 
 def solution(mesh):
@@ -458,7 +516,11 @@
         P(AXES),
     )
     rows_total, cols_total = (mesh.shape[axis] for axis in ("row", "col"))
-    split_mesh = jax.sharding.Mesh(mesh.devices.reshape(rows_total, cols_total // 2, 2), AXES)
+    high = cols_total // 2
+    wide = high if rows_total % high == 0 else 1
+    split_mesh = jax.sharding.Mesh(
+        mesh.devices.reshape(rows_total // wide, wide, high, 2), AXES
+    )
     return jax.shard_map(
         per_device, mesh=split_mesh, in_specs=in_specs, out_specs=P(None, AXES), check_vma=False
     )

time: 141 us -> 126 us (0.89)
  blocking collectives: 28.1 us -> 0 us
  waiting for transfers between devices: 9.82 us -> 21.2 us
  Pallas kernels: 53.6 us -> 64.9 us
  matrix products: 11.5 us -> 0.62 us
  starting transfers between devices: 9.35 us -> 19.6 us
  local copies, waits for them, and re-layouts: 19.8 us -> 11.1 us
    all_to_all x1 -> x0, blocking collectives: 28.1 us -> none  [per_device(): lax.all_to_all(jnp.broadcast_to(packed[None], (peers, height, clusters)),...]
    ppermute x4 -> x16, starting transfers between devices: 5.07 us -> 19.6 us  [the longest x14 17.6 us: swapped(): return lax.ppermute(values, axes, [(i, i ^ offset) for i in range(count)])]
    ppermute x4 -> x16, waiting for transfers between devices: 9.82 us -> 21.2 us  [the longest x14 14.9 us: swapped(): return lax.ppermute(values, axes, [(i, i ^ offset) for i in range(count)])]
    pallas_call x2 -> x4, Pallas kernels: 34.1 us -> 45.3 us  [the longest x1 22.6 us: per_device(): pl.pallas_call(lambda *refs: scatter_kernel(third_live, *refs), grid_spec...]
    dot_general x3 -> x0, matrix products: 10.9 us -> none  [the longest x1 4.95 us: per_device(): jnp.einsum('csk,skp->ckp', sampled, weights_out, precision=precise)]
    reshape x5 -> x1, local copies, waits for them, and re-layouts: 6 us -> 1.07 us  [per_device(): mine = mine.reshape(wide, high, deep, height, clusters)]
    all_to_all x1 -> x0, starting transfers between devices: 4.28 us -> none  [per_device(): sampled = lax.all_to_all(sampled, PEERS, 0, 0, tiled=True)]
    unnamed x18 -> x14, local copies, waits for them, and re-layouts: 4.23 us -> 1.87 us
  transfers between devices with their start and end apart: 5 -> 16, of which waited for: 3 -> 7; matrix products, arithmetic and copies ran while one was open for 7% -> 5% of each run, Pallas kernels for 0% -> 0%
where the time goes in v4:
time: 126 us
  Pallas kernels  64.9 us (52%)
  waiting for transfers between devices  21.2 us (17%)
  starting transfers between devices  19.6 us (16%)
  local copies, waits for them, and re-layouts  11.1 us (9%)
  other arithmetic  7.59 us (6%)
    pallas_call x1, Pallas kernels, per_device(): pl.pallas_call(lambda *refs: scatter_kernel(third_live, *refs), grid_spec...  22.6 us
    pallas_call x1, Pallas kernels, per_device(): pl.pallas_call(dft_kernel, grid=(bins,), in_specs=[smem, smem, plane, tab...  19.6 us
    ppermute x14, starting transfers between devices, swapped(): return lax.ppermute(values, axes, [(i, i ^ offset) for i in range(count)])  17.6 us
    ppermute x14, waiting for transfers between devices, swapped(): return lax.ppermute(values, axes, [(i, i ^ offset) for i in range(count)])  14.9 us
    pallas_call x1, Pallas kernels, per_device(): pl.pallas_call(gather_kernel, grid_spec=pltpu.PrefetchScalarGridSpec(num_...  13.4 us
    ppermute x2, waiting for transfers between devices, row_shift(): lax.ppermute(values, ROW, [(i, (i + by) % count) for i in range(count)])  6.27 us
    pallas_call x1, Pallas kernels, per_device(): pl.pallas_call(spread_kernel, out_shape=jax.ShapeDtypeStruct((height, clu...  5.23 us
    pallas_call x1, Pallas kernels, per_device(): pl.pallas_call(final_kernel, in_specs=[smem] + [vmem] * (2 + deep), out_s...  4.11 us
  transfers between devices with their start and end apart: 16, of which 7 were waited for; matrix products, arithmetic and copies ran while one was open for 5% of the time, Pallas kernels for 0%

profile of v4, /device:TPU:0, one launch (start us, length us, event | category | flops | bytes accessed | tf_op | source)
XLA Modules:
  0.0 125.8 jit_solution(2877939353440702335)
XLA Ops:
  0.0 0.0 copy-start
  0.0 0.0 copy-start.6
  0.0 5.2 %spread.1 = f32[84,128]{1,0:T(8,128)} custom-call(f32[3,16384]{1,0:T(4,128)} %density.1, f32[27,16384]{1,0:T(8,128)} %weights.2, s32[3,128]{1,0:T(4,128)} %corners.1), custom_call_target="tpu_custom_call" | custom-call | tf_op jit(solution)/shard_map/spread/pallas_call | solution.py:392
  5.2 3.1 %collective-permute-start.2 = (f32[84,128]{1,0:T(8,128)}, f32[84,128]{1,0:T(8,128)S(1)}, u32[]{:S(2)}, u32[]{:S(2)}) collective-permute-start(f32[84,128]{1,0:T(8,128)} %spread.1), channel_id=1, source_target_pairs={{0,8},{8,0},{16,24},{24,16},{1,9},{9,1},{17,25},{25,17},{2,10},{10... | collective-permute-start | bytes 129032 | tf_op jit(solution)/shard_map/ppermute | solution.py:25
  8.3 2.6 %collective-permute-start.3 = (f32[84,128]{1,0:T(8,128)}, f32[84,128]{1,0:T(8,128)S(1)}, u32[]{:S(2)}, u32[]{:S(2)}) collective-permute-start(f32[84,128]{1,0:T(8,128)} %spread.1), channel_id=1, source_target_pairs={{0,16},{8,24},{16,0},{24,8},{1,17},{9,25},{17,1},{25,9},{2,18},{10... | collective-permute-start | bytes 129032 | tf_op jit(solution)/shard_map/ppermute | solution.py:25
  10.9 0.0 collective-permute-start.4
  10.9 0.0 collective-permute-done.2
  10.9 3.4 %collective-permute-done.3 = f32[84,128]{1,0:T(8,128)S(1)} collective-permute-done((f32[84,128]{1,0:T(8,128)}, f32[84,128]{1,0:T(8,128)S(1)}, u32[]{:S(2)}, u32[]{:S(2)}) %collective-permute-start.3) | collective-permute-done | bytes 43040 | tf_op jit(solution)/shard_map/ppermute | solution.py:25
  14.3 2.6 %collective-permute-done.4 = f32[84,128]{1,0:T(8,128)S(1)} collective-permute-done((f32[84,128]{1,0:T(8,128)}, f32[84,128]{1,0:T(8,128)S(1)}, u32[]{:S(2)}, u32[]{:S(2)}) %collective-permute-start.4) | collective-permute-done | bytes 43040 | tf_op jit(solution)/shard_map/ppermute | solution.py:25
  16.9 1.5 %fusion.6 = (f32[1,4,84,128]{3,2,1,0:T(8,128)}, f32[4,84,128]{2,1,0:T(8,128)}) fusion(f32[1,84,128]{2,1,0:T(8,128)S(1)} %bitcast.71, f32[1,84,128]{2,1,0:T(8,128)S(1)} %bitcast.70, f32[1,84,128]{2,1,0:T(8,128)S(1)} %bitcast.69, f32[1,84,128]{2,1,0:T(8,128)} %bitcast.65), kind=kLoop, calls=%fused_computation.32 | loop fusion | flops 129024 | bytes 516096 | tf_op jit(solution)/shard_map/stack | solution.py:398
  18.5 1.5 %collective-permute-start.5 = (f32[4,84,128]{2,1,0:T(8,128)}, f32[4,84,128]{2,1,0:T(8,128)}, u32[]{:S(2)}, u32[]{:S(2)}) collective-permute-start(f32[4,84,128]{2,1,0:T(8,128)} %get-tuple-element.19), channel_id=1, source_target_pairs={{0,2},{2,0},{4,6},{6,4},{1,3},{3,1},{5,7},{7,5},{8,10},{10,8},{12,... | collective-permute-start | bytes 516104 | tf_op jit(solution)/shard_map/ppermute | solution.py:25
  20.0 1.5 %collective-permute-start.6 = (f32[4,84,128]{2,1,0:T(8,128)}, f32[4,84,128]{2,1,0:T(8,128)}, u32[]{:S(2)}, u32[]{:S(2)}) collective-permute-start(f32[4,84,128]{2,1,0:T(8,128)} %get-tuple-element.19), channel_id=1, source_target_pairs={{0,4},{2,6},{4,0},{6,2},{1,5},{3,7},{5,1},{7,3},{8,12},{10,14},{12... | collective-permute-start | bytes 516104 | tf_op jit(solution)/shard_map/ppermute | solution.py:25
  21.5 0.5 collective-permute-start.7
  22.0 4.2 %collective-permute-done.5 = f32[4,84,128]{2,1,0:T(8,128)} collective-permute-done((f32[4,84,128]{2,1,0:T(8,128)}, f32[4,84,128]{2,1,0:T(8,128)}, u32[]{:S(2)}, u32[]{:S(2)}) %collective-permute-start.5) | collective-permute-done | bytes 172064 | tf_op jit(solution)/shard_map/ppermute | solution.py:25
  26.2 0.5 collective-permute-done.6
  26.7 2.1 %collective-permute-done.7 = f32[4,84,128]{2,1,0:T(8,128)} collective-permute-done((f32[4,84,128]{2,1,0:T(8,128)}, f32[4,84,128]{2,1,0:T(8,128)}, u32[]{:S(2)}, u32[]{:S(2)}) %collective-permute-start.7) | collective-permute-done | bytes 172064 | tf_op jit(solution)/shard_map/ppermute | solution.py:25
  28.8 1.2 pad_maximum_fusion
  30.0 0.0 copy-start.1
  30.0 0.9 copy-done.1
  30.9 1.1 copy.17
  32.0 0.0 collective-permute-start.8
  32.0 0.7 stack.70.refs_0_.where
  32.6 0.6 multiply_subtract_fusion.signs
  33.2 0.6 pad_maximum_fusion.4.thirds
  33.8 0.0 copy-done.6
  33.8 1.7 %convert_bitcast_fusion = bf16[3,128,128]{2,0,1:T(4,128)(2,1)} fusion(f32[3,16384]{1,0:T(4,128)} %density.1), kind=kLoop, calls=%fused_computation.11 | loop fusion | flops 49152 | bytes 294912 | tf_op jit(solution)/shard_map/convert_element_type | solution.py:35
  35.5 0.0 collective-permute-done.8
  35.5 2.0 %copy.19.refs_2_.other = f32[2,2,4,84,128]{4,3,2,1,0:T(8,128)} copy(f32[2,2,4,84,128]{4,2,3,1,0:T(4,128)} %collective-permute-done.8) | data formatting | bytes 1376256 | tf_op jit(solution)/shard_map/ppermute | solution.py:25
  37.5 22.6 %scatter.1 = (f32[2,24,256,128]{3,2,1,0:T(8,128)}, f32[32,3,8,128]{3,2,1,0:T(8,128)}) custom-call(s32[5]{0:T(128)} %stack.70.refs_0_.where, f32[2,2,4,84,128]{4,3,2,1,0:T(8,128)} %bitcast.61, f32[2,2,4,84,128]{4,3,2,1,0:T(8,128)} %copy.19.refs_2_.other), custom_call_target="tpu_custom_call" | custom-call | tf_op jit(solution)/shard_map/scatter/pallas_call | solution.py:433
  60.1 19.6 %spectral.1 = f32[2,3,4,2,256,128]{5,4,3,2,1,0:T(8,128)} custom-call(f32[2]{0:T(128)} %multiply_subtract_fusion.signs, f32[2,4]{1,0:T(2,128)} %pad_maximum_fusion.4.thirds, f32[2,3,4,2,256,128]{5,4,3,2,1,0:T(8,128)} %bitcast.63, bf16[2,2,256,256]{3,2,1,0:T(8,128)(2,1)} %constant.63.clone.tx.ty, bf16[2,2,256,256]{3,2,1,0:T(8,128)(2,1)} %constant.64.clone.txt.tyt, ...), custom_call_target="tpu_custom_call" | custom-call | tf_op jit(solution)/shard_map/spectral/pallas_call | solution.py:457
  79.7 13.4 %gather.7 = f32[2,2,2,4,81,128]{5,4,3,2,1,0:T(8,128)} custom-call(s32[5]{0:T(128)} %stack.70.refs_0_.where, f32[2,2,4,84,128]{4,3,2,1,0:T(8,128)} %bitcast.62, f32[2,2,4,84,128]{4,3,2,1,0:T(8,128)} %copy.19.refs_2_.other, f32[32,3,8,128]{3,2,1,0:T(8,128)} %get-tuple-element.7.phases, f32[2,24,256,128]{3,2,1,0:T(8,128)} %bitcast.59), custom_call_target="tpu_custom_call" | custom-call | tf_op jit(solution)/shard_map/gather/pallas_call | solution.py:472
  93.1 2.3 %fusion.7 = (f32[1,2,2,4,81,128]{5,4,3,2,1,0:T(8,128)S(1)}, f32[1,2,2,4,81,128]{5,4,3,2,1,0:T(8,128)}) fusion(f32[2,2,2,4,81,128]{5,4,3,2,1,0:T(8,128)} %gather.7), kind=kLoop, calls=%fused_computation.33 | loop fusion | bytes 2654208 | tf_op jit(solution)/shard_map/slice | solution.py:492
  95.4 1.0 copy.20
  96.4 0.5 collective-permute-start.9
  97.6 1.5 %gather_fusion = bf16[12,3,128]{2,1,0:T(4,128)(2,1)S(1)} fusion(bf16[3,128,128]{2,0,1:T(4,128)(2,1)} %convert_bitcast_fusion, s32[1024]{0:T(1024)S(1)} %pad_clamp_fusion), kind=kCustom, calls=%fused_computation | custom fusion | bytes 18480 | tf_op jit(solution)/shard_map/gather | solution.py:38
  99.1 0.0 copy-start.2
  99.1 0.0 copy-done
  99.1 0.6 fusion
  99.7 0.1 bitcast_select_fusion
  99.8 0.0 collective-permute-done.9
  99.8 0.3 copy-done.2
  100.2 1.2 bitcast_add_fusion
  101.4 1.5 %collective-permute-start.10 = (f32[4,81,128]{2,1,0:T(8,128)S(1)}, f32[4,81,128]{2,1,0:T(8,128)S(1)}, u32[]{:S(2)}, u32[]{:S(2)}) collective-permute-start(f32[4,81,128]{2,1,0:T(8,128)S(1)} %get-tuple-element.13), channel_id=1, source_target_pairs={{0,2},{2,0},{4,6},{6,4},{1,3},{3,1},{5,7},{7,5},{8,10},{10,8},{12,... | collective-permute-start | bytes 497672 | tf_op jit(solution)/shard_map/ppermute | solution.py:25
  102.9 1.5 %collective-permute-start.11 = (f32[4,81,128]{2,1,0:T(8,128)S(1)}, f32[4,81,128]{2,1,0:T(8,128)S(1)}, u32[]{:S(2)}, u32[]{:S(2)}) collective-permute-start(f32[4,81,128]{2,1,0:T(8,128)S(1)} %get-tuple-element.11), channel_id=1, source_target_pairs={{0,4},{2,6},{4,0},{6,2},{1,5},{3,7},{5,1},{7,3},{8,12},{10,14},{12... | collective-permute-start | bytes 497672 | tf_op jit(solution)/shard_map/ppermute | solution.py:25
  104.4 0.6 collective-permute-start.12
  105.0 1.4 %collective-permute-start = (f32[4,3,128]{2,1,0:T(4,128)S(1)}, f32[4,3,128]{2,1,0:T(4,128)S(1)}, u32[]{:S(2)}, u32[]{:S(2)}) collective-permute-start(f32[4,3,128]{2,1,0:T(4,128)S(1)} %get-tuple-element.20), channel_id=1, source_target_pairs={{0,28},{4,0},{8,4},{12,8},{16,12},{20,16},{24,20},{28,24},{1,29},{... | collective-permute-start | bytes 18440 | tf_op jit(solution)/shard_map/ppermute | solution.py:30
  106.4 0.6 collective-permute-start.1
  107.0 6.3 %collective-permute-done = f32[4,3,128]{2,1,0:T(4,128)S(1)} collective-permute-done((f32[4,3,128]{2,1,0:T(4,128)S(1)}, f32[4,3,128]{2,1,0:T(4,128)S(1)}, u32[]{:S(2)}, u32[]{:S(2)}) %collective-permute-start) | collective-permute-done | bytes 6176 | tf_op jit(solution)/shard_map/ppermute | solution.py:30
  113.3 0.0 collective-permute-done.1
  113.3 0.0 collective-permute-done.10
  113.3 0.0 collective-permute-done.11
  113.3 0.0 collective-permute-done.12
  113.4 0.6 slice_bitcast_fusion.4
  114.0 0.0 collective-permute-start.13
  114.0 1.3 collective-permute-start.14
  115.3 3.1 %collective-permute-start.15 = (f32[81,128]{1,0:T(8,128)S(1)}, f32[81,128]{1,0:T(8,128)S(1)}, u32[]{:S(2)}, u32[]{:S(2)}) collective-permute-start(f32[81,128]{1,0:T(8,128)S(1)} %get-tuple-element.14), channel_id=1, source_target_pairs={{0,24},{8,16},{16,8},{24,0},{1,25},{9,17},{17,9},{25,1},{2,26},{10... | collective-permute-start | bytes 124424 | tf_op jit(solution)/shard_map/ppermute | solution.py:25
  118.4 0.6 pad_maximum_fusion.2.near
  119.0 0.0 collective-permute-done.13.refs_1_
  119.0 0.0 collective-permute-done.14.refs_2_
  119.0 2.1 %collective-permute-done.15.refs_3_ = f32[81,128]{1,0:T(8,128)S(1)} collective-permute-done((f32[81,128]{1,0:T(8,128)S(1)}, f32[81,128]{1,0:T(8,128)S(1)}, u32[]{:S(2)}, u32[]{:S(2)}) %collective-permute-start.15) | collective-permute-done | bytes 41504 | tf_op jit(solution)/shard_map/ppermute | solution.py:25
  121.1 0.0 copy-done.3
  121.1 0.0 copy-done.4
  121.1 0.6 copy-done.5
  121.7 4.1 %final.1 = f32[3,16384]{1,0:T(4,128)} custom-call(s32[12]{0:T(128)} %landing.1, f32[12,3,128]{2,1,0:T(4,128)} %pad_maximum_fusion.2.near, f32[27,16384]{1,0:T(8,128)} %weights.3, f32[81,128]{1,0:T(8,128)} %get-tuple-element.17.refs_0_, f32[81,128]{1,0:T(8,128)} %copy-done.3, f32[81,128]{1,0:T(8,128)} %copy-done.4, f32[81,128]{1,0:T(8,128)} %copy-done.5), custom_call_target="tpu_custom_call" | custom-call | tf_op jit(solution)/shard_map/final/pallas_call | solution.py:499
  (14 shorter events, 0.1 us)
Async XLA Ops:
  0.0 99.1 %copy-start = (bf16[12,3,3,128,128]{4,3,2,1,0:T(8,128)(2,1)S(1)}, bf16[12,3,3,128,128]{4,3,2,1,0:T(8,128)(2,1)}, u32[]{:S(2)}) copy-start(bf16[12,3,3,128,128]{4,3,2,1,0:T(8,128)(2,1)} %param.14) | copy-start | bytes 10616836
  0.0 33.8 %copy-start.6 = (s32[12]{0:T(128)S(1)}, s32[12]{0:T(128)}, u32[]{:S(2)}) copy-start(s32[12]{0:T(128)} %param.15) | copy-start | bytes 148
  5.2 5.6 %collective-permute-start.2 = (f32[84,128]{1,0:T(8,128)}, f32[84,128]{1,0:T(8,128)S(1)}, u32[]{:S(2)}, u32[]{:S(2)}) collective-permute-start(f32[84,128]{1,0:T(8,128)} %spread.1), channel_id=1, source_target_pairs={{0,8},{8,0},{16,24},{24,16},{1,9},{9,1},{17,25},{25,17},{2,10},{10... | collective-permute-start | bytes 129032 | tf_op jit(solution)/shard_map/ppermute | solution.py:25
  8.3 6.0 %collective-permute-start.3 = (f32[84,128]{1,0:T(8,128)}, f32[84,128]{1,0:T(8,128)S(1)}, u32[]{:S(2)}, u32[]{:S(2)}) collective-permute-start(f32[84,128]{1,0:T(8,128)} %spread.1), channel_id=1, source_target_pairs={{0,16},{8,24},{16,0},{24,8},{1,17},{9,25},{17,1},{25,9},{2,18},{10... | collective-permute-start | bytes 129032 | tf_op jit(solution)/shard_map/ppermute | solution.py:25
  10.9 6.1 %collective-permute-start.4 = (f32[84,128]{1,0:T(8,128)}, f32[84,128]{1,0:T(8,128)S(1)}, u32[]{:S(2)}, u32[]{:S(2)}) collective-permute-start(f32[84,128]{1,0:T(8,128)} %spread.1), channel_id=1, source_target_pairs={{0,24},{8,16},{16,8},{24,0},{1,25},{9,17},{17,9},{25,1},{2,26},{10... | collective-permute-start | bytes 129032 | tf_op jit(solution)/shard_map/ppermute | solution.py:25
  18.5 7.7 %collective-permute-start.5 = (f32[4,84,128]{2,1,0:T(8,128)}, f32[4,84,128]{2,1,0:T(8,128)}, u32[]{:S(2)}, u32[]{:S(2)}) collective-permute-start(f32[4,84,128]{2,1,0:T(8,128)} %get-tuple-element.19), channel_id=1, source_target_pairs={{0,2},{2,0},{4,6},{6,4},{1,3},{3,1},{5,7},{7,5},{8,10},{10,8},{12,... | collective-permute-start | bytes 516104 | tf_op jit(solution)/shard_map/ppermute | solution.py:25
  20.0 6.7 %collective-permute-start.6 = (f32[4,84,128]{2,1,0:T(8,128)}, f32[4,84,128]{2,1,0:T(8,128)}, u32[]{:S(2)}, u32[]{:S(2)}) collective-permute-start(f32[4,84,128]{2,1,0:T(8,128)} %get-tuple-element.19), channel_id=1, source_target_pairs={{0,4},{2,6},{4,0},{6,2},{1,5},{3,7},{5,1},{7,3},{8,12},{10,14},{12... | collective-permute-start | bytes 516104 | tf_op jit(solution)/shard_map/ppermute | solution.py:25
  21.5 7.3 %collective-permute-start.7 = (f32[4,84,128]{2,1,0:T(8,128)}, f32[4,84,128]{2,1,0:T(8,128)}, u32[]{:S(2)}, u32[]{:S(2)}) collective-permute-start(f32[4,84,128]{2,1,0:T(8,128)} %get-tuple-element.19), channel_id=1, source_target_pairs={{0,6},{2,4},{4,2},{6,0},{1,7},{3,5},{5,3},{7,1},{8,14},{10,12},{12... | collective-permute-start | bytes 516104 | tf_op jit(solution)/shard_map/ppermute | solution.py:25
  30.0 0.9 copy-start.1
  32.0 3.5 %collective-permute-start.8 = (f32[2,2,4,84,128]{4,2,3,1,0:T(4,128)}, f32[2,2,4,84,128]{4,2,3,1,0:T(4,128)}, u32[]{:S(2)}, u32[]{:S(2)}) collective-permute-start(f32[2,2,4,84,128]{4,2,3,1,0:T(4,128)} %copy.17), channel_id=1, source_target_pairs={{0,1},{1,0},{2,3},{3,2},{4,5},{5,4},{6,7},{7,6},{8,9},{9,8},{10,11... | collective-permute-start | bytes 2064392 | tf_op jit(solution)/shard_map/ppermute | solution.py:25
  96.4 3.4 %collective-permute-start.9 = (f32[4,4,81,128]{3,1,2,0:T(4,128)}, f32[4,4,81,128]{3,1,2,0:T(4,128)}, u32[]{:S(2)}, u32[]{:S(2)}) collective-permute-start(f32[4,4,81,128]{3,1,2,0:T(4,128)} %copy.20), channel_id=1, source_target_pairs={{0,1},{1,0},{2,3},{3,2},{4,5},{5,4},{6,7},{7,6},{8,9},{9,8},{10,11... | collective-permute-start | bytes 1990664 | tf_op jit(solution)/shard_map/ppermute | solution.py:25
  99.1 1.1 copy-start.2
  101.4 11.9 %collective-permute-start.10 = (f32[4,81,128]{2,1,0:T(8,128)S(1)}, f32[4,81,128]{2,1,0:T(8,128)S(1)}, u32[]{:S(2)}, u32[]{:S(2)}) collective-permute-start(f32[4,81,128]{2,1,0:T(8,128)S(1)} %get-tuple-element.13), channel_id=1, source_target_pairs={{0,2},{2,0},{4,6},{6,4},{1,3},{3,1},{5,7},{7,5},{8,10},{10,8},{12,... | collective-permute-start | bytes 497672 | tf_op jit(solution)/shard_map/ppermute | solution.py:25
  102.9 10.4 %collective-permute-start.11 = (f32[4,81,128]{2,1,0:T(8,128)S(1)}, f32[4,81,128]{2,1,0:T(8,128)S(1)}, u32[]{:S(2)}, u32[]{:S(2)}) collective-permute-start(f32[4,81,128]{2,1,0:T(8,128)S(1)} %get-tuple-element.11), channel_id=1, source_target_pairs={{0,4},{2,6},{4,0},{6,2},{1,5},{3,7},{5,1},{7,3},{8,12},{10,14},{12... | collective-permute-start | bytes 497672 | tf_op jit(solution)/shard_map/ppermute | solution.py:25
  104.4 8.9 %collective-permute-start.12 = (f32[4,81,128]{2,1,0:T(8,128)S(1)}, f32[4,81,128]{2,1,0:T(8,128)S(1)}, u32[]{:S(2)}, u32[]{:S(2)}) collective-permute-start(f32[4,81,128]{2,1,0:T(8,128)S(1)} %get-tuple-element.12), channel_id=1, source_target_pairs={{0,6},{2,4},{4,2},{6,0},{1,7},{3,5},{5,3},{7,1},{8,14},{10,12},{12... | collective-permute-start | bytes 497672 | tf_op jit(solution)/shard_map/ppermute | solution.py:25
  105.0 8.3 %collective-permute-start = (f32[4,3,128]{2,1,0:T(4,128)S(1)}, f32[4,3,128]{2,1,0:T(4,128)S(1)}, u32[]{:S(2)}, u32[]{:S(2)}) collective-permute-start(f32[4,3,128]{2,1,0:T(4,128)S(1)} %get-tuple-element.20), channel_id=1, source_target_pairs={{0,28},{4,0},{8,4},{12,8},{16,12},{20,16},{24,20},{28,24},{1,29},{... | collective-permute-start | bytes 18440 | tf_op jit(solution)/shard_map/ppermute | solution.py:30
  106.4 6.9 %collective-permute-start.1 = (f32[4,3,128]{2,1,0:T(4,128)S(1)}, f32[4,3,128]{2,1,0:T(4,128)S(1)}, u32[]{:S(2)}, u32[]{:S(2)}) collective-permute-start(f32[4,3,128]{2,1,0:T(4,128)S(1)} %get-tuple-element.21), channel_id=1, source_target_pairs={{0,4},{4,8},{8,12},{12,16},{16,20},{20,24},{24,28},{28,0},{1,5},{5... | collective-permute-start | bytes 18440 | tf_op jit(solution)/shard_map/ppermute | solution.py:30
  114.0 5.0 %collective-permute-start.13 = (f32[81,128]{1,0:T(8,128)S(1)}, f32[81,128]{1,0:T(8,128)S(1)}, u32[]{:S(2)}, u32[]{:S(2)}) collective-permute-start(f32[81,128]{1,0:T(8,128)S(1)} %get-tuple-element.16), channel_id=1, source_target_pairs={{0,8},{8,0},{16,24},{24,16},{1,9},{9,1},{17,25},{25,17},{2,10},{10... | collective-permute-start | bytes 124424 | tf_op jit(solution)/shard_map/ppermute | solution.py:25
  114.0 5.0 %collective-permute-start.14 = (f32[81,128]{1,0:T(8,128)S(1)}, f32[81,128]{1,0:T(8,128)S(1)}, u32[]{:S(2)}, u32[]{:S(2)}) collective-permute-start(f32[81,128]{1,0:T(8,128)S(1)} %get-tuple-element.15), channel_id=1, source_target_pairs={{0,16},{8,24},{16,0},{24,8},{1,17},{9,25},{17,1},{25,9},{2,18},{10... | collective-permute-start | bytes 124424 | tf_op jit(solution)/shard_map/ppermute | solution.py:25
  115.3 5.8 %collective-permute-start.15 = (f32[81,128]{1,0:T(8,128)S(1)}, f32[81,128]{1,0:T(8,128)S(1)}, u32[]{:S(2)}, u32[]{:S(2)}) collective-permute-start(f32[81,128]{1,0:T(8,128)S(1)} %get-tuple-element.14), channel_id=1, source_target_pairs={{0,24},{8,16},{16,8},{24,0},{1,25},{9,17},{17,9},{25,1},{2,26},{10... | collective-permute-start | bytes 124424 | tf_op jit(solution)/shard_map/ppermute | solution.py:25
  119.0 2.1 %copy-start.3 = (f32[81,128]{1,0:T(8,128)}, f32[81,128]{1,0:T(8,128)S(1)}, u32[]{:S(2)}) copy-start(f32[81,128]{1,0:T(8,128)S(1)} %collective-permute-done.13.refs_1_) | copy-start | bytes 124420
  119.0 2.1 %copy-start.4 = (f32[81,128]{1,0:T(8,128)}, f32[81,128]{1,0:T(8,128)S(1)}, u32[]{:S(2)}) copy-start(f32[81,128]{1,0:T(8,128)S(1)} %collective-permute-done.14.refs_2_) | copy-start | bytes 124420
  121.1 0.6 copy-start.5

commit v5 on v4

v5 whole, which is shorter than its diff:
```python
import functools
import math

import jax
import jax.numpy as jnp
import numpy as np
from jax import lax
from jax.experimental import pallas as pl
from jax.experimental.pallas import tpu as pltpu
from jax.sharding import PartitionSpec as P

G = 256
HALF = G // 2
STENCIL = 27
SIDE = 3
FINE = 4
SAMPLES = 3 * STENCIL
HEIGHT = 88
TILE = 16
ROW = ("z", "x")
PLANE = ("x", "y")
AXES = ("z", "x", "y", "core")

screen_shift = 0.5


def swapped(values, axes, offset):
    count = lax.axis_size(axes)
    return lax.ppermute(values, axes, [(i, i ^ offset) for i in range(count)])


def row_shift(values, by):
    count = lax.axis_size(ROW)
    return lax.ppermute(values, ROW, [(i, (i + by) % count) for i in range(count)])


def near_field(charges, near_tiles, pair_target, pair_count):
    panels = charges.shape[2]
    rounded = charges.astype(jnp.bfloat16)
    slot_total = pair_target.shape[0]
    slot_group = slot_total // 3
    picked = rounded[:, pair_target, :]
    partial_value = jnp.einsum(
        "qabij,aqi->qbj", near_tiles, picked, preferred_element_type=jnp.float32
    )
    live_mask = jnp.arange(slot_total, dtype=jnp.int32) < pair_count[0]
    partial_value = jnp.where(
        live_mask[:, None, None], partial_value, jnp.zeros_like(partial_value)
    )
    leaving = partial_value[slot_group:].reshape(slot_group, 2, 3, panels)
    crossing = jnp.stack([row_shift(leaving[:, 0], -1), row_shift(leaving[:, 1], 1)], axis=1)
    return jnp.concatenate(
        [partial_value[:slot_group], crossing.reshape(2 * slot_group, 3, panels)], axis=0
    )


def half_tables():
    cells = np.arange(HALF)
    parts = []
    for parity in range(2):
        product = cells[:, None] * (2 * cells[None, :] + parity) % G
        angles = product * (2.0 * np.pi / G)
        cosines, sines = np.cos(angles), np.sin(angles)
        table = np.block([[cosines, -sines], [sines, cosines]]).astype(np.float32)
        high = table.astype(jnp.bfloat16)
        low = (table - high.astype(np.float32)).astype(jnp.bfloat16)
        parts.append(np.stack([high, low]))
    return np.stack(parts)


def split(values):
    high = values.astype(jnp.bfloat16)
    low = (values - high.astype(jnp.float32)).astype(jnp.bfloat16)
    return high, low


def dot(left, right):
    return jnp.dot(left, right, preferred_element_type=jnp.float32)


def three_pass(left_high, left_low, right_high, right_low):
    return (
        dot(left_high, right_low) + dot(left_low, right_high) + dot(left_high, right_high)
    )


def spread_kernel(density, weights, corners, out):
    clusters = corners.shape[1]
    panels = density.shape[1] // clusters
    unroll = 8
    lane = lax.broadcasted_iota(jnp.int32, (STENCIL, clusters), 1)

    def some(i, sums):
        for j in range(unroll):
            k = i * unroll + j
            at = pl.ds(pl.multiple_of(k * panels, panels), panels)
            weight = weights[:, at]
            sums = tuple(
                jnp.where(
                    lane == k,
                    jnp.sum(weight * density[a : a + 1, at], axis=1, keepdims=True),
                    sums[a],
                )
                for a in range(3)
            )
        return sums

    blank = jnp.zeros((STENCIL, clusters), jnp.float32)
    sums = lax.fori_loop(0, clusters // unroll, some, (blank, blank, blank))
    for a in range(3):
        out[a * STENCIL : (a + 1) * STENCIL, :] = sums[a]
    out[SAMPLES : SAMPLES + 3, :] = corners[...].astype(jnp.float32)
    out[SAMPLES + 3 :, :] = jnp.zeros((HEIGHT - SAMPLES - 3, clusters), jnp.float32)


def final_kernel(landing, near, weights, *refs):
    *samples, out = refs
    clusters = samples[0].shape[1]
    panels = weights.shape[1] // clusters
    total = sum(sample[...] for sample in samples[1:]) + samples[0][...]
    columns = [total[a * STENCIL : (a + 1) * STENCIL] for a in range(3)]
    for k in range(clusters):
        at = slice(k * panels, (k + 1) * panels)
        weight = weights[:, at]
        for a in range(3):
            out[a : a + 1, at] = jnp.sum(
                columns[a][:, k : k + 1] * weight, axis=0, keepdims=True
            )
    for q in range(near.shape[0]):
        at = pl.ds(pl.multiple_of(landing[q] * panels, panels), panels)
        out[:, at] = out[:, at] + near[q]


def ordered(wide, high, where, sources, stencils):
    row = pl.program_id(0)
    deep = (row // wide) ^ where[2]
    for o in range(wide * high):

        @pl.when((row % wide) ^ where[3] == o // high)
        def _():
            y = (o % high) ^ where[4]
            stencils[2 * y + where[0]] = sources[o][deep]
            stencils[2 * y + 1 - where[0]] = sources[wide * high + o][deep]


def cosine(turns):
    turns = turns & (G - 1)
    turns = jnp.minimum(turns, G - turns)
    flipped = turns > G // 4
    angle = jnp.where(flipped, G // 2 - turns, turns).astype(jnp.float32) * (2.0 * math.pi / G)
    square = angle * angle
    total = jnp.full_like(square, 1.0 / math.factorial(12))
    for order in (10, 8, 6, 4, 2, 0):
        total = total * square + (-1.0) ** (order // 2) / math.factorial(order)
    return jnp.where(flipped, -total, total)


def regrouped(values, span, left):
    if len(values) == 2:
        turned = [pltpu.roll(value, span, axis=1) for value in values]
        return [
            jnp.where(left, values[0], turned[1]),
            jnp.where(left, turned[0], values[1]),
        ]
    return [
        jnp.concatenate([value[:, i * span : (i + 1) * span] for value in values], axis=1)
        for i in range(len(values))
    ]


def scatter_kernel(live, wide, high, where, *refs):
    *sources, out, phases, stencils, total = refs
    sides, parts, slab, lanes = out.shape
    cols, _, clusters = stencils.shape
    span = G // cols
    coarse_cells = slab // FINE
    corner = pl.program_id(0) * slab
    ordered(wide, high, where, sources, stencils)
    bins = lax.broadcasted_iota(jnp.int32, phases.shape[2:], 0)
    waves = bins // 2 + where[1]
    quarter = bins % 2 * (G // 4)
    kept = bins < 2 * live
    bf16 = jnp.bfloat16
    column = lax.broadcasted_iota(jnp.int32, (TILE, clusters), 0)
    ones = jnp.ones((TILE, clusters), bf16)
    zeros = jnp.zeros((TILE, clusters), bf16)
    for c in range(cols):
        first, second, third = (
            stencils[c, SAMPLES + i : SAMPLES + i + 1, :].astype(jnp.int32) for i in range(3)
        )
        for z in range(SIDE):
            phases[c, z] = jnp.where(kept, cosine((third + z) * waves + quarter), 0.0)
        hots, spreads = [], []
        for x in range(SIDE):
            cell = first - corner + x
            fine = (cell & (FINE - 1)) * span + second - c * span
            fine = jnp.broadcast_to(fine, (TILE, clusters))
            coarse = jnp.broadcast_to(cell // FINE, (TILE, clusters)).astype(jnp.int16)
            for y in range(SIDE):
                target = (fine + y).astype(jnp.int16)
                hots.append(
                    jnp.concatenate(
                        [
                            jnp.where((column + j).astype(jnp.int16) == target, ones, zeros)
                            for j in range(0, FINE * span, TILE)
                        ],
                        axis=0,
                    )
                )
                modes = []
                for a in range(3):
                    row = a * STENCIL + x * 9 + y * 3
                    modes.append(
                        sum(
                            stencils[c, row + z : row + z + 1, :] * phases[c, z]
                            for z in range(SIDE)
                        )
                    )
                modes = jnp.concatenate(modes, axis=0)
                low = modes - modes.astype(bf16).astype(jnp.float32)
                tile = jnp.concatenate([modes, low], axis=0).astype(bf16)
                pieces = []
                for h in range(coarse_cells):
                    chosen = coarse == jnp.asarray(h, jnp.int16)
                    for j in range(0, 2 * parts, TILE):
                        pieces.append(jnp.where(chosen, tile[j : j + TILE], zeros))
                spreads.append(jnp.concatenate(pieces, axis=0))
        result = lax.dot_general(
            jnp.concatenate(spreads, axis=1),
            jnp.concatenate(hots, axis=1),
            (((1,), (1,)), ((), ())),
            preferred_element_type=jnp.float32,
        )
        for part in range(total.shape[1]):
            total[c, part] = result[:, part * lanes : (part + 1) * lanes]
    across = lanes // span
    left = lax.broadcasted_iota(jnp.int32, (coarse_cells, lanes), 1) < span
    for part in range(total.shape[1]):
        for v in range(parts):
            for side in range(sides):
                values = [
                    total[c, part, pl.ds(v, coarse_cells, stride=2 * parts), :]
                    + total[c, part, pl.ds(parts + v, coarse_cells, stride=2 * parts), :]
                    for c in range(side * across, (side + 1) * across)
                ]
                for i, row in enumerate(regrouped(values, span, left)):
                    at = pl.ds(part * across + i, coarse_cells, stride=FINE)
                    out[side, v, at, :] = row


def dft_kernel(factor, live, where, field, tx, txt, ty, tyt, out, lines, modes):
    pars = ty.shape[0]
    width = pars * HALF
    odds = [where[5] + p for p in range(pars)]
    signs = [1.0 - 2.0 * odd.astype(jnp.float32) for odd in odds]

    for p in range(pars):
        for a in range(3):
            values = [field[0, a, 0, i] + signs[p] * field[1, a, 0, i] for i in range(2)]
            result = three_pass(*split(jnp.concatenate(values, axis=1)), ty[p, 0], ty[p, 1])
            for part in range(2):
                lines[a, part, :, p * HALF : (p + 1) * HALF] = result[
                    :, part * HALF : (part + 1) * HALF
                ]
    for a in range(3):
        for q in range(2):
            values = []
            for part in range(2):
                top, bottom = lines[a, part, :HALF], lines[a, part, HALF:]
                values.append(top - bottom if q else top + bottom)
            result = three_pass(txt[q, 0], txt[q, 1], *split(jnp.concatenate(values, axis=0)))
            for part in range(2):
                modes[a, part, q * HALF : (q + 1) * HALF] = result[
                    part * HALF : (part + 1) * HALF
                ]

    m = pl.program_id(0)
    bin_third = where[1] + m
    kthird = bin_third.astype(jnp.float32)
    scale = jnp.where(bin_third == 0, factor, 2.0 * factor)
    scale = jnp.where(m < live, scale, 0.0)
    chunk = 32
    lane = lax.broadcasted_iota(jnp.int32, (1, HALF), 1)
    seconds = []
    for odd in odds:
        bin_second = 2 * lane + odd
        ksecond = jnp.where(bin_second < HALF, bin_second, bin_second - G).astype(jnp.float32)
        seconds.append((ksecond, jnp.where(bin_second == HALF, 0.0, scale)))

    def project(i, carry):
        rows = pl.ds(pl.multiple_of(i * chunk, chunk), chunk)
        at = lax.broadcasted_iota(jnp.int32, (chunk, 1), 0) + i * chunk
        bin_first = jnp.where(at < HALF, 2 * at, 2 * at - (G - 1))
        kfirst = jnp.where(bin_first < HALF, bin_first, bin_first - G).astype(jnp.float32)
        kept = jnp.where(bin_first == HALF, 0.0, 1.0)
        kfirst, kept = (jnp.broadcast_to(k, (chunk, HALF)) for k in (kfirst, kept))
        partly = kfirst * kfirst + kthird * kthird
        for p, (ksecond, weight) in enumerate(seconds):
            at = slice(p * HALF, (p + 1) * HALF)
            squared = partly + ksecond * ksecond
            shifted = squared + screen_shift
            floored = jnp.maximum(squared, 1.0)
            both = 1.0 / (shifted * floored)
            inverse = shifted * both
            weighting = floored * both * (kept * weight)
            for part in range(2):
                u, v, w = (modes[a, part, rows, at] for a in range(3))
                inner = (kfirst * u + ksecond * v + kthird * w) * inverse
                lines[0, part, rows, at] = (u - kfirst * inner) * weighting
                lines[1, part, rows, at] = (v - ksecond * inner) * weighting
                lines[2, part, rows, at] = (w - kthird * inner) * weighting
        return carry

    lax.fori_loop(0, G // chunk, project, 0)

    for a in range(3):
        results = []
        for q in range(2):
            values = [lines[a, part, q * HALF : (q + 1) * HALF] for part in range(2)]
            results.append(
                three_pass(tx[q, 0], tx[q, 1], *split(jnp.concatenate(values, axis=0)))
            )
        for part in range(2):
            even, odd = (r[part * HALF : (part + 1) * HALF] for r in results)
            modes[a, part, :HALF] = even + odd
            modes[a, part, HALF:] = even - odd
    for a in range(3):
        near = far = None
        for p in range(pars):
            values = [modes[a, part, :, p * HALF : (p + 1) * HALF] for part in range(2)]
            result = three_pass(*split(jnp.concatenate(values, axis=1)), tyt[p, 0], tyt[p, 1])
            near = result if near is None else near + result
            far = signs[p] * result if far is None else far + signs[p] * result
        for part in range(2):
            out[0, a, 0, part] = near[:, part * HALF : (part + 1) * HALF]
            out[1, a, 0, part] = far[:, part * HALF : (part + 1) * HALF]


def gather_kernel(wide, high, where, *refs):
    *sources, phases, field, mine, other, stencils, lines, found, results = refs
    _, parts, slab, _ = field.shape
    cols, _, clusters = stencils.shape
    ordered(wide, high, where, sources, stencils)
    bins = parts // 3
    span = G // cols
    corner = (pl.program_id(0) * slab).astype(jnp.float32)
    for side in range(2):
        for v in range(parts):
            lines[side, pl.ds(v, slab, stride=parts), :] = field[side, v]
    halves = [split(lines[side]) for side in range(2)]
    rows = lax.broadcasted_iota(jnp.int32, (2 * span, clusters), 0)
    rows = jnp.where(rows < span, rows, rows - span).astype(jnp.float32)
    for c in range(cols):
        first = stencils[c, SAMPLES : SAMPLES + 1, :] - corner
        second = stencils[c, SAMPLES + 1 : SAMPLES + 2, :] - c * span
        hot = jnp.concatenate(
            [jnp.where(rows == second + y, 1.0, 0.0) for y in range(SIDE)], axis=1
        ).astype(jnp.bfloat16)
        side, start = divmod(c * span, HALF)
        pair = [half[:, start : start + span] for half in halves[side]]
        found[c % 2] = dot(jnp.concatenate(pair, axis=1), hot)
        target = (c + where[0]) % 2, (c // 2) ^ where[4]
        tall = jnp.broadcast_to(first, (8, clusters))
        for y in range(SIDE):
            lanes = slice(y * clusters, (y + 1) * clusters)
            sums = [[jnp.zeros((8, clusters), jnp.float32)] * (parts // 8) for _ in range(SIDE)]
            chosen = {}
            for cell in range(slab):
                if cell <= slab - SIDE:
                    chosen[cell] = tall == cell
                for j in range(parts // 8):
                    at = cell * parts + j * 8
                    value = found[c % 2, at : at + 8, lanes]
                    for x in range(SIDE):
                        if cell - x in chosen:
                            sums[x][j] = jnp.where(chosen[cell - x], value, sums[x][j])
            for x in range(SIDE):
                total = jnp.concatenate(sums[x], axis=0)
                for a in range(3):
                    mode = total[a * bins : (a + 1) * bins]
                    for z in range(SIDE):
                        at = a * STENCIL + x * 9 + y * 3 + z
                        results[*target, at : at + 1, :] = jnp.sum(
                            mode * phases[c, z], axis=0, keepdims=True
                        )
        results[*target, SAMPLES:, :] = jnp.zeros((HEIGHT - SAMPLES, clusters), jnp.float32)
    for j in range(high):
        mine[0, j, 0] = results[0, j]
        other[0, j, 0] = results[1, j]


def per_device(
    density,
    interp_weight,
    proj_weight,
    stencil_corner,
    near_tiles,
    pair_target,
    pair_landing,
    pair_count,
):
    clusters = stencil_corner.shape[1]
    panels = density.shape[1] // clusters
    deep, wide, high = (lax.axis_size(axis) for axis in AXES[:3])
    here = [lax.axis_index(axis) for axis in AXES]
    rows_total = deep * wide
    cols_total = high * lax.axis_size("core")
    devices = rows_total * cols_total
    device = lax.axis_index(AXES)
    slab = G // rows_total
    kept_bins = G // 2
    third_parts = min(devices, kept_bins)
    second_parts = devices // third_parts
    pars = 2 // second_parts
    third_live = kept_bins // third_parts
    bins = max(4, third_live)
    parts = 3 * 2 * bins
    width = pars * HALF
    f32, bf16 = jnp.float32, jnp.bfloat16

    charges = density.reshape(3, clusters, panels)
    packed = pl.pallas_call(
        spread_kernel,
        out_shape=jax.ShapeDtypeStruct((HEIGHT, clusters), f32),
        name="spread",
    )(density, interp_weight, stencil_corner)
    line = jnp.stack([packed] + [swapped(packed, "z", o) for o in range(1, deep)])
    sources = [line] + [swapped(line, PLANE, o) for o in range(1, wide * high)]
    sources += [swapped(source, "core", 1) for source in sources]

    factor = 1.0 / math.sqrt(density.shape[1] * devices)
    first_parity = device % second_parts
    where = jnp.stack(
        [here[3], device // second_parts * third_live, here[0], here[1], here[2], first_parity]
    ).astype(jnp.int32)

    tables = half_tables()
    tx = jnp.asarray(tables)
    txt = jnp.asarray(np.ascontiguousarray(np.swapaxes(tables, 2, 3)))
    if pars == 2:
        ty, tyt = tx, txt
    else:
        ty = lax.dynamic_slice_in_dim(tx, first_parity, 1, axis=0)
        tyt = lax.dynamic_slice_in_dim(txt, first_parity, 1, axis=0)

    smem = pl.BlockSpec(memory_space=pltpu.SMEM)
    line_block = pl.BlockSpec((deep, HEIGHT, clusters), lambda r, where: (0, 0, 0))
    phase_row = pl.BlockSpec(
        (cols_total, SIDE, 2 * bins, clusters), lambda r, where: (r, 0, 0, 0)
    )
    slab_block = pl.BlockSpec((2, parts, slab, HALF), lambda r, where: (0, 0, r, 0))
    span = G // cols_total
    field, phases = pl.pallas_call(
        functools.partial(scatter_kernel, third_live, wide, high),
        grid_spec=pltpu.PrefetchScalarGridSpec(
            num_scalar_prefetch=1,
            grid=(rows_total,),
            in_specs=[line_block] * len(sources),
            out_specs=[slab_block, phase_row],
            scratch_shapes=[
                pltpu.VMEM((cols_total, HEIGHT, clusters), f32),
                pltpu.VMEM((cols_total, FINE * span // HALF, slab // FINE * 2 * parts, HALF), f32),
            ],
        ),
        out_shape=[
            jax.ShapeDtypeStruct((2, parts, G, HALF), f32),
            jax.ShapeDtypeStruct((devices, SIDE, 2 * bins, clusters), f32),
        ],
        name="scatter",
    )(where, *sources)

    plane = pl.BlockSpec((2, 3, 1, 2, G, HALF), lambda m: (0, 0, m, 0, 0, 0))
    table = pl.BlockSpec((2, 2, G, G), lambda m: (0, 0, 0, 0))
    table_y = pl.BlockSpec((pars, 2, G, G), lambda m: (0, 0, 0, 0))
    field = pl.pallas_call(
        functools.partial(dft_kernel, factor, third_live),
        grid=(bins,),
        in_specs=[smem, plane, table, table, table_y, table_y],
        out_specs=plane,
        out_shape=jax.ShapeDtypeStruct((2, 3, bins, 2, G, HALF), f32),
        scratch_shapes=[
            pltpu.VMEM((3, 2, G, width), f32),
            pltpu.VMEM((3, 2, G, width), f32),
        ],
        name="spectral",
    )(where, field.reshape(2, 3, bins, 2, G, HALF), tx, txt, ty, tyt)

    sample_block = pl.BlockSpec(
        (1, high, 1, HEIGHT, clusters),
        lambda r, where: ((r % wide) ^ where[3], 0, (r // wide) ^ where[2], 0, 0),
    )
    mine, other = pl.pallas_call(
        functools.partial(gather_kernel, wide, high),
        grid_spec=pltpu.PrefetchScalarGridSpec(
            num_scalar_prefetch=1,
            grid=(rows_total,),
            in_specs=[line_block] * len(sources) + [phase_row, slab_block],
            out_specs=[sample_block] * 2,
            scratch_shapes=[
                pltpu.VMEM((cols_total, HEIGHT, clusters), f32),
                pltpu.VMEM((2, slab * parts, HALF), f32),
                pltpu.VMEM((2, slab * parts, SIDE * clusters), f32),
                pltpu.VMEM((2, high, HEIGHT, clusters), f32),
            ],
        ),
        out_shape=[jax.ShapeDtypeStruct((wide, high, deep, HEIGHT, clusters), f32)] * 2,
        name="gather",
    )(where, *sources, phases, field.reshape(2, parts, G, HALF))
    sampled = (mine + swapped(other, "core", 1)).reshape(wide * high, deep, HEIGHT, clusters)
    line = sampled[0] + sum(swapped(sampled[o], PLANE, o) for o in range(1, wide * high))
    samples = [line[0]] + [swapped(line[o], "z", o) for o in range(1, deep)]
    near = near_field(
        density.reshape(3, clusters, panels), near_tiles, pair_target, pair_count
    )
    vmem = pl.BlockSpec(memory_space=pltpu.VMEM)
    return pl.pallas_call(
        final_kernel,
        in_specs=[smem] + [vmem] * (2 + deep),
        out_shape=jax.ShapeDtypeStruct(density.shape, f32),
        name="final",
    )(pair_landing, near, proj_weight, *samples)


def solution(mesh):
    in_specs = (
        P(None, AXES),
        P(None, AXES),
        P(None, AXES),
        P(None, AXES),
        P(AXES, None, None, None, None),
        P(AXES),
        P(AXES),
        P(AXES),
    )
    rows_total, cols_total = (mesh.shape[axis] for axis in ("row", "col"))
    high = cols_total // 2
    wide = high if rows_total % high == 0 else 1
    split_mesh = jax.sharding.Mesh(
        mesh.devices.reshape(rows_total // wide, wide, high, 2), AXES
    )
    return jax.shard_map(
        per_device, mesh=split_mesh, in_specs=in_specs, out_specs=P(None, AXES), check_vma=False
    )
```

time: 126 us -> 108 us (0.86)
  Pallas kernels: 64.9 us -> 57 us
  local copies, waits for them, and re-layouts: 11.1 us -> 5.17 us
  other arithmetic: 7.59 us -> 5.14 us
  waiting for transfers between devices: 21.2 us -> 19.1 us
    pallas_call x4, Pallas kernels: 60.8 us -> 52.9 us  [the longest x1 17.2 us: per_device(): pl.pallas_call(functools.partial(scatter_kernel, third_live, wide, high),...]
    another operation x3 -> x1, other arithmetic: 3.37 us -> 0.87 us  [per_device(): jnp.stack([packed] + [swapped(packed, 'z', o) for o in range(1, deep)])]
    slice x1 -> x0, local copies, waits for them, and re-layouts: 2.3 us -> none  [per_device(): sampled = sampled[0] + swapped(sampled[1], 'core', 1)]
    ppermute x1 -> x0, local copies, waits for them, and re-layouts: 2.03 us -> none  [swapped(): return lax.ppermute(values, axes, [(i, i ^ offset) for i in range(count)])]
    ppermute x14 -> x17, waiting for transfers between devices: 14.9 us -> 13.1 us  [swapped(): return lax.ppermute(values, axes, [(i, i ^ offset) for i in range(count)])]
    ppermute x14 -> x17, starting transfers between devices: 17.6 us -> 17.7 us  [swapped(): return lax.ppermute(values, axes, [(i, i ^ offset) for i in range(count)])]
  transfers between devices with their start and end apart: 16 -> 19, of which waited for: 7 -> 9; matrix products, arithmetic and copies ran while one was open for 5% -> 5% of each run, Pallas kernels for 0% -> 0%
where the time goes in v5:
time: 108 us
  Pallas kernels  57 us (53%)
  starting transfers between devices  19.7 us (18%)
  waiting for transfers between devices  19.1 us (18%)
  local copies, waits for them, and re-layouts  5.17 us (5%)
  other arithmetic  5.14 us (5%)
    ppermute x17, starting transfers between devices, swapped(): return lax.ppermute(values, axes, [(i, i ^ offset) for i in range(count)])  17.7 us
    pallas_call x1, Pallas kernels, per_device(): pl.pallas_call(functools.partial(scatter_kernel, third_live, wide, high),...  17.2 us
    pallas_call x1, Pallas kernels, per_device(): pl.pallas_call(functools.partial(dft_kernel, factor, third_live), grid=(b...  16.9 us
    pallas_call x1, Pallas kernels, per_device(): pl.pallas_call(functools.partial(gather_kernel, wide, high), grid_spec=pl...  13.6 us
    ppermute x17, waiting for transfers between devices, swapped(): return lax.ppermute(values, axes, [(i, i ^ offset) for i in range(count)])  13.1 us
    ppermute x2, waiting for transfers between devices, row_shift(): lax.ppermute(values, ROW, [(i, (i + by) % count) for i in range(count)])  5.96 us
    pallas_call x1, Pallas kernels, per_device(): pl.pallas_call(spread_kernel, out_shape=jax.ShapeDtypeStruct((HEIGHT, clu...  5.22 us
    pallas_call x1, Pallas kernels, per_device(): pl.pallas_call(final_kernel, in_specs=[smem] + [vmem] * (2 + deep), out_s...  4.11 us
  transfers between devices with their start and end apart: 19, of which 9 were waited for; matrix products, arithmetic and copies ran while one was open for 5% of the time, Pallas kernels for 0%

profile of v5, /device:TPU:0, one launch (start us, length us, event | category | flops | bytes accessed | tf_op | source)
XLA Modules:
  0.0 107.5 jit_solution(67224352997399603)
XLA Ops:
  0.0 0.0 copy-start
  0.0 5.2 %spread.1 = f32[88,128]{1,0:T(8,128)} custom-call(f32[3,16384]{1,0:T(4,128)} %density.1, f32[27,16384]{1,0:T(8,128)} %weights.2, s32[3,128]{1,0:T(4,128)} %corners.1), custom_call_target="tpu_custom_call" | custom-call | tf_op jit(solution)/shard_map/spread/pallas_call | solution.py:422
  5.2 3.1 %collective-permute-start.2 = (f32[88,128]{1,0:T(8,128)}, f32[88,128]{1,0:T(8,128)}, u32[]{:S(2)}, u32[]{:S(2)}) collective-permute-start(f32[88,128]{1,0:T(8,128)} %spread.1), channel_id=1, source_target_pairs={{0,8},{8,0},{16,24},{24,16},{1,9},{9,1},{17,25},{25,17},{2,10},{10... | collective-permute-start | bytes 135176 | tf_op jit(solution)/shard_map/ppermute | solution.py:29
  8.3 2.6 %collective-permute-start.3 = (f32[88,128]{1,0:T(8,128)}, f32[88,128]{1,0:T(8,128)}, u32[]{:S(2)}, u32[]{:S(2)}) collective-permute-start(f32[88,128]{1,0:T(8,128)} %spread.1), channel_id=1, source_target_pairs={{0,16},{8,24},{16,0},{24,8},{1,17},{9,25},{17,1},{25,9},{2,18},{10... | collective-permute-start | bytes 135176 | tf_op jit(solution)/shard_map/ppermute | solution.py:29
  10.9 0.0 collective-permute-start.4
  11.5 0.7 stack.51.where
  12.2 0.0 collective-permute-done.2
  12.2 2.2 %collective-permute-done.3 = f32[88,128]{1,0:T(8,128)} collective-permute-done((f32[88,128]{1,0:T(8,128)}, f32[88,128]{1,0:T(8,128)}, u32[]{:S(2)}, u32[]{:S(2)}) %collective-permute-start.3) | collective-permute-done | bytes 45088 | tf_op jit(solution)/shard_map/ppermute | solution.py:29
  14.4 2.6 %collective-permute-done.4 = f32[88,128]{1,0:T(8,128)} collective-permute-done((f32[88,128]{1,0:T(8,128)}, f32[88,128]{1,0:T(8,128)}, u32[]{:S(2)}, u32[]{:S(2)}) %collective-permute-start.4) | collective-permute-done | bytes 45088 | tf_op jit(solution)/shard_map/ppermute | solution.py:29
  17.0 0.9 pad_maximum_fusion.refs_0_
  17.9 0.0 copy-start.1
  17.9 1.6 %collective-permute-start.6 = (f32[4,88,128]{2,1,0:T(8,128)S(1)}, f32[4,88,128]{2,1,0:T(8,128)S(1)}, u32[]{:S(2)}, u32[]{:S(2)}) collective-permute-start(f32[4,88,128]{2,1,0:T(8,128)S(1)} %pad_maximum_fusion.refs_0_), channel_id=1, source_target_pairs={{0,4},{2,6},{4,0},{6,2},{1,5},{3,7},{5,1},{7,3},{8,12},{10,14},{12... | collective-permute-start | bytes 540680 | tf_op jit(solution)/shard_map/ppermute | solution.py:29
  19.5 1.5 %collective-permute-start.7 = (f32[4,88,128]{2,1,0:T(8,128)S(1)}, f32[4,88,128]{2,1,0:T(8,128)S(1)}, u32[]{:S(2)}, u32[]{:S(2)}) collective-permute-start(f32[4,88,128]{2,1,0:T(8,128)S(1)} %pad_maximum_fusion.refs_0_), channel_id=1, source_target_pairs={{0,6},{2,4},{4,2},{6,0},{1,7},{3,5},{5,3},{7,1},{8,14},{10,12},{12... | collective-permute-start | bytes 540680 | tf_op jit(solution)/shard_map/ppermute | solution.py:29
  21.0 0.5 collective-permute-start.5
  21.5 1.6 %convert_bitcast_fusion = bf16[3,128,128]{2,0,1:T(4,128)(2,1)} fusion(f32[3,16384]{1,0:T(4,128)} %density.1), kind=kLoop, calls=%fused_computation.9 | loop fusion | flops 49152 | bytes 294912 | tf_op jit(solution)/shard_map/convert_element_type | solution.py:39
  23.1 0.0 copy-done.1
  23.1 0.0 collective-permute-start.8
  23.1 1.7 %collective-permute-done.6.refs_2_ = f32[4,88,128]{2,1,0:T(8,128)S(1)} collective-permute-done((f32[4,88,128]{2,1,0:T(8,128)S(1)}, f32[4,88,128]{2,1,0:T(8,128)S(1)}, u32[]{:S(2)}, u32[]{:S(2)}) %collective-permute-start.6) | collective-permute-done | bytes 180256 | tf_op jit(solution)/shard_map/ppermute | solution.py:29
  24.8 0.0 collective-permute-start.10
  24.8 2.7 %collective-permute-done.7.refs_3_ = f32[4,88,128]{2,1,0:T(8,128)S(1)} collective-permute-done((f32[4,88,128]{2,1,0:T(8,128)S(1)}, f32[4,88,128]{2,1,0:T(8,128)S(1)}, u32[]{:S(2)}, u32[]{:S(2)}) %collective-permute-start.7) | collective-permute-done | bytes 180256 | tf_op jit(solution)/shard_map/ppermute | solution.py:29
  27.6 0.0 collective-permute-start.11
  27.6 1.4 %collective-permute-done.5.refs_1_ = f32[4,88,128]{2,1,0:T(8,128)S(1)} collective-permute-done((f32[4,88,128]{2,1,0:T(8,128)S(1)}, f32[4,88,128]{2,1,0:T(8,128)S(1)}, u32[]{:S(2)}, u32[]{:S(2)}) %collective-permute-start.5) | collective-permute-done | bytes 180256 | tf_op jit(solution)/shard_map/ppermute | solution.py:29
  28.9 0.0 collective-permute-start.9
  28.9 0.7 compare_select_fusion
  29.6 0.0 collective-permute-done.8.refs_4_
  29.6 0.0 copy-done.3
  29.6 0.0 collective-permute-done.10.refs_6_
  29.6 0.0 copy-done.4
  29.7 0.0 collective-permute-done.11.refs_7_
  29.7 0.6 copy-done.6
  30.3 0.1 copy-done.7
  30.4 0.7 copy-done.8
  31.0 0.0 collective-permute-done.9.refs_5_
  31.0 17.2 %scatter.1 = (f32[2,24,256,128]{3,2,1,0:T(8,128)}, f32[32,3,8,128]{3,2,1,0:T(8,128)}) custom-call(s32[6]{0:T(128)} %stack.51.where, f32[4,88,128]{2,1,0:T(8,128)} %copy-done.1, f32[4,88,128]{2,1,0:T(8,128)} %copy-done.5, f32[4,88,128]{2,1,0:T(8,128)} %copy-done.3, f32[4,88,128]{2,1,0:T(8,128)} %copy-done.4, f32[4,88,128]{2,1,0:T(8,128)} %copy-done.6, ...), custom_call_target="tpu_custom_call" | custom-call | tf_op jit(solution)/shard_map/scatter/pallas_call | solution.py:453
  48.2 16.9 %spectral.1 = f32[2,3,4,2,256,128]{5,4,3,2,1,0:T(8,128)} custom-call(s32[6]{0:T(128)} %stack.51.where, f32[2,3,4,2,256,128]{5,4,3,2,1,0:T(8,128)} %bitcast.52, bf16[2,2,256,256]{3,2,1,0:T(8,128)(2,1)} %constant.52.clone.tx.ty, bf16[2,2,256,256]{3,2,1,0:T(8,128)(2,1)} %constant.53.clone.txt.tyt, bf16[2,2,256,256]{3,2,1,0:T(8,128)(2,1)} %constant.52.clone.tx.ty, ...), custom_call_target="tpu_custom_call" | custom-call | tf_op jit(solution)/shard_map/spectral/pallas_call | solution.py:475
  65.1 13.6 %gather.7 = (f32[2,2,4,88,128]{4,3,2,1,0:T(8,128)}, f32[2,2,4,88,128]{4,3,2,1,0:T(8,128)}) custom-call(s32[6]{0:T(128)} %stack.51.where, f32[4,88,128]{2,1,0:T(8,128)} %copy-done.1, f32[4,88,128]{2,1,0:T(8,128)} %copy-done.5, f32[4,88,128]{2,1,0:T(8,128)} %copy-done.3, f32[4,88,128]{2,1,0:T(8,128)} %copy-done.4, f32[4,88,128]{2,1,0:T(8,128)} %copy-done.6, ...), custom_call_target="tpu_custom_call" | custom-call | tf_op jit(solution)/shard_map/gather/pallas_call | solution.py:492
  78.8 0.5 collective-permute-start.12
  79.3 1.5 %gather_fusion = bf16[12,3,128]{2,1,0:T(4,128)(2,1)S(1)} fusion(bf16[3,128,128]{2,0,1:T(4,128)(2,1)} %convert_bitcast_fusion, s32[1024]{0:T(1024)S(1)} %pad_clamp_fusion), kind=kCustom, calls=%fused_computation | custom fusion | bytes 18480 | tf_op jit(solution)/shard_map/gather | solution.py:42
  80.8 0.6 fusion
  81.4 0.1 bitcast_select_fusion
  81.5 0.0 collective-permute-done.12
  81.5 0.3 copy-done.2
  81.9 1.2 %add.31 = f32[2,2,4,88,128]{4,3,2,1,0:T(8,128)S(1)} add(f32[2,2,4,88,128]{4,3,2,1,0:T(8,128)S(1)} %copy-done.2, f32[2,2,4,88,128]{4,3,2,1,0:T(8,128)} %collective-permute-done.12) | non-fusion elementwise | flops 180224 | bytes 2162688 | tf_op jit(solution)/shard_map/add | solution.py:509
  83.1 0.6 collective-permute-start.13
  83.7 1.5 %collective-permute-start.14 = (f32[4,88,128]{2,1,0:T(8,128)S(1)}, f32[4,88,128]{2,1,0:T(8,128)S(1)}, u32[]{:S(2)}, u32[]{:S(2)}) collective-permute-start(f32[4,88,128]{2,1,0:T(8,128)S(1)} %get-tuple-element.13), channel_id=1, source_target_pairs={{0,4},{2,6},{4,0},{6,2},{1,5},{3,7},{5,1},{7,3},{8,12},{10,14},{12... | collective-permute-start | bytes 540680 | tf_op jit(solution)/shard_map/ppermute | solution.py:29
  85.2 1.4 %collective-permute-start.15 = (f32[4,88,128]{2,1,0:T(8,128)S(1)}, f32[4,88,128]{2,1,0:T(8,128)S(1)}, u32[]{:S(2)}, u32[]{:S(2)}) collective-permute-start(f32[4,88,128]{2,1,0:T(8,128)S(1)} %get-tuple-element.14), channel_id=1, source_target_pairs={{0,6},{2,4},{4,2},{6,0},{1,7},{3,5},{5,3},{7,1},{8,14},{10,12},{12... | collective-permute-start | bytes 540680 | tf_op jit(solution)/shard_map/ppermute | solution.py:29
  86.7 1.6 %collective-permute-start = (f32[4,3,128]{2,1,0:T(4,128)S(1)}, f32[4,3,128]{2,1,0:T(4,128)S(1)}, u32[]{:S(2)}, u32[]{:S(2)}) collective-permute-start(f32[4,3,128]{2,1,0:T(4,128)S(1)} %get-tuple-element.20), channel_id=1, source_target_pairs={{0,28},{4,0},{8,4},{12,8},{16,12},{20,16},{24,20},{28,24},{1,29},{... | collective-permute-start | bytes 18440 | tf_op jit(solution)/shard_map/ppermute | solution.py:34
  88.3 0.4 collective-permute-start.1
  88.7 5.4 %collective-permute-done = f32[4,3,128]{2,1,0:T(4,128)S(1)} collective-permute-done((f32[4,3,128]{2,1,0:T(4,128)S(1)}, f32[4,3,128]{2,1,0:T(4,128)S(1)}, u32[]{:S(2)}, u32[]{:S(2)}) %collective-permute-start) | collective-permute-done | bytes 6176 | tf_op jit(solution)/shard_map/ppermute | solution.py:34
  94.1 0.6 collective-permute-done.1
  94.7 0.0 collective-permute-done.13
  94.7 0.0 collective-permute-done.14
  94.7 0.3 collective-permute-done.15
  95.0 0.1 fusion.2
  95.0 0.6 slice_bitcast_fusion.4
  95.6 0.0 collective-permute-start.16
  95.7 1.3 %collective-permute-start.17 = (f32[88,128]{1,0:T(8,128)S(1)}, f32[88,128]{1,0:T(8,128)S(1)}, u32[]{:S(2)}, u32[]{:S(2)}) collective-permute-start(f32[88,128]{1,0:T(8,128)S(1)} %get-tuple-element.17), channel_id=1, source_target_pairs={{0,16},{8,24},{16,0},{24,8},{1,17},{9,25},{17,1},{25,9},{2,18},{10... | collective-permute-start | bytes 135176 | tf_op jit(solution)/shard_map/ppermute | solution.py:29
  96.9 3.1 %collective-permute-start.18 = (f32[88,128]{1,0:T(8,128)S(1)}, f32[88,128]{1,0:T(8,128)S(1)}, u32[]{:S(2)}, u32[]{:S(2)}) collective-permute-start(f32[88,128]{1,0:T(8,128)S(1)} %get-tuple-element.16), channel_id=1, source_target_pairs={{0,24},{8,16},{16,8},{24,0},{1,25},{9,17},{17,9},{25,1},{2,26},{10... | collective-permute-start | bytes 135176 | tf_op jit(solution)/shard_map/ppermute | solution.py:29
  100.0 0.6 pad_maximum_fusion.1.near
  100.6 0.0 collective-permute-done.16.refs_1_
  100.7 0.0 collective-permute-done.17.refs_2_
  100.7 2.1 %collective-permute-done.18.refs_3_ = f32[88,128]{1,0:T(8,128)S(1)} collective-permute-done((f32[88,128]{1,0:T(8,128)S(1)}, f32[88,128]{1,0:T(8,128)S(1)}, u32[]{:S(2)}, u32[]{:S(2)}) %collective-permute-start.18) | collective-permute-done | bytes 45088 | tf_op jit(solution)/shard_map/ppermute | solution.py:29
  102.8 0.6 copy-done.11
  103.4 4.1 %final.1 = f32[3,16384]{1,0:T(4,128)} custom-call(s32[12]{0:T(128)} %landing.1, f32[12,3,128]{2,1,0:T(4,128)} %pad_maximum_fusion.1.near, f32[27,16384]{1,0:T(8,128)} %weights.3, f32[88,128]{1,0:T(8,128)} %get-tuple-element.19.refs_0_, f32[88,128]{1,0:T(8,128)} %copy-done.9, f32[88,128]{1,0:T(8,128)} %copy-done.10, f32[88,128]{1,0:T(8,128)} %copy-done.11), custom_call_target="tpu_custom_call" | custom-call | tf_op jit(solution)/shard_map/final/pallas_call | solution.py:516
  (21 shorter events, 0.1 us)
Async XLA Ops:
  0.0 80.8 %copy-start = (bf16[12,3,3,128,128]{4,3,2,1,0:T(8,128)(2,1)S(1)}, bf16[12,3,3,128,128]{4,3,2,1,0:T(8,128)(2,1)}, u32[]{:S(2)}) copy-start(bf16[12,3,3,128,128]{4,3,2,1,0:T(8,128)(2,1)} %param.14) | copy-start | bytes 10616836
  5.2 7.0 %collective-permute-start.2 = (f32[88,128]{1,0:T(8,128)}, f32[88,128]{1,0:T(8,128)}, u32[]{:S(2)}, u32[]{:S(2)}) collective-permute-start(f32[88,128]{1,0:T(8,128)} %spread.1), channel_id=1, source_target_pairs={{0,8},{8,0},{16,24},{24,16},{1,9},{9,1},{17,25},{25,17},{2,10},{10... | collective-permute-start | bytes 135176 | tf_op jit(solution)/shard_map/ppermute | solution.py:29
  8.3 6.1 %collective-permute-start.3 = (f32[88,128]{1,0:T(8,128)}, f32[88,128]{1,0:T(8,128)}, u32[]{:S(2)}, u32[]{:S(2)}) collective-permute-start(f32[88,128]{1,0:T(8,128)} %spread.1), channel_id=1, source_target_pairs={{0,16},{8,24},{16,0},{24,8},{1,17},{9,25},{17,1},{25,9},{2,18},{10... | collective-permute-start | bytes 135176 | tf_op jit(solution)/shard_map/ppermute | solution.py:29
  10.9 6.2 %collective-permute-start.4 = (f32[88,128]{1,0:T(8,128)}, f32[88,128]{1,0:T(8,128)}, u32[]{:S(2)}, u32[]{:S(2)}) collective-permute-start(f32[88,128]{1,0:T(8,128)} %spread.1), channel_id=1, source_target_pairs={{0,24},{8,16},{16,8},{24,0},{1,25},{9,17},{17,9},{25,1},{2,26},{10... | collective-permute-start | bytes 135176 | tf_op jit(solution)/shard_map/ppermute | solution.py:29
  17.9 5.2 %copy-start.1 = (f32[4,88,128]{2,1,0:T(8,128)}, f32[4,88,128]{2,1,0:T(8,128)S(1)}, u32[]{:S(2)}) copy-start(f32[4,88,128]{2,1,0:T(8,128)S(1)} %pad_maximum_fusion.refs_0_) | copy-start | bytes 540676
  17.9 6.9 %collective-permute-start.6 = (f32[4,88,128]{2,1,0:T(8,128)S(1)}, f32[4,88,128]{2,1,0:T(8,128)S(1)}, u32[]{:S(2)}, u32[]{:S(2)}) collective-permute-start(f32[4,88,128]{2,1,0:T(8,128)S(1)} %pad_maximum_fusion.refs_0_), channel_id=1, source_target_pairs={{0,4},{2,6},{4,0},{6,2},{1,5},{3,7},{5,1},{7,3},{8,12},{10,14},{12... | collective-permute-start | bytes 540680 | tf_op jit(solution)/shard_map/ppermute | solution.py:29
  19.5 8.1 %collective-permute-start.7 = (f32[4,88,128]{2,1,0:T(8,128)S(1)}, f32[4,88,128]{2,1,0:T(8,128)S(1)}, u32[]{:S(2)}, u32[]{:S(2)}) collective-permute-start(f32[4,88,128]{2,1,0:T(8,128)S(1)} %pad_maximum_fusion.refs_0_), channel_id=1, source_target_pairs={{0,6},{2,4},{4,2},{6,0},{1,7},{3,5},{5,3},{7,1},{8,14},{10,12},{12... | collective-permute-start | bytes 540680 | tf_op jit(solution)/shard_map/ppermute | solution.py:29
  21.0 8.0 %collective-permute-start.5 = (f32[4,88,128]{2,1,0:T(8,128)S(1)}, f32[4,88,128]{2,1,0:T(8,128)S(1)}, u32[]{:S(2)}, u32[]{:S(2)}) collective-permute-start(f32[4,88,128]{2,1,0:T(8,128)S(1)} %pad_maximum_fusion.refs_0_), channel_id=1, source_target_pairs={{0,2},{2,0},{4,6},{6,4},{1,3},{3,1},{5,7},{7,5},{8,10},{10,8},{12,... | collective-permute-start | bytes 540680 | tf_op jit(solution)/shard_map/ppermute | solution.py:29
  23.1 6.5 %collective-permute-start.8 = (f32[4,88,128]{2,1,0:T(8,128)S(1)}, f32[4,88,128]{2,1,0:T(8,128)S(1)}, u32[]{:S(2)}, u32[]{:S(2)}) collective-permute-start(f32[4,88,128]{2,1,0:T(8,128)S(1)} %pad_maximum_fusion.refs_0_), channel_id=1, source_target_pairs={{0,1},{1,0},{2,3},{3,2},{4,5},{5,4},{6,7},{7,6},{8,9},{9,8},{10,11... | collective-permute-start | bytes 540680 | tf_op jit(solution)/shard_map/ppermute | solution.py:29
  24.8 4.8 %copy-start.3 = (f32[4,88,128]{2,1,0:T(8,128)}, f32[4,88,128]{2,1,0:T(8,128)S(1)}, u32[]{:S(2)}) copy-start(f32[4,88,128]{2,1,0:T(8,128)S(1)} %collective-permute-done.6.refs_2_) | copy-start | bytes 540676
  24.8 4.8 %collective-permute-start.10 = (f32[4,88,128]{2,1,0:T(8,128)S(1)}, f32[4,88,128]{2,1,0:T(8,128)S(1)}, u32[]{:S(2)}, u32[]{:S(2)}) collective-permute-start(f32[4,88,128]{2,1,0:T(8,128)S(1)} %collective-permute-done.6.refs_2_), channel_id=1, source_target_pairs={{0,1},{1,0},{2,3},{3,2},{4,5},{5,4},{6,7},{7,6},{8,9},{9,8},{10,11... | collective-permute-start | bytes 540680 | tf_op jit(solution)/shard_map/ppermute | solution.py:29
  27.6 2.1 %copy-start.4 = (f32[4,88,128]{2,1,0:T(8,128)}, f32[4,88,128]{2,1,0:T(8,128)S(1)}, u32[]{:S(2)}) copy-start(f32[4,88,128]{2,1,0:T(8,128)S(1)} %collective-permute-done.7.refs_3_) | copy-start | bytes 540676
  27.6 2.1 %collective-permute-start.11 = (f32[4,88,128]{2,1,0:T(8,128)S(1)}, f32[4,88,128]{2,1,0:T(8,128)S(1)}, u32[]{:S(2)}, u32[]{:S(2)}) collective-permute-start(f32[4,88,128]{2,1,0:T(8,128)S(1)} %collective-permute-done.7.refs_3_), channel_id=1, source_target_pairs={{0,1},{1,0},{2,3},{3,2},{4,5},{5,4},{6,7},{7,6},{8,9},{9,8},{10,11... | collective-permute-start | bytes 540680 | tf_op jit(solution)/shard_map/ppermute | solution.py:29
  28.9 0.7 copy-start.5
  28.9 2.1 %collective-permute-start.9 = (f32[4,88,128]{2,1,0:T(8,128)S(1)}, f32[4,88,128]{2,1,0:T(8,128)}, u32[]{:S(2)}, u32[]{:S(2)}) collective-permute-start(f32[4,88,128]{2,1,0:T(8,128)S(1)} %collective-permute-done.5.refs_1_), channel_id=1, source_target_pairs={{0,1},{1,0},{2,3},{3,2},{4,5},{5,4},{6,7},{7,6},{8,9},{9,8},{10,11... | collective-permute-start | bytes 540680 | tf_op jit(solution)/shard_map/ppermute | solution.py:29
  29.6 0.7 copy-start.6
  29.6 0.7 copy-start.7
  30.4 0.7 copy-start.8
  78.8 2.8 %collective-permute-start.12 = (f32[2,2,4,88,128]{4,3,2,1,0:T(8,128)}, f32[2,2,4,88,128]{4,3,2,1,0:T(8,128)}, u32[]{:S(2)}, u32[]{:S(2)}) collective-permute-start(f32[2,2,4,88,128]{4,3,2,1,0:T(8,128)} %get-tuple-element.12), channel_id=1, source_target_pairs={{0,1},{1,0},{2,3},{3,2},{4,5},{5,4},{6,7},{7,6},{8,9},{9,8},{10,11... | collective-permute-start | bytes 2162696 | tf_op jit(solution)/shard_map/ppermute | solution.py:29
  80.7 1.1 %copy-start.2 = (f32[2,2,4,88,128]{4,3,2,1,0:T(8,128)S(1)}, f32[2,2,4,88,128]{4,3,2,1,0:T(8,128)}, u32[]{:S(2)}) copy-start(f32[2,2,4,88,128]{4,3,2,1,0:T(8,128)} %get-tuple-element.11) | copy-start | bytes 2162692
  83.1 11.6 %collective-permute-start.13 = (f32[4,88,128]{2,1,0:T(8,128)S(1)}, f32[4,88,128]{2,1,0:T(8,128)S(1)}, u32[]{:S(2)}, u32[]{:S(2)}) collective-permute-start(f32[4,88,128]{2,1,0:T(8,128)S(1)} %get-tuple-element.15), channel_id=1, source_target_pairs={{0,2},{2,0},{4,6},{6,4},{1,3},{3,1},{5,7},{7,5},{8,10},{10,8},{12,... | collective-permute-start | bytes 540680 | tf_op jit(solution)/shard_map/ppermute | solution.py:29
  83.7 10.9 %collective-permute-start.14 = (f32[4,88,128]{2,1,0:T(8,128)S(1)}, f32[4,88,128]{2,1,0:T(8,128)S(1)}, u32[]{:S(2)}, u32[]{:S(2)}) collective-permute-start(f32[4,88,128]{2,1,0:T(8,128)S(1)} %get-tuple-element.13), channel_id=1, source_target_pairs={{0,4},{2,6},{4,0},{6,2},{1,5},{3,7},{5,1},{7,3},{8,12},{10,14},{12... | collective-permute-start | bytes 540680 | tf_op jit(solution)/shard_map/ppermute | solution.py:29
  85.2 9.7 %collective-permute-start.15 = (f32[4,88,128]{2,1,0:T(8,128)S(1)}, f32[4,88,128]{2,1,0:T(8,128)S(1)}, u32[]{:S(2)}, u32[]{:S(2)}) collective-permute-start(f32[4,88,128]{2,1,0:T(8,128)S(1)} %get-tuple-element.14), channel_id=1, source_target_pairs={{0,6},{2,4},{4,2},{6,0},{1,7},{3,5},{5,3},{7,1},{8,14},{10,12},{12... | collective-permute-start | bytes 540680 | tf_op jit(solution)/shard_map/ppermute | solution.py:29
  86.7 7.4 %collective-permute-start = (f32[4,3,128]{2,1,0:T(4,128)S(1)}, f32[4,3,128]{2,1,0:T(4,128)S(1)}, u32[]{:S(2)}, u32[]{:S(2)}) collective-permute-start(f32[4,3,128]{2,1,0:T(4,128)S(1)} %get-tuple-element.20), channel_id=1, source_target_pairs={{0,28},{4,0},{8,4},{12,8},{16,12},{20,16},{24,20},{28,24},{1,29},{... | collective-permute-start | bytes 18440 | tf_op jit(solution)/shard_map/ppermute | solution.py:34
  88.3 6.3 %collective-permute-start.1 = (f32[4,3,128]{2,1,0:T(4,128)S(1)}, f32[4,3,128]{2,1,0:T(4,128)S(1)}, u32[]{:S(2)}, u32[]{:S(2)}) collective-permute-start(f32[4,3,128]{2,1,0:T(4,128)S(1)} %get-tuple-element.21), channel_id=1, source_target_pairs={{0,4},{4,8},{8,12},{12,16},{16,20},{20,24},{24,28},{28,0},{1,5},{5... | collective-permute-start | bytes 18440 | tf_op jit(solution)/shard_map/ppermute | solution.py:34
  95.6 5.0 %collective-permute-start.16 = (f32[88,128]{1,0:T(8,128)S(1)}, f32[88,128]{1,0:T(8,128)S(1)}, u32[]{:S(2)}, u32[]{:S(2)}) collective-permute-start(f32[88,128]{1,0:T(8,128)S(1)} %get-tuple-element.18), channel_id=1, source_target_pairs={{0,8},{8,0},{16,24},{24,16},{1,9},{9,1},{17,25},{25,17},{2,10},{10... | collective-permute-start | bytes 135176 | tf_op jit(solution)/shard_map/ppermute | solution.py:29
  95.7 5.0 %collective-permute-start.17 = (f32[88,128]{1,0:T(8,128)S(1)}, f32[88,128]{1,0:T(8,128)S(1)}, u32[]{:S(2)}, u32[]{:S(2)}) collective-permute-start(f32[88,128]{1,0:T(8,128)S(1)} %get-tuple-element.17), channel_id=1, source_target_pairs={{0,16},{8,24},{16,0},{24,8},{1,17},{9,25},{17,1},{25,9},{2,18},{10... | collective-permute-start | bytes 135176 | tf_op jit(solution)/shard_map/ppermute | solution.py:29
  96.9 5.8 %collective-permute-start.18 = (f32[88,128]{1,0:T(8,128)S(1)}, f32[88,128]{1,0:T(8,128)S(1)}, u32[]{:S(2)}, u32[]{:S(2)}) collective-permute-start(f32[88,128]{1,0:T(8,128)S(1)} %get-tuple-element.16), channel_id=1, source_target_pairs={{0,24},{8,16},{16,8},{24,0},{1,25},{9,17},{17,9},{25,1},{2,26},{10... | collective-permute-start | bytes 135176 | tf_op jit(solution)/shard_map/ppermute | solution.py:29
  100.7 2.1 %copy-start.9 = (f32[88,128]{1,0:T(8,128)}, f32[88,128]{1,0:T(8,128)S(1)}, u32[]{:S(2)}) copy-start(f32[88,128]{1,0:T(8,128)S(1)} %collective-permute-done.16.refs_1_) | copy-start | bytes 135172
  100.7 2.1 %copy-start.10 = (f32[88,128]{1,0:T(8,128)}, f32[88,128]{1,0:T(8,128)S(1)}, u32[]{:S(2)}) copy-start(f32[88,128]{1,0:T(8,128)S(1)} %collective-permute-done.17.refs_2_) | copy-start | bytes 135172
  102.8 0.6 copy-start.11

commit v6 on v5

--- a/solution.py
+++ b/solution.py
@@ -27,6 +27,10 @@
 def swapped(values, axes, offset):
     count = lax.axis_size(axes)
     return lax.ppermute(values, axes, [(i, i ^ offset) for i in range(count)])
+
+
+def in_vmem(values):
+    return pltpu.with_memory_space_constraint(values, pltpu.VMEM)
 
 
 def row_shift(values, by):
@@ -170,9 +174,10 @@
 
 def scatter_kernel(live, wide, high, where, *refs):
     *sources, out, phases, stencils, total = refs
-    sides, parts, slab, lanes = out.shape
+    sides, parts, _, lanes = out.shape
     cols, _, clusters = stencils.shape
     span = G // cols
+    slab = total.shape[2] // (2 * parts) * FINE
     coarse_cells = slab // FINE
     corner = pl.program_id(0) * slab
     ordered(wide, high, where, sources, stencils)
@@ -190,6 +195,7 @@
         )
         for z in range(SIDE):
             phases[c, z] = jnp.where(kept, cosine((third + z) * waves + quarter), 0.0)
+        phases[c, SIDE, :2] = stencils[c, SAMPLES : SAMPLES + 2, :]
         hots, spreads = [], []
         for x in range(SIDE):
             cell = first - corner + x
@@ -244,19 +250,22 @@
                     for c in range(side * across, (side + 1) * across)
                 ]
                 for i, row in enumerate(regrouped(values, span, left)):
-                    at = pl.ds(part * across + i, coarse_cells, stride=FINE)
+                    at = pl.ds(corner + part * across + i, coarse_cells, stride=FINE)
                     out[side, v, at, :] = row
 
 
-def dft_kernel(factor, live, where, field, tx, txt, ty, tyt, out, lines, modes):
-    pars = ty.shape[0]
+def dft_kernel(factor, live, pars, where, field, *refs):
+    *tables, out, lines, modes = refs
+    tx, txt = tables[:2]
+    ty, tyt = tables[-2:]
+    m = pl.program_id(0)
     width = pars * HALF
     odds = [where[5] + p for p in range(pars)]
     signs = [1.0 - 2.0 * odd.astype(jnp.float32) for odd in odds]
 
     for p in range(pars):
         for a in range(3):
-            values = [field[0, a, 0, i] + signs[p] * field[1, a, 0, i] for i in range(2)]
+            values = [field[0, a, m, i] + signs[p] * field[1, a, m, i] for i in range(2)]
             result = three_pass(*split(jnp.concatenate(values, axis=1)), ty[p, 0], ty[p, 1])
             for part in range(2):
                 lines[a, part, :, p * HALF : (p + 1) * HALF] = result[
@@ -274,7 +283,6 @@
                     part * HALF : (part + 1) * HALF
                 ]
 
-    m = pl.program_id(0)
     bin_third = where[1] + m
     kthird = bin_third.astype(jnp.float32)
     scale = jnp.where(bin_third == 0, factor, 2.0 * factor)
@@ -332,27 +340,28 @@
             near = result if near is None else near + result
             far = signs[p] * result if far is None else far + signs[p] * result
         for part in range(2):
-            out[0, a, 0, part] = near[:, part * HALF : (part + 1) * HALF]
-            out[1, a, 0, part] = far[:, part * HALF : (part + 1) * HALF]
-
-
-def gather_kernel(wide, high, where, *refs):
-    *sources, phases, field, mine, other, stencils, lines, found, results = refs
-    _, parts, slab, _ = field.shape
-    cols, _, clusters = stencils.shape
-    ordered(wide, high, where, sources, stencils)
+            out[0, a, m, part] = near[:, part * HALF : (part + 1) * HALF]
+            out[1, a, m, part] = far[:, part * HALF : (part + 1) * HALF]
+
+
+def gather_kernel(where, phases, field, mine, other, lines, found, results):
+    parts = field.shape[1]
+    cols, _, _, clusters = phases.shape
+    high = mine.shape[1]
+    slab = lines.shape[1] // parts
+    start_row = pl.multiple_of(pl.program_id(0) * slab, slab)
     bins = parts // 3
     span = G // cols
     corner = (pl.program_id(0) * slab).astype(jnp.float32)
     for side in range(2):
         for v in range(parts):
-            lines[side, pl.ds(v, slab, stride=parts), :] = field[side, v]
+            lines[side, pl.ds(v, slab, stride=parts), :] = field[side, v, pl.ds(start_row, slab), :]
     halves = [split(lines[side]) for side in range(2)]
     rows = lax.broadcasted_iota(jnp.int32, (2 * span, clusters), 0)
     rows = jnp.where(rows < span, rows, rows - span).astype(jnp.float32)
     for c in range(cols):
-        first = stencils[c, SAMPLES : SAMPLES + 1, :] - corner
-        second = stencils[c, SAMPLES + 1 : SAMPLES + 2, :] - c * span
+        first = phases[c, SIDE, :1] - corner
+        second = phases[c, SIDE, 1:2] - c * span
         hot = jnp.concatenate(
             [jnp.where(rows == second + y, 1.0, 0.0) for y in range(SIDE)], axis=1
         ).astype(jnp.bfloat16)
@@ -422,11 +431,13 @@
     packed = pl.pallas_call(
         spread_kernel,
         out_shape=jax.ShapeDtypeStruct((HEIGHT, clusters), f32),
+        compiler_params=pltpu.CompilerParams(vmem_limit_bytes=24 << 20),
         name="spread",
     )(density, interp_weight, stencil_corner)
     line = jnp.stack([packed] + [swapped(packed, "z", o) for o in range(1, deep)])
     sources = [line] + [swapped(line, PLANE, o) for o in range(1, wide * high)]
     sources += [swapped(source, "core", 1) for source in sources]
+    sources = [in_vmem(source) for source in sources]
 
     factor = 1.0 / math.sqrt(density.shape[1] * devices)
     first_parity = device % second_parts
@@ -437,18 +448,17 @@
     tables = half_tables()
     tx = jnp.asarray(tables)
     txt = jnp.asarray(np.ascontiguousarray(np.swapaxes(tables, 2, 3)))
-    if pars == 2:
-        ty, tyt = tx, txt
-    else:
-        ty = lax.dynamic_slice_in_dim(tx, first_parity, 1, axis=0)
-        tyt = lax.dynamic_slice_in_dim(txt, first_parity, 1, axis=0)
+    tables = [tx, txt]
+    if pars == 1:
+        tables += [lax.dynamic_slice_in_dim(t, first_parity, 1, axis=0) for t in tables]
+    tables = [in_vmem(table) for table in tables]
 
     smem = pl.BlockSpec(memory_space=pltpu.SMEM)
-    line_block = pl.BlockSpec((deep, HEIGHT, clusters), lambda r, where: (0, 0, 0))
+    line_block = pl.BlockSpec(memory_space=pltpu.VMEM)
     phase_row = pl.BlockSpec(
-        (cols_total, SIDE, 2 * bins, clusters), lambda r, where: (r, 0, 0, 0)
-    )
-    slab_block = pl.BlockSpec((2, parts, slab, HALF), lambda r, where: (0, 0, r, 0))
+        (cols_total, SIDE + 1, 2 * bins, clusters), lambda r, where: (r, 0, 0, 0)
+    )
+    vmem = pl.BlockSpec(memory_space=pltpu.VMEM)
     span = G // cols_total
     field, phases = pl.pallas_call(
         functools.partial(scatter_kernel, third_live, wide, high),
@@ -456,69 +466,70 @@
             num_scalar_prefetch=1,
             grid=(rows_total,),
             in_specs=[line_block] * len(sources),
-            out_specs=[slab_block, phase_row],
+            out_specs=[vmem, phase_row],
             scratch_shapes=[
                 pltpu.VMEM((cols_total, HEIGHT, clusters), f32),
                 pltpu.VMEM((cols_total, FINE * span // HALF, slab // FINE * 2 * parts, HALF), f32),
             ],
         ),
         out_shape=[
-            jax.ShapeDtypeStruct((2, parts, G, HALF), f32),
-            jax.ShapeDtypeStruct((devices, SIDE, 2 * bins, clusters), f32),
+            pltpu.VMEM((2, parts, G, HALF), f32),
+            jax.ShapeDtypeStruct((devices, SIDE + 1, 2 * bins, clusters), f32),
         ],
+        compiler_params=pltpu.CompilerParams(vmem_limit_bytes=24 << 20),
         name="scatter",
     )(where, *sources)
 
-    plane = pl.BlockSpec((2, 3, 1, 2, G, HALF), lambda m: (0, 0, m, 0, 0, 0))
-    table = pl.BlockSpec((2, 2, G, G), lambda m: (0, 0, 0, 0))
-    table_y = pl.BlockSpec((pars, 2, G, G), lambda m: (0, 0, 0, 0))
+    field = in_vmem(field.reshape(2, 3, bins, 2, G, HALF))
     field = pl.pallas_call(
-        functools.partial(dft_kernel, factor, third_live),
+        functools.partial(dft_kernel, factor, third_live, pars),
         grid=(bins,),
-        in_specs=[smem, plane, table, table, table_y, table_y],
-        out_specs=plane,
-        out_shape=jax.ShapeDtypeStruct((2, 3, bins, 2, G, HALF), f32),
+        in_specs=[smem] + [vmem] * (1 + len(tables)),
+        out_specs=vmem,
+        out_shape=pltpu.VMEM((2, 3, bins, 2, G, HALF), f32),
         scratch_shapes=[
             pltpu.VMEM((3, 2, G, width), f32),
             pltpu.VMEM((3, 2, G, width), f32),
         ],
+        compiler_params=pltpu.CompilerParams(vmem_limit_bytes=24 << 20),
         name="spectral",
-    )(where, field.reshape(2, 3, bins, 2, G, HALF), tx, txt, ty, tyt)
+    )(where, field, *tables)
 
     sample_block = pl.BlockSpec(
         (1, high, 1, HEIGHT, clusters),
         lambda r, where: ((r % wide) ^ where[3], 0, (r // wide) ^ where[2], 0, 0),
     )
     mine, other = pl.pallas_call(
-        functools.partial(gather_kernel, wide, high),
+        gather_kernel,
         grid_spec=pltpu.PrefetchScalarGridSpec(
             num_scalar_prefetch=1,
             grid=(rows_total,),
-            in_specs=[line_block] * len(sources) + [phase_row, slab_block],
+            in_specs=[phase_row, vmem],
             out_specs=[sample_block] * 2,
             scratch_shapes=[
-                pltpu.VMEM((cols_total, HEIGHT, clusters), f32),
                 pltpu.VMEM((2, slab * parts, HALF), f32),
                 pltpu.VMEM((2, slab * parts, SIDE * clusters), f32),
                 pltpu.VMEM((2, high, HEIGHT, clusters), f32),
             ],
         ),
         out_shape=[jax.ShapeDtypeStruct((wide, high, deep, HEIGHT, clusters), f32)] * 2,
+        compiler_params=pltpu.CompilerParams(vmem_limit_bytes=24 << 20),
         name="gather",
-    )(where, *sources, phases, field.reshape(2, parts, G, HALF))
+    )(where, phases, in_vmem(field.reshape(2, parts, G, HALF)))
     sampled = (mine + swapped(other, "core", 1)).reshape(wide * high, deep, HEIGHT, clusters)
     line = sampled[0] + sum(swapped(sampled[o], PLANE, o) for o in range(1, wide * high))
     samples = [line[0]] + [swapped(line[o], "z", o) for o in range(1, deep)]
+    samples = [in_vmem(sample) for sample in samples]
     near = near_field(
         density.reshape(3, clusters, panels), near_tiles, pair_target, pair_count
     )
-    vmem = pl.BlockSpec(memory_space=pltpu.VMEM)
     return pl.pallas_call(
         final_kernel,
         in_specs=[smem] + [vmem] * (2 + deep),
         out_shape=jax.ShapeDtypeStruct(density.shape, f32),
+        compiler_params=pltpu.CompilerParams(vmem_limit_bytes=24 << 20),
         name="final",
-    )(pair_landing, near, proj_weight, *samples)
+    )(pair_landing, near, in_vmem(proj_weight), *samples)
 
 
 def solution(mesh):

time: 108 us -> 101 us (0.935)
  Pallas kernels: 57 us -> 46 us
  local copies, waits for them, and re-layouts: 5.17 us -> 8.21 us
  waiting for transfers between devices: 19.1 us -> 21.4 us
    pallas_call x2, Pallas kernels: 30.5 us -> 25 us  [the longest x1 13.8 us: per_device(): pl.pallas_call(functools.partial(dft_kernel, factor, third_live, pars), g...]
    unnamed x24 -> x20, local copies, waits for them, and re-layouts: 2.36 us -> 6.58 us
    pallas_call x1, Pallas kernels: 17.2 us -> 14.4 us  [per_device(): pl.pallas_call(functools.partial(scatter_kernel, third_live, wide, high),...]
    ppermute x17, waiting for transfers between devices: 13.1 us -> 15.5 us  [swapped(): return lax.ppermute(values, axes, [(i, i ^ offset) for i in range(count)])]
    pallas_call x1, Pallas kernels: 5.22 us -> 3.48 us  [per_device(): pl.pallas_call(spread_kernel, out_shape=jax.ShapeDtypeStruct((HEIGHT, clu...]
  transfers between devices with their start and end apart: 19 -> 19, of which waited for: 9 -> 12; matrix products, arithmetic and copies ran while one was open for 5% -> 5% of each run, Pallas kernels for 0% -> 0%
where the time goes in v6:
time: 101 us
  Pallas kernels  46 us (46%)
  waiting for transfers between devices  21.4 us (21%)
  starting transfers between devices  19.4 us (19%)
  local copies, waits for them, and re-layouts  8.21 us (8%)
  other arithmetic  4.53 us (4%)
    ppermute x17, starting transfers between devices, swapped(): return lax.ppermute(values, axes, [(i, i ^ offset) for i in range(count)])  17.3 us
    ppermute x17, waiting for transfers between devices, swapped(): return lax.ppermute(values, axes, [(i, i ^ offset) for i in range(count)])  15.5 us
    pallas_call x1, Pallas kernels, per_device(): pl.pallas_call(functools.partial(scatter_kernel, third_live, wide, high),...  14.4 us
    pallas_call x1, Pallas kernels, per_device(): pl.pallas_call(functools.partial(dft_kernel, factor, third_live, pars), g...  13.8 us
    pallas_call x1, Pallas kernels, per_device(): pl.pallas_call(gather_kernel, grid_spec=pltpu.PrefetchScalarGridSpec(num_...  11.2 us
    unnamed x20, local copies, waits for them, and re-layouts  6.58 us
    ppermute x2, waiting for transfers between devices, row_shift(): lax.ppermute(values, ROW, [(i, (i + by) % count) for i in range(count)])  5.95 us
    pallas_call x1, Pallas kernels, per_device(): pl.pallas_call(spread_kernel, out_shape=jax.ShapeDtypeStruct((HEIGHT, clu...  3.48 us
  transfers between devices with their start and end apart: 19, of which 12 were waited for; matrix products, arithmetic and copies ran while one was open for 5% of the time, Pallas kernels for 0%

profile of v6, /device:TPU:0, one launch (start us, length us, event | category | flops | bytes accessed | tf_op | source)
XLA Modules:
  0.0 100.9 jit_solution(13427191775735570888)
XLA Ops:
  0.0 0.0 copy-start
  0.0 1.7 %copy-done.1 = f32[27,16384]{1,0:T(8,128)S(1)} copy-done((f32[27,16384]{1,0:T(8,128)S(1)}, f32[27,16384]{1,0:T(8,128)}, u32[]{:S(2)}) %copy-start.1) | copy-done | bytes 1769496
  1.7 0.9 copy-done.3
  2.7 0.7 copy-done.8
  3.4 3.5 %spread.1 = f32[88,128]{1,0:T(8,128)} custom-call(f32[3,16384]{1,0:T(4,128)S(1)} %copy-done.3, f32[27,16384]{1,0:T(8,128)S(1)} %copy-done.1, s32[3,128]{1,0:T(4,128)S(1)} %copy-done.8), custom_call_target="tpu_custom_call" | custom-call | tf_op jit(solution)/shard_map/spread/pallas_call | solution.py:431
  6.9 3.1 %collective-permute-start.2 = (f32[88,128]{1,0:T(8,128)}, f32[88,128]{1,0:T(8,128)}, u32[]{:S(2)}, u32[]{:S(2)}) collective-permute-start(f32[88,128]{1,0:T(8,128)} %spread.1), channel_id=1, source_target_pairs={{0,8},{8,0},{16,24},{24,16},{1,9},{9,1},{17,25},{25,17},{2,10},{10... | collective-permute-start | bytes 135176 | tf_op jit(solution)/shard_map/ppermute | solution.py:29
  9.9 2.6 %collective-permute-start.3 = (f32[88,128]{1,0:T(8,128)}, f32[88,128]{1,0:T(8,128)}, u32[]{:S(2)}, u32[]{:S(2)}) collective-permute-start(f32[88,128]{1,0:T(8,128)} %spread.1), channel_id=1, source_target_pairs={{0,16},{8,24},{16,0},{24,8},{1,17},{9,25},{17,1},{25,9},{2,18},{10... | collective-permute-start | bytes 135176 | tf_op jit(solution)/shard_map/ppermute | solution.py:29
  12.5 0.0 collective-permute-start.4
  13.2 0.1 stack.51.where
  13.2 0.0 collective-permute-done.2
  13.2 2.8 %collective-permute-done.3 = f32[88,128]{1,0:T(8,128)} collective-permute-done((f32[88,128]{1,0:T(8,128)}, f32[88,128]{1,0:T(8,128)}, u32[]{:S(2)}, u32[]{:S(2)}) %collective-permute-start.3) | collective-permute-done | bytes 45088 | tf_op jit(solution)/shard_map/ppermute | solution.py:29
  16.0 2.6 %collective-permute-done.4 = f32[88,128]{1,0:T(8,128)} collective-permute-done((f32[88,128]{1,0:T(8,128)}, f32[88,128]{1,0:T(8,128)}, u32[]{:S(2)}, u32[]{:S(2)}) %collective-permute-start.4) | collective-permute-done | bytes 45088 | tf_op jit(solution)/shard_map/ppermute | solution.py:29
  18.7 0.9 pad_maximum_fusion.refs_0_
  19.5 1.6 %collective-permute-start.6 = (f32[4,88,128]{2,1,0:T(8,128)S(1)}, f32[4,88,128]{2,1,0:T(8,128)S(1)}, u32[]{:S(2)}, u32[]{:S(2)}) collective-permute-start(f32[4,88,128]{2,1,0:T(8,128)S(1)} %pad_maximum_fusion.refs_0_), channel_id=1, source_target_pairs={{0,4},{2,6},{4,0},{6,2},{1,5},{3,7},{5,1},{7,3},{8,12},{10,14},{12... | collective-permute-start | bytes 540680 | tf_op jit(solution)/shard_map/ppermute | solution.py:29
  21.1 1.5 %collective-permute-start.7 = (f32[4,88,128]{2,1,0:T(8,128)S(1)}, f32[4,88,128]{2,1,0:T(8,128)S(1)}, u32[]{:S(2)}, u32[]{:S(2)}) collective-permute-start(f32[4,88,128]{2,1,0:T(8,128)S(1)} %pad_maximum_fusion.refs_0_), channel_id=1, source_target_pairs={{0,6},{2,4},{4,2},{6,0},{1,7},{3,5},{5,3},{7,1},{8,14},{10,12},{12... | collective-permute-start | bytes 540680 | tf_op jit(solution)/shard_map/ppermute | solution.py:29
  22.6 0.5 collective-permute-start.5
  23.1 1.6 %convert_bitcast_fusion = bf16[3,128,128]{2,0,1:T(4,128)(2,1)} fusion(f32[3,16384]{1,0:T(4,128)} %density.1), kind=kLoop, calls=%fused_computation.9 | loop fusion | flops 49152 | bytes 294912 | tf_op jit(solution)/shard_map/convert_element_type | solution.py:43
  24.7 0.0 collective-permute-start.8
  24.7 1.7 %collective-permute-done.6.refs_2_ = f32[4,88,128]{2,1,0:T(8,128)S(1)} collective-permute-done((f32[4,88,128]{2,1,0:T(8,128)S(1)}, f32[4,88,128]{2,1,0:T(8,128)S(1)}, u32[]{:S(2)}, u32[]{:S(2)}) %collective-permute-start.6) | collective-permute-done | bytes 180256 | tf_op jit(solution)/shard_map/ppermute | solution.py:29
  26.4 0.0 collective-permute-start.10
  26.5 2.7 %collective-permute-done.7.refs_3_ = f32[4,88,128]{2,1,0:T(8,128)S(1)} collective-permute-done((f32[4,88,128]{2,1,0:T(8,128)S(1)}, f32[4,88,128]{2,1,0:T(8,128)S(1)}, u32[]{:S(2)}, u32[]{:S(2)}) %collective-permute-start.7) | collective-permute-done | bytes 180256 | tf_op jit(solution)/shard_map/ppermute | solution.py:29
  29.2 0.0 collective-permute-start.11
  29.2 1.4 %collective-permute-done.5.refs_1_ = f32[4,88,128]{2,1,0:T(8,128)S(1)} collective-permute-done((f32[4,88,128]{2,1,0:T(8,128)S(1)}, f32[4,88,128]{2,1,0:T(8,128)S(1)}, u32[]{:S(2)}, u32[]{:S(2)}) %collective-permute-start.5) | collective-permute-done | bytes 180256 | tf_op jit(solution)/shard_map/ppermute | solution.py:29
  30.6 0.0 collective-permute-start.9
  30.6 0.7 compare_select_fusion
  31.2 0.0 collective-permute-done.8.refs_4_
  31.2 0.0 collective-permute-done.10.refs_6_
  31.2 0.0 collective-permute-done.11.refs_7_
  31.2 0.7 collective-permute-done.9.refs_5_
  32.0 14.4 %scatter.1 = (f32[2,24,256,128]{3,2,1,0:T(8,128)S(1)}, f32[32,4,8,128]{3,2,1,0:T(8,128)S(1)}) custom-call(s32[6]{0:T(128)S(1)} %stack.51.where, f32[4,88,128]{2,1,0:T(8,128)S(1)} %pad_maximum_fusion.refs_0_, f32[4,88,128]{2,1,0:T(8,128)S(1)} %collective-permute-done.5.refs_1_, f32[4,88,128]{2,1,0:T(8,128)S(1)} %collective-permute-done.6.refs_2_, ...), custom_call_target="tpu_custom_call" | custom-call | tf_op jit(solution)/shard_map/scatter/pallas_call | solution.py:463
  46.4 0.0 copy-start.6
  46.4 1.0 %copy-done.6 = bf16[2,2,256,256]{3,2,1,0:T(8,128)(2,1)S(1)} copy-done((bf16[2,2,256,256]{3,2,1,0:T(8,128)(2,1)S(1)}, bf16[2,2,256,256]{3,2,1,0:T(8,128)(2,1)}, u32[]{:S(2)}) %copy-start.6) | copy-done | bytes 524312
  47.5 1.0 %copy-done.7 = bf16[2,2,256,256]{3,2,1,0:T(8,128)(2,1)S(1)} copy-done((bf16[2,2,256,256]{3,2,1,0:T(8,128)(2,1)S(1)}, bf16[2,2,256,256]{3,2,1,0:T(8,128)(2,1)}, u32[]{:S(2)}) %copy-start.7) | copy-done | bytes 524312
  48.5 13.8 %spectral.1 = f32[2,3,4,2,256,128]{5,4,3,2,1,0:T(8,128)S(1)} custom-call(s32[6]{0:T(128)S(1)} %stack.51.where, f32[2,3,4,2,256,128]{5,4,3,2,1,0:T(8,128)S(1)} %bitcast.52, bf16[2,2,256,256]{3,2,1,0:T(8,128)(2,1)S(1)} %copy-done.6, bf16[2,2,256,256]{3,2,1,0:T(8,128)(2,1)S(1)} %copy-done.7), custom_call_target="tpu_custom_call" | custom-call | tf_op jit(solution)/shard_map/spectral/pallas_call | solution.py:484
  62.3 11.2 %gather.7 = (f32[2,2,4,88,128]{4,3,2,1,0:T(8,128)S(1)}, f32[2,2,4,88,128]{4,3,2,1,0:T(8,128)}) custom-call(s32[6]{0:T(128)S(1)} %stack.51.where, f32[32,4,8,128]{3,2,1,0:T(8,128)S(1)} %get-tuple-element.9.phases, f32[2,24,256,128]{3,2,1,0:T(8,128)S(1)} %bitcast.51), custom_call_target="tpu_custom_call" | custom-call | tf_op jit(solution)/shard_map/gather/pallas_call | solution.py:502
  73.5 0.9 copy-done.4
  74.4 0.1 collective-permute-start.12
  74.6 1.5 %gather_fusion = bf16[12,3,128]{2,1,0:T(4,128)(2,1)S(1)} fusion(bf16[3,128,128]{2,0,1:T(4,128)(2,1)} %convert_bitcast_fusion, s32[1024]{0:T(1024)S(1)} %pad_clamp_fusion), kind=kCustom, calls=%fused_computation | custom fusion | bytes 18480 | tf_op jit(solution)/shard_map/gather | solution.py:46
  76.1 0.0 copy-done
  76.1 0.0 copy-start.2
  76.1 0.0 copy-start.9
  76.1 0.6 fusion
  76.7 0.1 bitcast_select_fusion
  76.9 0.1 collective-permute-done.12
  77.0 0.2 copy-done.5
  77.2 1.2 %add.31 = f32[2,2,4,88,128]{4,3,2,1,0:T(8,128)S(1)} add(f32[2,2,4,88,128]{4,3,2,1,0:T(8,128)S(1)} %copy-done.5, f32[2,2,4,88,128]{4,3,2,1,0:T(8,128)} %collective-permute-done.12) | non-fusion elementwise | flops 180224 | bytes 2162688 | tf_op jit(solution)/shard_map/add | solution.py:519
  78.4 0.6 collective-permute-start.13
  79.0 1.5 %collective-permute-start.14 = (f32[4,88,128]{2,1,0:T(8,128)S(1)}, f32[4,88,128]{2,1,0:T(8,128)S(1)}, u32[]{:S(2)}, u32[]{:S(2)}) collective-permute-start(f32[4,88,128]{2,1,0:T(8,128)S(1)} %get-tuple-element.13), channel_id=1, source_target_pairs={{0,4},{2,6},{4,0},{6,2},{1,5},{3,7},{5,1},{7,3},{8,12},{10,14},{12... | collective-permute-start | bytes 540680 | tf_op jit(solution)/shard_map/ppermute | solution.py:29
  80.5 1.5 %collective-permute-start.15 = (f32[4,88,128]{2,1,0:T(8,128)S(1)}, f32[4,88,128]{2,1,0:T(8,128)S(1)}, u32[]{:S(2)}, u32[]{:S(2)}) collective-permute-start(f32[4,88,128]{2,1,0:T(8,128)S(1)} %get-tuple-element.14), channel_id=1, source_target_pairs={{0,6},{2,4},{4,2},{6,0},{1,7},{3,5},{5,3},{7,1},{8,14},{10,12},{12... | collective-permute-start | bytes 540680 | tf_op jit(solution)/shard_map/ppermute | solution.py:29
  82.0 1.6 %collective-permute-start = (f32[4,3,128]{2,1,0:T(4,128)S(1)}, f32[4,3,128]{2,1,0:T(4,128)S(1)}, u32[]{:S(2)}, u32[]{:S(2)}) collective-permute-start(f32[4,3,128]{2,1,0:T(4,128)S(1)} %get-tuple-element.20), channel_id=1, source_target_pairs={{0,28},{4,0},{8,4},{12,8},{16,12},{20,16},{24,20},{28,24},{1,29},{... | collective-permute-start | bytes 18440 | tf_op jit(solution)/shard_map/ppermute | solution.py:38
  83.6 0.4 collective-permute-start.1
  84.0 5.7 %collective-permute-done = f32[4,3,128]{2,1,0:T(4,128)S(1)} collective-permute-done((f32[4,3,128]{2,1,0:T(4,128)S(1)}, f32[4,3,128]{2,1,0:T(4,128)S(1)}, u32[]{:S(2)}, u32[]{:S(2)}) %collective-permute-start) | collective-permute-done | bytes 6176 | tf_op jit(solution)/shard_map/ppermute | solution.py:38
  89.7 0.3 collective-permute-done.1
  90.0 0.0 collective-permute-done.13
  90.0 0.0 collective-permute-done.14
  90.0 0.6 collective-permute-done.15
  90.7 0.1 collective-permute-start.16
  90.8 1.2 %collective-permute-start.17 = (f32[88,128]{1,0:T(8,128)S(1)}, f32[88,128]{1,0:T(8,128)S(1)}, u32[]{:S(2)}, u32[]{:S(2)}) collective-permute-start(f32[88,128]{1,0:T(8,128)S(1)} %get-tuple-element.17), channel_id=1, source_target_pairs={{0,16},{8,24},{16,0},{24,8},{1,17},{9,25},{17,1},{25,9},{2,18},{10... | collective-permute-start | bytes 135176 | tf_op jit(solution)/shard_map/ppermute | solution.py:29
  92.0 3.1 %collective-permute-start.18 = (f32[88,128]{1,0:T(8,128)S(1)}, f32[88,128]{1,0:T(8,128)S(1)}, u32[]{:S(2)}, u32[]{:S(2)}) collective-permute-start(f32[88,128]{1,0:T(8,128)S(1)} %get-tuple-element.16), channel_id=1, source_target_pairs={{0,24},{8,16},{16,8},{24,0},{1,25},{9,17},{17,9},{25,1},{2,26},{10... | collective-permute-start | bytes 135176 | tf_op jit(solution)/shard_map/ppermute | solution.py:29
  95.2 0.0 collective-permute-done.16.refs_1_
  95.2 0.8 collective-permute-done.17.refs_2_
  96.0 1.9 %collective-permute-done.18.refs_3_ = f32[88,128]{1,0:T(8,128)S(1)} collective-permute-done((f32[88,128]{1,0:T(8,128)S(1)}, f32[88,128]{1,0:T(8,128)S(1)}, u32[]{:S(2)}, u32[]{:S(2)}) %collective-permute-start.18) | collective-permute-done | bytes 45088 | tf_op jit(solution)/shard_map/ppermute | solution.py:29
  97.9 0.0 copy-done.2
  97.9 3.1 %final.1 = f32[3,16384]{1,0:T(4,128)} custom-call(s32[12]{0:T(128)S(1)} %copy-done.9, f32[12,3,128]{2,1,0:T(4,128)S(1)} %pad_maximum_fusion.1.near, f32[27,16384]{1,0:T(8,128)S(1)} %copy-done.2, f32[88,128]{1,0:T(8,128)S(1)} %get-tuple-element.19.refs_0_, f32[88,128]{1,0:T(8,128)S(1)} %collective-permute-done.16.refs_1_, ...), custom_call_target="tpu_custom_call" | custom-call | tf_op jit(solution)/shard_map/final/pallas_call | solution.py:526
  (17 shorter events, 0.1 us)
Async XLA Ops:
  0.0 76.1 %copy-start = (bf16[12,3,3,128,128]{4,3,2,1,0:T(8,128)(2,1)S(1)}, bf16[12,3,3,128,128]{4,3,2,1,0:T(8,128)(2,1)}, u32[]{:S(2)}) copy-start(bf16[12,3,3,128,128]{4,3,2,1,0:T(8,128)(2,1)} %param.14) | copy-start | bytes 10616836
  0.0 1.7 %copy-start.1 = (f32[27,16384]{1,0:T(8,128)S(1)}, f32[27,16384]{1,0:T(8,128)}, u32[]{:S(2)}) copy-start(f32[27,16384]{1,0:T(8,128)} %weights.2) | copy-start | bytes 5308420
  1.7 0.9 copy-start.3
  2.7 0.7 copy-start.8
  6.9 6.4 %collective-permute-start.2 = (f32[88,128]{1,0:T(8,128)}, f32[88,128]{1,0:T(8,128)}, u32[]{:S(2)}, u32[]{:S(2)}) collective-permute-start(f32[88,128]{1,0:T(8,128)} %spread.1), channel_id=1, source_target_pairs={{0,8},{8,0},{16,24},{24,16},{1,9},{9,1},{17,25},{25,17},{2,10},{10... | collective-permute-start | bytes 135176 | tf_op jit(solution)/shard_map/ppermute | solution.py:29
  9.9 6.1 %collective-permute-start.3 = (f32[88,128]{1,0:T(8,128)}, f32[88,128]{1,0:T(8,128)}, u32[]{:S(2)}, u32[]{:S(2)}) collective-permute-start(f32[88,128]{1,0:T(8,128)} %spread.1), channel_id=1, source_target_pairs={{0,16},{8,24},{16,0},{24,8},{1,17},{9,25},{17,1},{25,9},{2,18},{10... | collective-permute-start | bytes 135176 | tf_op jit(solution)/shard_map/ppermute | solution.py:29
  12.5 6.2 %collective-permute-start.4 = (f32[88,128]{1,0:T(8,128)}, f32[88,128]{1,0:T(8,128)}, u32[]{:S(2)}, u32[]{:S(2)}) collective-permute-start(f32[88,128]{1,0:T(8,128)} %spread.1), channel_id=1, source_target_pairs={{0,24},{8,16},{16,8},{24,0},{1,25},{9,17},{17,9},{25,1},{2,26},{10... | collective-permute-start | bytes 135176 | tf_op jit(solution)/shard_map/ppermute | solution.py:29
  19.5 6.9 %collective-permute-start.6 = (f32[4,88,128]{2,1,0:T(8,128)S(1)}, f32[4,88,128]{2,1,0:T(8,128)S(1)}, u32[]{:S(2)}, u32[]{:S(2)}) collective-permute-start(f32[4,88,128]{2,1,0:T(8,128)S(1)} %pad_maximum_fusion.refs_0_), channel_id=1, source_target_pairs={{0,4},{2,6},{4,0},{6,2},{1,5},{3,7},{5,1},{7,3},{8,12},{10,14},{12... | collective-permute-start | bytes 540680 | tf_op jit(solution)/shard_map/ppermute | solution.py:29
  21.1 8.1 %collective-permute-start.7 = (f32[4,88,128]{2,1,0:T(8,128)S(1)}, f32[4,88,128]{2,1,0:T(8,128)S(1)}, u32[]{:S(2)}, u32[]{:S(2)}) collective-permute-start(f32[4,88,128]{2,1,0:T(8,128)S(1)} %pad_maximum_fusion.refs_0_), channel_id=1, source_target_pairs={{0,6},{2,4},{4,2},{6,0},{1,7},{3,5},{5,3},{7,1},{8,14},{10,12},{12... | collective-permute-start | bytes 540680 | tf_op jit(solution)/shard_map/ppermute | solution.py:29
  22.6 8.0 %collective-permute-start.5 = (f32[4,88,128]{2,1,0:T(8,128)S(1)}, f32[4,88,128]{2,1,0:T(8,128)S(1)}, u32[]{:S(2)}, u32[]{:S(2)}) collective-permute-start(f32[4,88,128]{2,1,0:T(8,128)S(1)} %pad_maximum_fusion.refs_0_), channel_id=1, source_target_pairs={{0,2},{2,0},{4,6},{6,4},{1,3},{3,1},{5,7},{7,5},{8,10},{10,8},{12,... | collective-permute-start | bytes 540680 | tf_op jit(solution)/shard_map/ppermute | solution.py:29
  24.7 6.5 %collective-permute-start.8 = (f32[4,88,128]{2,1,0:T(8,128)S(1)}, f32[4,88,128]{2,1,0:T(8,128)S(1)}, u32[]{:S(2)}, u32[]{:S(2)}) collective-permute-start(f32[4,88,128]{2,1,0:T(8,128)S(1)} %pad_maximum_fusion.refs_0_), channel_id=1, source_target_pairs={{0,1},{1,0},{2,3},{3,2},{4,5},{5,4},{6,7},{7,6},{8,9},{9,8},{10,11... | collective-permute-start | bytes 540680 | tf_op jit(solution)/shard_map/ppermute | solution.py:29
  26.4 4.8 %collective-permute-start.10 = (f32[4,88,128]{2,1,0:T(8,128)S(1)}, f32[4,88,128]{2,1,0:T(8,128)S(1)}, u32[]{:S(2)}, u32[]{:S(2)}) collective-permute-start(f32[4,88,128]{2,1,0:T(8,128)S(1)} %collective-permute-done.6.refs_2_), channel_id=1, source_target_pairs={{0,1},{1,0},{2,3},{3,2},{4,5},{5,4},{6,7},{7,6},{8,9},{9,8},{10,11... | collective-permute-start | bytes 540680 | tf_op jit(solution)/shard_map/ppermute | solution.py:29
  29.2 2.0 %collective-permute-start.11 = (f32[4,88,128]{2,1,0:T(8,128)S(1)}, f32[4,88,128]{2,1,0:T(8,128)S(1)}, u32[]{:S(2)}, u32[]{:S(2)}) collective-permute-start(f32[4,88,128]{2,1,0:T(8,128)S(1)} %collective-permute-done.7.refs_3_), channel_id=1, source_target_pairs={{0,1},{1,0},{2,3},{3,2},{4,5},{5,4},{6,7},{7,6},{8,9},{9,8},{10,11... | collective-permute-start | bytes 540680 | tf_op jit(solution)/shard_map/ppermute | solution.py:29
  30.6 1.4 %collective-permute-start.9 = (f32[4,88,128]{2,1,0:T(8,128)S(1)}, f32[4,88,128]{2,1,0:T(8,128)S(1)}, u32[]{:S(2)}, u32[]{:S(2)}) collective-permute-start(f32[4,88,128]{2,1,0:T(8,128)S(1)} %collective-permute-done.5.refs_1_), channel_id=1, source_target_pairs={{0,1},{1,0},{2,3},{3,2},{4,5},{5,4},{6,7},{7,6},{8,9},{9,8},{10,11... | collective-permute-start | bytes 540680 | tf_op jit(solution)/shard_map/ppermute | solution.py:29
  46.4 1.0 %copy-start.6 = (bf16[2,2,256,256]{3,2,1,0:T(8,128)(2,1)S(1)}, bf16[2,2,256,256]{3,2,1,0:T(8,128)(2,1)}, u32[]{:S(2)}) copy-start(bf16[2,2,256,256]{3,2,1,0:T(8,128)(2,1)} %constant.52.clone.refs_0_) | copy-start | bytes 1572868
  47.5 1.0 %copy-start.7 = (bf16[2,2,256,256]{3,2,1,0:T(8,128)(2,1)S(1)}, bf16[2,2,256,256]{3,2,1,0:T(8,128)(2,1)}, u32[]{:S(2)}) copy-start(bf16[2,2,256,256]{3,2,1,0:T(8,128)(2,1)} %constant.53.clone.refs_1_) | copy-start | bytes 1572868
  73.5 0.9 copy-start.4
  74.4 2.5 %collective-permute-start.12 = (f32[2,2,4,88,128]{4,3,2,1,0:T(8,128)}, f32[2,2,4,88,128]{4,3,2,1,0:T(8,128)}, u32[]{:S(2)}, u32[]{:S(2)}) collective-permute-start(f32[2,2,4,88,128]{4,3,2,1,0:T(8,128)} %get-tuple-element.12), channel_id=1, source_target_pairs={{0,1},{1,0},{2,3},{3,2},{4,5},{5,4},{6,7},{7,6},{8,9},{9,8},{10,11... | collective-permute-start | bytes 2162696 | tf_op jit(solution)/shard_map/ppermute | solution.py:29
  76.1 1.1 %copy-start.5 = (f32[2,2,4,88,128]{4,3,2,1,0:T(8,128)S(1)}, f32[2,2,4,88,128]{4,3,2,1,0:T(8,128)}, u32[]{:S(2)}) copy-start(f32[2,2,4,88,128]{4,3,2,1,0:T(8,128)} %copy-done.4) | copy-start | bytes 2162692
  76.1 21.8 %copy-start.2 = (f32[27,16384]{1,0:T(8,128)S(1)}, f32[27,16384]{1,0:T(8,128)}, u32[]{:S(2)}) copy-start(f32[27,16384]{1,0:T(8,128)} %weights.3) | copy-start | bytes 5308420
  76.1 21.8 %copy-start.9 = (s32[12]{0:T(128)S(1)}, s32[12]{0:T(128)}, u32[]{:S(2)}) copy-start(s32[12]{0:T(128)} %landing.1) | copy-start | bytes 148
  78.4 11.6 %collective-permute-start.13 = (f32[4,88,128]{2,1,0:T(8,128)S(1)}, f32[4,88,128]{2,1,0:T(8,128)S(1)}, u32[]{:S(2)}, u32[]{:S(2)}) collective-permute-start(f32[4,88,128]{2,1,0:T(8,128)S(1)} %get-tuple-element.15), channel_id=1, source_target_pairs={{0,2},{2,0},{4,6},{6,4},{1,3},{3,1},{5,7},{7,5},{8,10},{10,8},{12,... | collective-permute-start | bytes 540680 | tf_op jit(solution)/shard_map/ppermute | solution.py:29
  79.0 11.0 %collective-permute-start.14 = (f32[4,88,128]{2,1,0:T(8,128)S(1)}, f32[4,88,128]{2,1,0:T(8,128)S(1)}, u32[]{:S(2)}, u32[]{:S(2)}) collective-permute-start(f32[4,88,128]{2,1,0:T(8,128)S(1)} %get-tuple-element.13), channel_id=1, source_target_pairs={{0,4},{2,6},{4,0},{6,2},{1,5},{3,7},{5,1},{7,3},{8,12},{10,14},{12... | collective-permute-start | bytes 540680 | tf_op jit(solution)/shard_map/ppermute | solution.py:29
  80.5 10.1 %collective-permute-start.15 = (f32[4,88,128]{2,1,0:T(8,128)S(1)}, f32[4,88,128]{2,1,0:T(8,128)S(1)}, u32[]{:S(2)}, u32[]{:S(2)}) collective-permute-start(f32[4,88,128]{2,1,0:T(8,128)S(1)} %get-tuple-element.14), channel_id=1, source_target_pairs={{0,6},{2,4},{4,2},{6,0},{1,7},{3,5},{5,3},{7,1},{8,14},{10,12},{12... | collective-permute-start | bytes 540680 | tf_op jit(solution)/shard_map/ppermute | solution.py:29
  82.0 7.7 %collective-permute-start = (f32[4,3,128]{2,1,0:T(4,128)S(1)}, f32[4,3,128]{2,1,0:T(4,128)S(1)}, u32[]{:S(2)}, u32[]{:S(2)}) collective-permute-start(f32[4,3,128]{2,1,0:T(4,128)S(1)} %get-tuple-element.20), channel_id=1, source_target_pairs={{0,28},{4,0},{8,4},{12,8},{16,12},{20,16},{24,20},{28,24},{1,29},{... | collective-permute-start | bytes 18440 | tf_op jit(solution)/shard_map/ppermute | solution.py:38
  83.6 6.3 %collective-permute-start.1 = (f32[4,3,128]{2,1,0:T(4,128)S(1)}, f32[4,3,128]{2,1,0:T(4,128)S(1)}, u32[]{:S(2)}, u32[]{:S(2)}) collective-permute-start(f32[4,3,128]{2,1,0:T(4,128)S(1)} %get-tuple-element.21), channel_id=1, source_target_pairs={{0,4},{4,8},{8,12},{12,16},{16,20},{20,24},{24,28},{28,0},{1,5},{5... | collective-permute-start | bytes 18440 | tf_op jit(solution)/shard_map/ppermute | solution.py:38
  90.7 4.5 %collective-permute-start.16 = (f32[88,128]{1,0:T(8,128)S(1)}, f32[88,128]{1,0:T(8,128)S(1)}, u32[]{:S(2)}, u32[]{:S(2)}) collective-permute-start(f32[88,128]{1,0:T(8,128)S(1)} %get-tuple-element.18), channel_id=1, source_target_pairs={{0,8},{8,0},{16,24},{24,16},{1,9},{9,1},{17,25},{25,17},{2,10},{10... | collective-permute-start | bytes 135176 | tf_op jit(solution)/shard_map/ppermute | solution.py:29
  90.8 5.2 %collective-permute-start.17 = (f32[88,128]{1,0:T(8,128)S(1)}, f32[88,128]{1,0:T(8,128)S(1)}, u32[]{:S(2)}, u32[]{:S(2)}) collective-permute-start(f32[88,128]{1,0:T(8,128)S(1)} %get-tuple-element.17), channel_id=1, source_target_pairs={{0,16},{8,24},{16,0},{24,8},{1,17},{9,25},{17,1},{25,9},{2,18},{10... | collective-permute-start | bytes 135176 | tf_op jit(solution)/shard_map/ppermute | solution.py:29
  92.0 5.8 %collective-permute-start.18 = (f32[88,128]{1,0:T(8,128)S(1)}, f32[88,128]{1,0:T(8,128)S(1)}, u32[]{:S(2)}, u32[]{:S(2)}) collective-permute-start(f32[88,128]{1,0:T(8,128)S(1)} %get-tuple-element.16), channel_id=1, source_target_pairs={{0,24},{8,16},{16,8},{24,0},{1,25},{9,17},{17,9},{25,1},{2,26},{10... | collective-permute-start | bytes 135176 | tf_op jit(solution)/shard_map/ppermute | solution.py:29

commit v7 on v6

--- a/solution.py
+++ b/solution.py
@@ -135,16 +135,19 @@
         out[:, at] = out[:, at] + near[q]
 
 
-def ordered(wide, high, where, sources, stencils):
-    row = pl.program_id(0)
-    deep = (row // wide) ^ where[2]
-    for o in range(wide * high):
-
-        @pl.when((row % wide) ^ where[3] == o // high)
-        def _():
+def ordered(group, high, step, where, sources, stencils):
+    deep = (step // group) ^ where[2]
+    for o in range(group * high):
+
+        def fill(o=o):
             y = (o % high) ^ where[4]
             stencils[2 * y + where[0]] = sources[o][deep]
-            stencils[2 * y + 1 - where[0]] = sources[wide * high + o][deep]
+            stencils[2 * y + 1 - where[0]] = sources[group * high + o][deep]
+
+        if group == 1:
+            fill()
+        else:
+            pl.when(step % group == o // high)(fill)
 
 
 def cosine(turns):
@@ -172,15 +175,18 @@
     ]
 
 
-def scatter_kernel(live, wide, high, where, *refs):
+def scatter_kernel(live, wide, high, begin, end, where, *refs):
     *sources, out, phases, stencils, total = refs
+    step = pl.program_id(0)
+    group = end - begin
+    row = step // group * wide + ((begin + step % group) ^ where[3])
     sides, parts, _, lanes = out.shape
     cols, _, clusters = stencils.shape
     span = G // cols
     slab = total.shape[2] // (2 * parts) * FINE
     coarse_cells = slab // FINE
-    corner = pl.program_id(0) * slab
-    ordered(wide, high, where, sources, stencils)
+    corner = row * slab
+    ordered(group, high, step, where, sources[: 2 * group * high], stencils)
     bins = lax.broadcasted_iota(jnp.int32, phases.shape[2:], 0)
     waves = bins // 2 + where[1]
     quarter = bins % 2 * (G // 4)
@@ -193,9 +199,11 @@
         first, second, third = (
             stencils[c, SAMPLES + i : SAMPLES + i + 1, :].astype(jnp.int32) for i in range(3)
         )
+        turned = []
         for z in range(SIDE):
-            phases[c, z] = jnp.where(kept, cosine((third + z) * waves + quarter), 0.0)
-        phases[c, SIDE, :2] = stencils[c, SAMPLES : SAMPLES + 2, :]
+            turned.append(jnp.where(kept, cosine((third + z) * waves + quarter), 0.0))
+            phases[row * cols + c, z] = turned[z]
+        phases[row * cols + c, SIDE, :2] = stencils[c, SAMPLES : SAMPLES + 2, :]
         hots, spreads = [], []
         for x in range(SIDE):
             cell = first - corner + x
@@ -215,10 +223,10 @@
                 )
                 modes = []
                 for a in range(3):
-                    row = a * STENCIL + x * 9 + y * 3
+                    at = a * STENCIL + x * 9 + y * 3
                     modes.append(
                         sum(
-                            stencils[c, row + z : row + z + 1, :] * phases[c, z]
+                            stencils[c, at + z : at + z + 1, :] * turned[z]
                             for z in range(SIDE)
                         )
                     )
@@ -249,9 +257,9 @@
                     + total[c, part, pl.ds(parts + v, coarse_cells, stride=2 * parts), :]
                     for c in range(side * across, (side + 1) * across)
                 ]
-                for i, row in enumerate(regrouped(values, span, left)):
+                for i, value in enumerate(regrouped(values, span, left)):
                     at = pl.ds(corner + part * across + i, coarse_cells, stride=FINE)
-                    out[side, v, at, :] = row
+                    out[side, v, at, :] = value
 
 
 def dft_kernel(factor, live, pars, where, field, *refs):
@@ -431,20 +439,10 @@
     packed = pl.pallas_call(
         spread_kernel,
         out_shape=jax.ShapeDtypeStruct((HEIGHT, clusters), f32),
-        compiler_params=pltpu.CompilerParams(vmem_limit_bytes=24 << 20),
         name="spread",
     )(density, interp_weight, stencil_corner)
     line = jnp.stack([packed] + [swapped(packed, "z", o) for o in range(1, deep)])
-    sources = [line] + [swapped(line, PLANE, o) for o in range(1, wide * high)]
-    sources += [swapped(source, "core", 1) for source in sources]
-    sources = [in_vmem(source) for source in sources]
-
-    factor = 1.0 / math.sqrt(density.shape[1] * devices)
     first_parity = device % second_parts
-    where = jnp.stack(
-        [here[3], device // second_parts * third_live, here[0], here[1], here[2], first_parity]
-    ).astype(jnp.int32)
-
     tables = half_tables()
     tx = jnp.asarray(tables)
     txt = jnp.asarray(np.ascontiguousarray(np.swapaxes(tables, 2, 3)))
@@ -452,33 +450,47 @@
     if pars == 1:
         tables += [lax.dynamic_slice_in_dim(t, first_parity, 1, axis=0) for t in tables]
     tables = [in_vmem(table) for table in tables]
+    line, *tables = lax.optimization_barrier((line, *tables))
+    sources = [line] + [swapped(line, PLANE, o) for o in range(1, wide * high)]
+
+    factor = 1.0 / math.sqrt(density.shape[1] * devices)
+    where = jnp.stack(
+        [here[3], device // second_parts * third_live, here[0], here[1], here[2], first_parity]
+    ).astype(jnp.int32)
 
     smem = pl.BlockSpec(memory_space=pltpu.SMEM)
-    line_block = pl.BlockSpec(memory_space=pltpu.VMEM)
     phase_row = pl.BlockSpec(
         (cols_total, SIDE + 1, 2 * bins, clusters), lambda r, where: (r, 0, 0, 0)
     )
     vmem = pl.BlockSpec(memory_space=pltpu.VMEM)
     span = G // cols_total
-    field, phases = pl.pallas_call(
-        functools.partial(scatter_kernel, third_live, wide, high),
-        grid_spec=pltpu.PrefetchScalarGridSpec(
-            num_scalar_prefetch=1,
-            grid=(rows_total,),
-            in_specs=[line_block] * len(sources),
-            out_specs=[vmem, phase_row],
+    filled = ()
+    for begin, end in ((0, 1), (1, wide)):
+        if begin == end:
+            continue
+        lines = sources[begin * high : end * high]
+        filled, lines = lax.optimization_barrier((filled, lines))
+        lines += [swapped(values, "core", 1) for values in lines]
+        operands = [in_vmem(values) for values in (*lines, *filled)]
+        first_filled = 1 + len(lines)
+        filled = pl.pallas_call(
+            functools.partial(scatter_kernel, third_live, wide, high, begin, end),
+            grid=(deep * (end - begin),),
+            in_specs=[smem] + [vmem] * len(operands),
+            out_specs=[vmem] * 2,
+            out_shape=[
+                pltpu.VMEM((2, parts, G, HALF), f32),
+                pltpu.VMEM((devices, SIDE + 1, 2 * bins, clusters), f32),
+            ],
             scratch_shapes=[
                 pltpu.VMEM((cols_total, HEIGHT, clusters), f32),
                 pltpu.VMEM((cols_total, FINE * span // HALF, slab // FINE * 2 * parts, HALF), f32),
             ],
-        ),
-        out_shape=[
-            pltpu.VMEM((2, parts, G, HALF), f32),
-            jax.ShapeDtypeStruct((devices, SIDE + 1, 2 * bins, clusters), f32),
-        ],
-        compiler_params=pltpu.CompilerParams(vmem_limit_bytes=24 << 20),
-        name="scatter",
-    )(where, *sources)
+            input_output_aliases={first_filled + i: i for i in range(len(filled))},
+            compiler_params=pltpu.CompilerParams(vmem_limit_bytes=24 << 20),
+            name="scatter",
+        )(where, *operands)
+    field, phases = filled
 
     field = in_vmem(field.reshape(2, 3, bins, 2, G, HALF))
     field = pl.pallas_call(

time: 101 us -> 98 us (0.970)
  local copies, waits for them, and re-layouts: 8.21 us -> 2.85 us
  Pallas kernels: 46 us -> 48.7 us
  waiting for transfers between devices: 21.4 us -> 19.7 us
  starting transfers between devices: 19.4 us -> 20.5 us
    unnamed x20 -> x16, local copies, waits for them, and re-layouts: 6.58 us -> 1.22 us
    ppermute x17, waiting for transfers between devices: 15.5 us -> 12.7 us  [swapped(): return lax.ppermute(values, axes, [(i, i ^ offset) for i in range(count)])]
    pallas_call x1, Pallas kernels: 3.48 us -> 5.23 us  [per_device(): pl.pallas_call(spread_kernel, out_shape=jax.ShapeDtypeStruct((HEIGHT, clu...]
    ppermute x17, starting transfers between devices: 17.3 us -> 18.5 us  [swapped(): return lax.ppermute(values, axes, [(i, i ^ offset) for i in range(count)])]
    pallas_call x1 -> x2, Pallas kernels: 14.4 us -> 15.4 us  [per_device(): pl.pallas_call(functools.partial(scatter_kernel, third_live, wide, high,...]
  transfers between devices with their start and end apart: 19 -> 19, of which waited for: 12 -> 8; matrix products, arithmetic and copies ran while one was open for 5% -> 4% of each run, Pallas kernels for 0% -> 8%
where the time goes in v7:
time: 98 us; the launch traced here: 97.7 us
  Pallas kernels  48.7 us (50%)
  starting transfers between devices  20.5 us (21%)
  waiting for transfers between devices  19.7 us (20%)
  other arithmetic  4.49 us (5%)
  local copies, waits for them, and re-layouts  2.85 us (3%)
    ppermute x17, starting transfers between devices, swapped(): return lax.ppermute(values, axes, [(i, i ^ offset) for i in range(count)])  18.5 us
    pallas_call x2, Pallas kernels, per_device(): pl.pallas_call(functools.partial(scatter_kernel, third_live, wide, high,...  15.4 us
    pallas_call x1, Pallas kernels, per_device(): pl.pallas_call(functools.partial(dft_kernel, factor, third_live, pars), g...  13.8 us
    ppermute x17, waiting for transfers between devices, swapped(): return lax.ppermute(values, axes, [(i, i ^ offset) for i in range(count)])  12.7 us
    pallas_call x1, Pallas kernels, per_device(): pl.pallas_call(gather_kernel, grid_spec=pltpu.PrefetchScalarGridSpec(num_...  11.2 us
    ppermute x2, waiting for transfers between devices, row_shift(): lax.ppermute(values, ROW, [(i, (i + by) % count) for i in range(count)])  6.96 us
    pallas_call x1, Pallas kernels, per_device(): pl.pallas_call(spread_kernel, out_shape=jax.ShapeDtypeStruct((HEIGHT, clu...  5.23 us
    pallas_call x1, Pallas kernels, per_device(): pl.pallas_call(final_kernel, in_specs=[smem] + [vmem] * (2 + deep), out_s...  3.05 us
  transfers between devices with their start and end apart: 19, of which 8 were waited for; matrix products, arithmetic and copies ran while one was open for 4% of the time, Pallas kernels for 8%

profile of v7, /device:TPU:0, one launch (start us, length us, event | category | flops | bytes accessed | tf_op | source)
XLA Modules:
  0.0 97.7 jit_solution(18305202221649299278)
XLA Ops:
  0.0 0.0 copy-start
  0.0 0.0 copy-start.7
  0.0 5.2 %spread.1 = f32[88,128]{1,0:T(8,128)} custom-call(f32[3,16384]{1,0:T(4,128)} %density.1, f32[27,16384]{1,0:T(8,128)} %weights.2, s32[3,128]{1,0:T(4,128)} %corners.1), custom_call_target="tpu_custom_call" | custom-call | tf_op jit(solution)/shard_map/spread/pallas_call | solution.py:439
  5.2 3.1 %collective-permute-start.2 = (f32[88,128]{1,0:T(8,128)}, f32[88,128]{1,0:T(8,128)S(1)}, u32[]{:S(2)}, u32[]{:S(2)}) collective-permute-start(f32[88,128]{1,0:T(8,128)} %spread.1), channel_id=1, source_target_pairs={{0,8},{8,0},{16,24},{24,16},{1,9},{9,1},{17,25},{25,17},{2,10},{10... | collective-permute-start | bytes 135176 | tf_op jit(solution)/shard_map/ppermute | solution.py:29
  8.3 2.6 %collective-permute-start.3 = (f32[88,128]{1,0:T(8,128)}, f32[88,128]{1,0:T(8,128)S(1)}, u32[]{:S(2)}, u32[]{:S(2)}) collective-permute-start(f32[88,128]{1,0:T(8,128)} %spread.1), channel_id=1, source_target_pairs={{0,16},{8,24},{16,0},{24,8},{1,17},{9,25},{17,1},{25,9},{2,18},{10... | collective-permute-start | bytes 135176 | tf_op jit(solution)/shard_map/ppermute | solution.py:29
  10.9 0.0 collective-permute-start.4
  10.9 0.0 collective-permute-done.2
  10.9 3.4 %collective-permute-done.3 = f32[88,128]{1,0:T(8,128)S(1)} collective-permute-done((f32[88,128]{1,0:T(8,128)}, f32[88,128]{1,0:T(8,128)S(1)}, u32[]{:S(2)}, u32[]{:S(2)}) %collective-permute-start.3) | collective-permute-done | bytes 45088 | tf_op jit(solution)/shard_map/ppermute | solution.py:29
  14.3 2.6 %collective-permute-done.4 = f32[88,128]{1,0:T(8,128)S(1)} collective-permute-done((f32[88,128]{1,0:T(8,128)}, f32[88,128]{1,0:T(8,128)S(1)}, u32[]{:S(2)}, u32[]{:S(2)}) %collective-permute-start.4) | collective-permute-done | bytes 45088 | tf_op jit(solution)/shard_map/ppermute | solution.py:29
  16.9 1.5 %pad_maximum_fusion.refs_0_ = f32[4,88,128]{2,1,0:T(8,128)} fusion(f32[1,88,128]{2,1,0:T(8,128)S(1)} %bitcast.61, f32[1,88,128]{2,1,0:T(8,128)S(1)} %bitcast.60, f32[1,88,128]{2,1,0:T(8,128)S(1)} %bitcast.59, f32[1,88,128]{2,1,0:T(8,128)} %bitcast.55), kind=kLoop, calls=%fused_computation.8 | loop fusion | flops 135168 | bytes 360448 | tf_op jit(solution)/shard_map/stack | solution.py:444
  18.4 1.5 %collective-permute-start.5 = (f32[4,88,128]{2,1,0:T(8,128)}, f32[4,88,128]{2,1,0:T(8,128)}, u32[]{:S(2)}, u32[]{:S(2)}) collective-permute-start(f32[4,88,128]{2,1,0:T(8,128)} %pad_maximum_fusion.refs_0_), channel_id=1, source_target_pairs={{0,2},{2,0},{4,6},{6,4},{1,3},{3,1},{5,7},{7,5},{8,10},{10,8},{12,... | collective-permute-start | bytes 540680 | tf_op jit(solution)/shard_map/ppermute | solution.py:29
  20.6 0.1 stack.51.where
  20.7 1.5 %collective-permute-start.8 = (f32[4,88,128]{2,1,0:T(8,128)}, f32[4,88,128]{2,1,0:T(8,128)S(1)}, u32[]{:S(2)}, u32[]{:S(2)}) collective-permute-start(f32[4,88,128]{2,1,0:T(8,128)} %pad_maximum_fusion.refs_0_), channel_id=1, source_target_pairs={{0,4},{2,6},{4,0},{6,2},{1,5},{3,7},{5,1},{7,3},{8,12},{10,14},{12... | collective-permute-start | bytes 540680 | tf_op jit(solution)/shard_map/ppermute | solution.py:29
  22.2 0.5 collective-permute-start.9
  22.6 3.0 %collective-permute-done.5.refs_1_ = f32[4,88,128]{2,1,0:T(8,128)} collective-permute-done((f32[4,88,128]{2,1,0:T(8,128)}, f32[4,88,128]{2,1,0:T(8,128)}, u32[]{:S(2)}, u32[]{:S(2)}) %collective-permute-start.5) | collective-permute-done | bytes 180256 | tf_op jit(solution)/shard_map/ppermute | solution.py:29
  25.7 0.0 collective-permute-start.6
  25.7 0.5 collective-permute-start.7
  26.2 1.7 %convert_bitcast_fusion = bf16[3,128,128]{2,0,1:T(4,128)(2,1)} fusion(f32[3,16384]{1,0:T(4,128)} %density.1), kind=kLoop, calls=%fused_computation.9 | loop fusion | flops 49152 | bytes 294912 | tf_op jit(solution)/shard_map/convert_element_type | solution.py:43
  27.8 0.0 collective-permute-done.6.refs_2_
  27.8 0.0 collective-permute-done.7.refs_3_
  27.8 8.0 %scatter.2 = (f32[2,24,256,128]{3,2,1,0:T(8,128)S(1)}, f32[32,4,8,128]{3,2,1,0:T(8,128)S(1)}) custom-call(s32[6]{0:T(128)S(1)} %stack.51.where, f32[4,88,128]{2,1,0:T(8,128)} %pad_maximum_fusion.refs_0_, f32[4,88,128]{2,1,0:T(8,128)} %collective-permute-done.5.refs_1_, f32[4,88,128]{2,1,0:T(8,128)S(1)} %collective-permute-done.6.refs_2_, ...), custom_call_target="tpu_custom_call" | custom-call | tf_op jit(solution)/shard_map/scatter/pallas_call | solution.py:476
  35.8 0.0 collective-permute-done.8.refs_0_
  35.8 0.0 collective-permute-done.9.refs_1_
  35.8 0.1 collective-permute-start.10
  35.9 0.5 collective-permute-start.11
  36.4 0.0 copy-done.7
  36.4 0.0 copy-start.4
  36.4 0.9 collective-permute-done.10.refs_2_
  37.3 0.3 collective-permute-done.11.refs_3_
  37.6 7.4 %scatter.3 = (f32[2,24,256,128]{3,2,1,0:T(8,128)S(1)}, f32[32,4,8,128]{3,2,1,0:T(8,128)S(1)}) custom-call(s32[6]{0:T(128)S(1)} %stack.51.where, f32[4,88,128]{2,1,0:T(8,128)S(1)} %collective-permute-done.8.refs_0_, f32[4,88,128]{2,1,0:T(8,128)S(1)} %collective-permute-done.9.refs_1_, ...), custom_call_target="tpu_custom_call", output_to_operand_aliasing={{0}: (5, {}), {1}: (6, {})} | custom-call | tf_op jit(solution)/shard_map/scatter/pallas_call | solution.py:476
  45.0 0.0 copy-done.4
  45.1 0.0 copy-done.5
  45.1 13.8 %spectral.1 = f32[2,3,4,2,256,128]{5,4,3,2,1,0:T(8,128)S(1)} custom-call(s32[6]{0:T(128)S(1)} %stack.51.where, f32[2,3,4,2,256,128]{5,4,3,2,1,0:T(8,128)S(1)} %bitcast.52, bf16[2,2,256,256]{3,2,1,0:T(8,128)(2,1)S(1)} %copy-done.4, bf16[2,2,256,256]{3,2,1,0:T(8,128)(2,1)S(1)} %copy-done.5), custom_call_target="tpu_custom_call" | custom-call | tf_op jit(solution)/shard_map/spectral/pallas_call | solution.py:496
  58.9 11.2 %gather.7 = (f32[2,2,4,88,128]{4,3,2,1,0:T(8,128)S(1)}, f32[2,2,4,88,128]{4,3,2,1,0:T(8,128)}) custom-call(s32[6]{0:T(128)S(1)} %stack.51.where, f32[32,4,8,128]{3,2,1,0:T(8,128)S(1)} %get-tuple-element.29.phases, f32[2,24,256,128]{3,2,1,0:T(8,128)S(1)} %bitcast.51), custom_call_target="tpu_custom_call" | custom-call | tf_op jit(solution)/shard_map/gather/pallas_call | solution.py:514
  70.1 0.9 copy-done.2
  71.0 0.2 collective-permute-start.12
  71.2 1.5 %gather_fusion = bf16[12,3,128]{2,1,0:T(4,128)(2,1)S(1)} fusion(bf16[3,128,128]{2,0,1:T(4,128)(2,1)} %convert_bitcast_fusion, s32[1024]{0:T(1024)S(1)} %pad_clamp_fusion), kind=kCustom, calls=%fused_computation | custom fusion | bytes 18480 | tf_op jit(solution)/shard_map/gather | solution.py:46
  72.7 0.0 copy-done
  72.7 0.0 copy-start.1
  72.7 0.0 copy-start.6
  72.8 0.6 fusion
  73.4 0.1 bitcast_select_fusion
  73.5 0.0 collective-permute-done.12
  73.5 0.3 copy-done.3
  73.8 1.2 %add.31 = f32[2,2,4,88,128]{4,3,2,1,0:T(8,128)S(1)} add(f32[2,2,4,88,128]{4,3,2,1,0:T(8,128)S(1)} %copy-done.3, f32[2,2,4,88,128]{4,3,2,1,0:T(8,128)} %collective-permute-done.12) | non-fusion elementwise | flops 180224 | bytes 2162688 | tf_op jit(solution)/shard_map/add | solution.py:531
  75.1 1.9 %collective-permute-start.13 = (f32[4,88,128]{2,1,0:T(8,128)S(1)}, f32[4,88,128]{2,1,0:T(8,128)S(1)}, u32[]{:S(2)}, u32[]{:S(2)}) collective-permute-start(f32[4,88,128]{2,1,0:T(8,128)S(1)} %get-tuple-element.37), channel_id=1, source_target_pairs={{0,2},{2,0},{4,6},{6,4},{1,3},{3,1},{5,7},{7,5},{8,10},{10,8},{12,... | collective-permute-start | bytes 540680 | tf_op jit(solution)/shard_map/ppermute | solution.py:29
  77.0 1.5 %collective-permute-start.14 = (f32[4,88,128]{2,1,0:T(8,128)S(1)}, f32[4,88,128]{2,1,0:T(8,128)S(1)}, u32[]{:S(2)}, u32[]{:S(2)}) collective-permute-start(f32[4,88,128]{2,1,0:T(8,128)S(1)} %get-tuple-element.35), channel_id=1, source_target_pairs={{0,4},{2,6},{4,0},{6,2},{1,5},{3,7},{5,1},{7,3},{8,12},{10,14},{12... | collective-permute-start | bytes 540680 | tf_op jit(solution)/shard_map/ppermute | solution.py:29
  78.5 0.1 collective-permute-start.15
  78.6 1.5 %collective-permute-start = (f32[4,3,128]{2,1,0:T(4,128)S(1)}, f32[4,3,128]{2,1,0:T(4,128)S(1)}, u32[]{:S(2)}, u32[]{:S(2)}) collective-permute-start(f32[4,3,128]{2,1,0:T(4,128)S(1)} %get-tuple-element.42), channel_id=1, source_target_pairs={{0,28},{4,0},{8,4},{12,8},{16,12},{20,16},{24,20},{28,24},{1,29},{... | collective-permute-start | bytes 18440 | tf_op jit(solution)/shard_map/ppermute | solution.py:38
  80.1 0.6 collective-permute-start.1
  80.7 7.0 %collective-permute-done = f32[4,3,128]{2,1,0:T(4,128)S(1)} collective-permute-done((f32[4,3,128]{2,1,0:T(4,128)S(1)}, f32[4,3,128]{2,1,0:T(4,128)S(1)}, u32[]{:S(2)}, u32[]{:S(2)}) %collective-permute-start) | collective-permute-done | bytes 6176 | tf_op jit(solution)/shard_map/ppermute | solution.py:38
  87.6 0.0 collective-permute-done.1
  87.6 0.0 collective-permute-done.13
  87.6 0.0 collective-permute-done.14
  87.6 0.0 collective-permute-done.15
  87.7 0.1 collective-permute-start.16
  87.8 0.8 collective-permute-start.17
  88.6 3.6 %collective-permute-start.18 = (f32[88,128]{1,0:T(8,128)S(1)}, f32[88,128]{1,0:T(8,128)S(1)}, u32[]{:S(2)}, u32[]{:S(2)}) collective-permute-start(f32[88,128]{1,0:T(8,128)S(1)} %get-tuple-element.38), channel_id=1, source_target_pairs={{0,24},{8,16},{16,8},{24,0},{1,25},{9,17},{17,9},{25,1},{2,26},{10... | collective-permute-start | bytes 135176 | tf_op jit(solution)/shard_map/ppermute | solution.py:29
  92.2 0.0 collective-permute-done.16.refs_1_
  92.2 0.8 collective-permute-done.17.refs_2_
  93.0 1.7 %collective-permute-done.18.refs_3_ = f32[88,128]{1,0:T(8,128)S(1)} collective-permute-done((f32[88,128]{1,0:T(8,128)S(1)}, f32[88,128]{1,0:T(8,128)S(1)}, u32[]{:S(2)}, u32[]{:S(2)}) %collective-permute-start.18) | collective-permute-done | bytes 45088 | tf_op jit(solution)/shard_map/ppermute | solution.py:29
  94.7 0.0 copy-done.1
  94.7 0.0 copy-done.6
  94.7 3.1 %final.1 = f32[3,16384]{1,0:T(4,128)} custom-call(s32[12]{0:T(128)S(1)} %copy-done.6, f32[12,3,128]{2,1,0:T(4,128)S(1)} %pad_maximum_fusion.1.near, f32[27,16384]{1,0:T(8,128)S(1)} %copy-done.1, f32[88,128]{1,0:T(8,128)S(1)} %get-tuple-element.41.refs_0_, f32[88,128]{1,0:T(8,128)S(1)} %collective-permute-done.16.refs_1_, ...), custom_call_target="tpu_custom_call" | custom-call | tf_op jit(solution)/shard_map/final/pallas_call | solution.py:538
  (14 shorter events, 0.1 us)
Async XLA Ops:
  0.0 72.7 %copy-start = (bf16[12,3,3,128,128]{4,3,2,1,0:T(8,128)(2,1)S(1)}, bf16[12,3,3,128,128]{4,3,2,1,0:T(8,128)(2,1)}, u32[]{:S(2)}) copy-start(bf16[12,3,3,128,128]{4,3,2,1,0:T(8,128)(2,1)} %param.14) | copy-start | bytes 10616836
  0.0 36.4 %copy-start.7 = (s32[12]{0:T(128)S(1)}, s32[12]{0:T(128)}, u32[]{:S(2)}) copy-start(s32[12]{0:T(128)} %param.15) | copy-start | bytes 148
  5.2 5.6 %collective-permute-start.2 = (f32[88,128]{1,0:T(8,128)}, f32[88,128]{1,0:T(8,128)S(1)}, u32[]{:S(2)}, u32[]{:S(2)}) collective-permute-start(f32[88,128]{1,0:T(8,128)} %spread.1), channel_id=1, source_target_pairs={{0,8},{8,0},{16,24},{24,16},{1,9},{9,1},{17,25},{25,17},{2,10},{10... | collective-permute-start | bytes 135176 | tf_op jit(solution)/shard_map/ppermute | solution.py:29
  8.3 6.0 %collective-permute-start.3 = (f32[88,128]{1,0:T(8,128)}, f32[88,128]{1,0:T(8,128)S(1)}, u32[]{:S(2)}, u32[]{:S(2)}) collective-permute-start(f32[88,128]{1,0:T(8,128)} %spread.1), channel_id=1, source_target_pairs={{0,16},{8,24},{16,0},{24,8},{1,17},{9,25},{17,1},{25,9},{2,18},{10... | collective-permute-start | bytes 135176 | tf_op jit(solution)/shard_map/ppermute | solution.py:29
  10.9 6.1 %collective-permute-start.4 = (f32[88,128]{1,0:T(8,128)}, f32[88,128]{1,0:T(8,128)S(1)}, u32[]{:S(2)}, u32[]{:S(2)}) collective-permute-start(f32[88,128]{1,0:T(8,128)} %spread.1), channel_id=1, source_target_pairs={{0,24},{8,16},{16,8},{24,0},{1,25},{9,17},{17,9},{25,1},{2,26},{10... | collective-permute-start | bytes 135176 | tf_op jit(solution)/shard_map/ppermute | solution.py:29
  18.4 7.2 %collective-permute-start.5 = (f32[4,88,128]{2,1,0:T(8,128)}, f32[4,88,128]{2,1,0:T(8,128)}, u32[]{:S(2)}, u32[]{:S(2)}) collective-permute-start(f32[4,88,128]{2,1,0:T(8,128)} %pad_maximum_fusion.refs_0_), channel_id=1, source_target_pairs={{0,2},{2,0},{4,6},{6,4},{1,3},{3,1},{5,7},{7,5},{8,10},{10,8},{12,... | collective-permute-start | bytes 540680 | tf_op jit(solution)/shard_map/ppermute | solution.py:29
  20.7 15.2 %collective-permute-start.8 = (f32[4,88,128]{2,1,0:T(8,128)}, f32[4,88,128]{2,1,0:T(8,128)S(1)}, u32[]{:S(2)}, u32[]{:S(2)}) collective-permute-start(f32[4,88,128]{2,1,0:T(8,128)} %pad_maximum_fusion.refs_0_), channel_id=1, source_target_pairs={{0,4},{2,6},{4,0},{6,2},{1,5},{3,7},{5,1},{7,3},{8,12},{10,14},{12... | collective-permute-start | bytes 540680 | tf_op jit(solution)/shard_map/ppermute | solution.py:29
  22.2 13.7 %collective-permute-start.9 = (f32[4,88,128]{2,1,0:T(8,128)}, f32[4,88,128]{2,1,0:T(8,128)S(1)}, u32[]{:S(2)}, u32[]{:S(2)}) collective-permute-start(f32[4,88,128]{2,1,0:T(8,128)} %pad_maximum_fusion.refs_0_), channel_id=1, source_target_pairs={{0,6},{2,4},{4,2},{6,0},{1,7},{3,5},{5,3},{7,1},{8,14},{10,12},{12... | collective-permute-start | bytes 540680 | tf_op jit(solution)/shard_map/ppermute | solution.py:29
  25.7 2.2 %collective-permute-start.6 = (f32[4,88,128]{2,1,0:T(8,128)}, f32[4,88,128]{2,1,0:T(8,128)S(1)}, u32[]{:S(2)}, u32[]{:S(2)}) collective-permute-start(f32[4,88,128]{2,1,0:T(8,128)} %pad_maximum_fusion.refs_0_), channel_id=1, source_target_pairs={{0,1},{1,0},{2,3},{3,2},{4,5},{5,4},{6,7},{7,6},{8,9},{9,8},{10,11... | collective-permute-start | bytes 540680 | tf_op jit(solution)/shard_map/ppermute | solution.py:29
  25.7 2.2 %collective-permute-start.7 = (f32[4,88,128]{2,1,0:T(8,128)}, f32[4,88,128]{2,1,0:T(8,128)S(1)}, u32[]{:S(2)}, u32[]{:S(2)}) collective-permute-start(f32[4,88,128]{2,1,0:T(8,128)} %collective-permute-done.5.refs_1_), channel_id=1, source_target_pairs={{0,1},{1,0},{2,3},{3,2},{4,5},{5,4},{6,7},{7,6},{8,9},{9,8},{10,11... | collective-permute-start | bytes 540680 | tf_op jit(solution)/shard_map/ppermute | solution.py:29
  35.8 1.5 %collective-permute-start.10 = (f32[4,88,128]{2,1,0:T(8,128)S(1)}, f32[4,88,128]{2,1,0:T(8,128)S(1)}, u32[]{:S(2)}, u32[]{:S(2)}) collective-permute-start(f32[4,88,128]{2,1,0:T(8,128)S(1)} %collective-permute-done.8.refs_0_), channel_id=1, source_target_pairs={{0,1},{1,0},{2,3},{3,2},{4,5},{5,4},{6,7},{7,6},{8,9},{9,8},{10,11... | collective-permute-start | bytes 540680 | tf_op jit(solution)/shard_map/ppermute | solution.py:29
  35.9 1.7 %collective-permute-start.11 = (f32[4,88,128]{2,1,0:T(8,128)S(1)}, f32[4,88,128]{2,1,0:T(8,128)S(1)}, u32[]{:S(2)}, u32[]{:S(2)}) collective-permute-start(f32[4,88,128]{2,1,0:T(8,128)S(1)} %collective-permute-done.9.refs_1_), channel_id=1, source_target_pairs={{0,1},{1,0},{2,3},{3,2},{4,5},{5,4},{6,7},{7,6},{8,9},{9,8},{10,11... | collective-permute-start | bytes 540680 | tf_op jit(solution)/shard_map/ppermute | solution.py:29
  36.4 8.6 %copy-start.4 = (bf16[2,2,256,256]{3,2,1,0:T(8,128)(2,1)S(1)}, bf16[2,2,256,256]{3,2,1,0:T(8,128)(2,1)}, u32[]{:S(2)}) copy-start(bf16[2,2,256,256]{3,2,1,0:T(8,128)(2,1)} %constant.52.clone.refs_0_) | copy-start | bytes 1572868
  36.4 8.6 %copy-start.5 = (bf16[2,2,256,256]{3,2,1,0:T(8,128)(2,1)S(1)}, bf16[2,2,256,256]{3,2,1,0:T(8,128)(2,1)}, u32[]{:S(2)}) copy-start(bf16[2,2,256,256]{3,2,1,0:T(8,128)(2,1)} %constant.53.clone.refs_1_) | copy-start | bytes 1572868
  70.1 0.9 copy-start.2
  71.0 2.5 %collective-permute-start.12 = (f32[2,2,4,88,128]{4,3,2,1,0:T(8,128)}, f32[2,2,4,88,128]{4,3,2,1,0:T(8,128)}, u32[]{:S(2)}, u32[]{:S(2)}) collective-permute-start(f32[2,2,4,88,128]{4,3,2,1,0:T(8,128)} %get-tuple-element.34), channel_id=1, source_target_pairs={{0,1},{1,0},{2,3},{3,2},{4,5},{5,4},{6,7},{7,6},{8,9},{9,8},{10,11... | collective-permute-start | bytes 2162696 | tf_op jit(solution)/shard_map/ppermute | solution.py:29
  72.7 1.1 %copy-start.3 = (f32[2,2,4,88,128]{4,3,2,1,0:T(8,128)S(1)}, f32[2,2,4,88,128]{4,3,2,1,0:T(8,128)}, u32[]{:S(2)}) copy-start(f32[2,2,4,88,128]{4,3,2,1,0:T(8,128)} %copy-done.2) | copy-start | bytes 2162692
  72.7 22.0 %copy-start.1 = (f32[27,16384]{1,0:T(8,128)S(1)}, f32[27,16384]{1,0:T(8,128)}, u32[]{:S(2)}) copy-start(f32[27,16384]{1,0:T(8,128)} %weights.3) | copy-start | bytes 5308420
  72.7 21.9 %copy-start.6 = (s32[12]{0:T(128)S(1)}, s32[12]{0:T(128)}, u32[]{:S(2)}) copy-start(s32[12]{0:T(128)} %landing.1) | copy-start | bytes 148
  75.1 12.6 %collective-permute-start.13 = (f32[4,88,128]{2,1,0:T(8,128)S(1)}, f32[4,88,128]{2,1,0:T(8,128)S(1)}, u32[]{:S(2)}, u32[]{:S(2)}) collective-permute-start(f32[4,88,128]{2,1,0:T(8,128)S(1)} %get-tuple-element.37), channel_id=1, source_target_pairs={{0,2},{2,0},{4,6},{6,4},{1,3},{3,1},{5,7},{7,5},{8,10},{10,8},{12,... | collective-permute-start | bytes 540680 | tf_op jit(solution)/shard_map/ppermute | solution.py:29
  77.0 10.6 %collective-permute-start.14 = (f32[4,88,128]{2,1,0:T(8,128)S(1)}, f32[4,88,128]{2,1,0:T(8,128)S(1)}, u32[]{:S(2)}, u32[]{:S(2)}) collective-permute-start(f32[4,88,128]{2,1,0:T(8,128)S(1)} %get-tuple-element.35), channel_id=1, source_target_pairs={{0,4},{2,6},{4,0},{6,2},{1,5},{3,7},{5,1},{7,3},{8,12},{10,14},{12... | collective-permute-start | bytes 540680 | tf_op jit(solution)/shard_map/ppermute | solution.py:29
  78.5 9.1 %collective-permute-start.15 = (f32[4,88,128]{2,1,0:T(8,128)S(1)}, f32[4,88,128]{2,1,0:T(8,128)S(1)}, u32[]{:S(2)}, u32[]{:S(2)}) collective-permute-start(f32[4,88,128]{2,1,0:T(8,128)S(1)} %get-tuple-element.36), channel_id=1, source_target_pairs={{0,6},{2,4},{4,2},{6,0},{1,7},{3,5},{5,3},{7,1},{8,14},{10,12},{12... | collective-permute-start | bytes 540680 | tf_op jit(solution)/shard_map/ppermute | solution.py:29
  78.6 9.0 %collective-permute-start = (f32[4,3,128]{2,1,0:T(4,128)S(1)}, f32[4,3,128]{2,1,0:T(4,128)S(1)}, u32[]{:S(2)}, u32[]{:S(2)}) collective-permute-start(f32[4,3,128]{2,1,0:T(4,128)S(1)} %get-tuple-element.42), channel_id=1, source_target_pairs={{0,28},{4,0},{8,4},{12,8},{16,12},{20,16},{24,20},{28,24},{1,29},{... | collective-permute-start | bytes 18440 | tf_op jit(solution)/shard_map/ppermute | solution.py:38
  80.1 7.5 %collective-permute-start.1 = (f32[4,3,128]{2,1,0:T(4,128)S(1)}, f32[4,3,128]{2,1,0:T(4,128)S(1)}, u32[]{:S(2)}, u32[]{:S(2)}) collective-permute-start(f32[4,3,128]{2,1,0:T(4,128)S(1)} %get-tuple-element.43), channel_id=1, source_target_pairs={{0,4},{4,8},{8,12},{12,16},{16,20},{20,24},{24,28},{28,0},{1,5},{5... | collective-permute-start | bytes 18440 | tf_op jit(solution)/shard_map/ppermute | solution.py:38
  87.7 4.5 %collective-permute-start.16 = (f32[88,128]{1,0:T(8,128)S(1)}, f32[88,128]{1,0:T(8,128)S(1)}, u32[]{:S(2)}, u32[]{:S(2)}) collective-permute-start(f32[88,128]{1,0:T(8,128)S(1)} %get-tuple-element.40), channel_id=1, source_target_pairs={{0,8},{8,0},{16,24},{24,16},{1,9},{9,1},{17,25},{25,17},{2,10},{10... | collective-permute-start | bytes 135176 | tf_op jit(solution)/shard_map/ppermute | solution.py:29
  87.8 5.2 %collective-permute-start.17 = (f32[88,128]{1,0:T(8,128)S(1)}, f32[88,128]{1,0:T(8,128)S(1)}, u32[]{:S(2)}, u32[]{:S(2)}) collective-permute-start(f32[88,128]{1,0:T(8,128)S(1)} %get-tuple-element.39), channel_id=1, source_target_pairs={{0,16},{8,24},{16,0},{24,8},{1,17},{9,25},{17,1},{25,9},{2,18},{10... | collective-permute-start | bytes 135176 | tf_op jit(solution)/shard_map/ppermute | solution.py:29
  88.6 6.1 %collective-permute-start.18 = (f32[88,128]{1,0:T(8,128)S(1)}, f32[88,128]{1,0:T(8,128)S(1)}, u32[]{:S(2)}, u32[]{:S(2)}) collective-permute-start(f32[88,128]{1,0:T(8,128)S(1)} %get-tuple-element.38), channel_id=1, source_target_pairs={{0,24},{8,16},{16,8},{24,0},{1,25},{9,17},{17,9},{25,1},{2,26},{10... | collective-permute-start | bytes 135176 | tf_op jit(solution)/shard_map/ppermute | solution.py:29

commit v8 on v7

--- a/solution.py
+++ b/solution.py
@@ -39,10 +39,8 @@
 
 
 def near_field(charges, near_tiles, pair_target, pair_count):
-    panels = charges.shape[2]
     rounded = charges.astype(jnp.bfloat16)
     slot_total = pair_target.shape[0]
-    slot_group = slot_total // 3
     picked = rounded[:, pair_target, :]
     partial_value = jnp.einsum(
         "qabij,aqi->qbj", near_tiles, picked, preferred_element_type=jnp.float32
@@ -51,6 +49,11 @@
     partial_value = jnp.where(
         live_mask[:, None, None], partial_value, jnp.zeros_like(partial_value)
     )
+    return partial_value
+
+
+def near_exchange(partial_value):
+    slot_group, panels = partial_value.shape[0] // 3, partial_value.shape[2]
     leaving = partial_value[slot_group:].reshape(slot_group, 2, 3, panels)
     crossing = jnp.stack([row_shift(leaving[:, 0], -1), row_shift(leaving[:, 1], 1)], axis=1)
     return jnp.concatenate(
@@ -450,7 +453,10 @@
     if pars == 1:
         tables += [lax.dynamic_slice_in_dim(t, first_parity, 1, axis=0) for t in tables]
     tables = [in_vmem(table) for table in tables]
-    line, *tables = lax.optimization_barrier((line, *tables))
+    near = near_field(
+        density.reshape(3, clusters, panels), near_tiles, pair_target, pair_count
+    )
+    line, near, *tables = lax.optimization_barrier((line, near, *tables))
     sources = [line] + [swapped(line, PLANE, o) for o in range(1, wide * high)]
 
     factor = 1.0 / math.sqrt(density.shape[1] * devices)
@@ -465,11 +471,11 @@
     vmem = pl.BlockSpec(memory_space=pltpu.VMEM)
     span = G // cols_total
     filled = ()
-    for begin, end in ((0, 1), (1, wide)):
-        if begin == end:
-            continue
+    for begin, end in ((0, 1), (1, wide))[: min(2, wide)]:
         lines = sources[begin * high : end * high]
-        filled, lines = lax.optimization_barrier((filled, lines))
+        if begin:
+            filled, lines, near = lax.optimization_barrier((filled, lines, near))
+            near = near_exchange(near)
         lines += [swapped(values, "core", 1) for values in lines]
         operands = [in_vmem(values) for values in (*lines, *filled)]
         first_filled = 1 + len(lines)
@@ -490,6 +496,8 @@
             compiler_params=pltpu.CompilerParams(vmem_limit_bytes=24 << 20),
             name="scatter",
         )(where, *operands)
+    if wide == 1:
+        near = near_exchange(near)
     field, phases = filled
 
     field = in_vmem(field.reshape(2, 3, bins, 2, G, HALF))
@@ -506,6 +514,7 @@
         compiler_params=pltpu.CompilerParams(vmem_limit_bytes=24 << 20),
         name="spectral",
     )(where, field, *tables)
+    field, near = lax.optimization_barrier((field, near))
 
     sample_block = pl.BlockSpec(
         (1, high, 1, HEIGHT, clusters),
@@ -532,9 +541,6 @@
     line = sampled[0] + sum(swapped(sampled[o], PLANE, o) for o in range(1, wide * high))
     samples = [line[0]] + [swapped(line[o], "z", o) for o in range(1, deep)]
     samples = [in_vmem(sample) for sample in samples]
-    near = near_field(
-        density.reshape(3, clusters, panels), near_tiles, pair_target, pair_count
-    )
     return pl.pallas_call(
         final_kernel,
         in_specs=[smem] + [vmem] * (2 + deep),

time: 98 us -> 106 us (1.082)
  waiting for transfers between devices: 19.7 us -> 22.9 us
  starting transfers between devices: 20.5 us -> 23.4 us
    ppermute x17, waiting for transfers between devices: 12.7 us -> 17.7 us  [swapped(): return lax.ppermute(values, axes, [(i, i ^ offset) for i in range(count)])]
    ppermute x2, starting transfers between devices: 2.03 us -> 4.51 us  [row_shift(): lax.ppermute(values, ROW, [(i, (i + by) % count) for i in range(count)])]
    ppermute x2, waiting for transfers between devices: 6.96 us -> 5.13 us  [row_shift(): lax.ppermute(values, ROW, [(i, (i + by) % count) for i in range(count)])]
    slice x2, local copies, waits for them, and re-layouts: 0.01 us -> 1.42 us  [the longest x1 0.72 us: near_exchange(): leaving = partial_value[slot_group:].reshape(slot_group, 2, 3, panels)]
    unnamed x16 -> x14, local copies, waits for them, and re-layouts: 1.22 us -> 0.04 us
    add x1, other arithmetic: 1.2 us -> 0.1 us  [per_device(): mine + swapped(other, 'core', 1)]
  transfers between devices with their start and end apart: 19 -> 19, of which waited for: 8 -> 10; matrix products, arithmetic and copies ran while one was open for 4% -> 6% of each run, Pallas kernels for 8% -> 8%
where the time goes in v8:
time: 106 us
  Pallas kernels  49.7 us (47%)
  starting transfers between devices  23.4 us (22%)
  waiting for transfers between devices  22.9 us (22%)
  other arithmetic  5.2 us (5%)
  local copies, waits for them, and re-layouts  3.08 us (3%)
    ppermute x17, starting transfers between devices, swapped(): return lax.ppermute(values, axes, [(i, i ^ offset) for i in range(count)])  18.9 us
    ppermute x17, waiting for transfers between devices, swapped(): return lax.ppermute(values, axes, [(i, i ^ offset) for i in range(count)])  17.7 us
    pallas_call x2, Pallas kernels, per_device(): pl.pallas_call(functools.partial(scatter_kernel, third_live, wide, high,...  16.2 us
    pallas_call x1, Pallas kernels, per_device(): pl.pallas_call(functools.partial(dft_kernel, factor, third_live, pars), g...  14.5 us
    pallas_call x1, Pallas kernels, per_device(): pl.pallas_call(gather_kernel, grid_spec=pltpu.PrefetchScalarGridSpec(num_...  10.7 us
    pallas_call x1, Pallas kernels, per_device(): pl.pallas_call(spread_kernel, out_shape=jax.ShapeDtypeStruct((HEIGHT, clu...  5.22 us
    ppermute x2, waiting for transfers between devices, row_shift(): lax.ppermute(values, ROW, [(i, (i + by) % count) for i in range(count)])  5.13 us
    ppermute x2, starting transfers between devices, row_shift(): lax.ppermute(values, ROW, [(i, (i + by) % count) for i in range(count)])  4.51 us
  transfers between devices with their start and end apart: 19, of which 10 were waited for; matrix products, arithmetic and copies ran while one was open for 6% of the time, Pallas kernels for 8%

profile of v8, /device:TPU:0, one launch (start us, length us, event | category | flops | bytes accessed | tf_op | source)
XLA Modules:
  0.0 105.8 jit_solution(10367419740156932133)
XLA Ops:
  0.0 0.0 copy-start
  0.0 5.2 %spread.1 = f32[88,128]{1,0:T(8,128)} custom-call(f32[3,16384]{1,0:T(4,128)} %density.1, f32[27,16384]{1,0:T(8,128)} %weights.2, s32[3,128]{1,0:T(4,128)} %corners.1), custom_call_target="tpu_custom_call" | custom-call | tf_op jit(solution)/shard_map/spread/pallas_call | solution.py:442
  5.2 5.1 %collective-permute-start.2 = (f32[88,128]{1,0:T(8,128)}, f32[88,128]{1,0:T(8,128)}, u32[]{:S(2)}, u32[]{:S(2)}) collective-permute-start(f32[88,128]{1,0:T(8,128)} %spread.1), channel_id=1, source_target_pairs={{0,24},{8,16},{16,8},{24,0},{1,25},{9,17},{17,9},{25,1},{2,26},{10... | collective-permute-start | bytes 135176 | tf_op jit(solution)/shard_map/ppermute | solution.py:29
  10.3 0.0 collective-permute-start.1
  10.3 0.6 collective-permute-start
  10.9 1.6 %convert_bitcast_fusion = bf16[3,128,128]{2,0,1:T(4,128)(2,1)} fusion(f32[3,16384]{1,0:T(4,128)} %density.1), kind=kLoop, calls=%fused_computation.9 | loop fusion | flops 49152 | bytes 294912 | tf_op jit(solution)/shard_map/convert_element_type | solution.py:42
  13.2 0.5 iota_compare_fusion
  13.7 0.7 compare_select_fusion
  14.4 1.5 %gather_fusion = bf16[12,3,128]{2,1,0:T(4,128)(2,1)S(1)} fusion(bf16[3,128,128]{2,0,1:T(4,128)(2,1)} %convert_bitcast_fusion, s32[1024]{0:T(1024)S(1)} %pad_clamp_fusion), kind=kCustom, calls=%fused_computation | custom fusion | bytes 18480 | tf_op jit(solution)/shard_map/gather | solution.py:44
  15.9 0.0 copy-start.5
  15.9 0.0 copy-done
  15.9 0.6 fusion
  16.5 0.7 bitcast_select_fusion
  17.2 0.0 collective-permute-done.2
  17.2 0.0 collective-permute-done.1
  17.2 0.0 collective-permute-done
  17.2 0.0 copy-done.5
  17.2 1.5 %pad_maximum_fusion.refs_0_ = f32[4,88,128]{2,1,0:T(8,128)} fusion(f32[1,88,128]{2,1,0:T(8,128)} %bitcast.8, f32[1,88,128]{2,1,0:T(8,128)} %bitcast.7, f32[1,88,128]{2,1,0:T(8,128)} %bitcast.6, f32[1,88,128]{2,1,0:T(8,128)S(1)} %bitcast.55), kind=kLoop, calls=%fused_computation.8 | loop fusion | flops 135168 | bytes 360448 | tf_op jit(solution)/shard_map/stack | solution.py:447
  18.7 1.7 %collective-permute-start.3 = (f32[4,88,128]{2,1,0:T(8,128)}, f32[4,88,128]{2,1,0:T(8,128)}, u32[]{:S(2)}, u32[]{:S(2)}) collective-permute-start(f32[4,88,128]{2,1,0:T(8,128)} %pad_maximum_fusion.refs_0_), channel_id=1, source_target_pairs={{0,2},{2,0},{4,6},{6,4},{1,3},{3,1},{5,7},{7,5},{8,10},{10,8},{12,... | collective-permute-start | bytes 540680 | tf_op jit(solution)/shard_map/ppermute | solution.py:29
  20.5 0.0 collective-permute-start.4
  20.5 4.3 %collective-permute-done.3.refs_1_ = f32[4,88,128]{2,1,0:T(8,128)} collective-permute-done((f32[4,88,128]{2,1,0:T(8,128)}, f32[4,88,128]{2,1,0:T(8,128)}, u32[]{:S(2)}, u32[]{:S(2)}) %collective-permute-start.3) | collective-permute-done | bytes 180256 | tf_op jit(solution)/shard_map/ppermute | solution.py:29
  24.8 0.0 collective-permute-start.5
  24.8 2.4 %collective-permute-start.7 = (f32[4,88,128]{2,1,0:T(8,128)}, f32[4,88,128]{2,1,0:T(8,128)}, u32[]{:S(2)}, u32[]{:S(2)}) collective-permute-start(f32[4,88,128]{2,1,0:T(8,128)} %pad_maximum_fusion.refs_0_), channel_id=1, source_target_pairs={{0,6},{2,4},{4,2},{6,0},{1,7},{3,5},{5,3},{7,1},{8,14},{10,12},{12... | collective-permute-start | bytes 540680 | tf_op jit(solution)/shard_map/ppermute | solution.py:29
  27.2 0.5 collective-permute-start.6
  27.8 0.1 stack.48.where
  27.9 0.0 collective-permute-done.4.refs_2_
  27.9 0.0 collective-permute-done.5.refs_3_
  27.9 8.1 %scatter.2 = (f32[2,24,256,128]{3,2,1,0:T(8,128)S(1)}, f32[32,4,8,128]{3,2,1,0:T(8,128)S(1)}) custom-call(s32[6]{0:T(128)S(1)} %stack.48.where, f32[4,88,128]{2,1,0:T(8,128)} %pad_maximum_fusion.refs_0_, f32[4,88,128]{2,1,0:T(8,128)} %collective-permute-done.3.refs_1_, f32[4,88,128]{2,1,0:T(8,128)} %collective-permute-done.4.refs_2_, ...), custom_call_target="tpu_custom_call" | custom-call | tf_op jit(solution)/shard_map/scatter/pallas_call | solution.py:482
  36.0 0.0 collective-permute-done.7.refs_1_
  36.0 0.9 collective-permute-done.6.refs_0_
  36.9 0.7 slice.37
  37.6 4.5 %collective-permute-start.10 = (f32[4,3,128]{2,1,0:T(4,128)S(1)}, f32[4,3,128]{2,1,0:T(4,128)S(1)}, u32[]{:S(2)}, u32[]{:S(2)}) collective-permute-start(f32[4,3,128]{2,1,0:T(4,128)S(1)} %get-tuple-element.46), channel_id=1, source_target_pairs={{0,28},{4,0},{8,4},{12,8},{16,12},{20,16},{24,20},{28,24},{1,29},{... | collective-permute-start | bytes 18440 | tf_op jit(solution)/shard_map/ppermute | solution.py:38
  42.1 0.0 collective-permute-start.11
  42.1 0.7 slice.36
  42.8 0.0 collective-permute-start.8
  42.8 0.5 collective-permute-start.9
  43.3 0.2 collective-permute-done.10
  43.5 5.0 %collective-permute-done.11 = f32[4,3,128]{2,1,0:T(4,128)S(1)} collective-permute-done((f32[4,3,128]{2,1,0:T(4,128)S(1)}, f32[4,3,128]{2,1,0:T(4,128)S(1)}, u32[]{:S(2)}, u32[]{:S(2)}) %collective-permute-start.11) | collective-permute-done | bytes 6176 | tf_op jit(solution)/shard_map/ppermute | solution.py:38
  48.5 0.0 copy-start.2
  48.5 0.0 copy-start.3
  48.5 0.0 collective-permute-done.8.refs_2_
  48.5 0.0 collective-permute-done.9.refs_3_
  48.5 8.1 %scatter.3 = (f32[2,24,256,128]{3,2,1,0:T(8,128)S(1)}, f32[32,4,8,128]{3,2,1,0:T(8,128)S(1)}) custom-call(s32[6]{0:T(128)S(1)} %stack.48.where, f32[4,88,128]{2,1,0:T(8,128)} %collective-permute-done.6.refs_0_, f32[4,88,128]{2,1,0:T(8,128)} %collective-permute-done.7.refs_1_, ...), custom_call_target="tpu_custom_call", output_to_operand_aliasing={{0}: (5, {}), {1}: (6, {})} | custom-call | tf_op jit(solution)/shard_map/scatter/pallas_call | solution.py:482
  56.6 14.5 %spectral.1 = f32[2,3,4,2,256,128]{5,4,3,2,1,0:T(8,128)S(1)} custom-call(s32[6]{0:T(128)S(1)} %stack.48.where, f32[2,3,4,2,256,128]{5,4,3,2,1,0:T(8,128)S(1)} %bitcast.52, bf16[2,2,256,256]{3,2,1,0:T(8,128)(2,1)S(1)} %copy-done.3, bf16[2,2,256,256]{3,2,1,0:T(8,128)(2,1)S(1)} %copy-done.2), custom_call_target="tpu_custom_call" | custom-call | tf_op jit(solution)/shard_map/spectral/pallas_call | solution.py:504
  71.2 10.7 %gather.7 = (f32[2,2,4,88,128]{4,3,2,1,0:T(8,128)S(1)}, f32[2,2,4,88,128]{4,3,2,1,0:T(8,128)S(1)}) custom-call(s32[6]{0:T(128)S(1)} %stack.48.where, f32[32,4,8,128]{3,2,1,0:T(8,128)S(1)} %get-tuple-element.35.phases, f32[2,24,256,128]{3,2,1,0:T(8,128)S(1)} %bitcast.51), custom_call_target="tpu_custom_call" | custom-call | tf_op jit(solution)/shard_map/gather/pallas_call | solution.py:523
  81.9 0.0 copy-start.1
  81.9 0.0 copy-start.4
  81.9 0.1 collective-permute-start.12
  82.0 2.2 %collective-permute-done.12 = f32[2,2,4,88,128]{4,3,2,1,0:T(8,128)S(1)} collective-permute-done((f32[2,2,4,88,128]{4,3,2,1,0:T(8,128)S(1)}, f32[2,2,4,88,128]{4,3,2,1,0:T(8,128)S(1)}, u32[]{:S(2)}, u32[]{:S(2)}) %collective-permute-start.12) | collective-permute-done | bytes 720928 | tf_op jit(solution)/shard_map/ppermute | solution.py:29
  84.1 0.1 add.31
  84.3 0.1 collective-permute-start.14
  84.4 1.9 %collective-permute-start.15 = (f32[4,88,128]{2,1,0:T(8,128)S(1)}, f32[4,88,128]{2,1,0:T(8,128)S(1)}, u32[]{:S(2)}, u32[]{:S(2)}) collective-permute-start(f32[4,88,128]{2,1,0:T(8,128)S(1)} %get-tuple-element.40), channel_id=1, source_target_pairs={{0,6},{2,4},{4,2},{6,0},{1,7},{3,5},{5,3},{7,1},{8,14},{10,12},{12... | collective-permute-start | bytes 540680 | tf_op jit(solution)/shard_map/ppermute | solution.py:29
  86.3 1.5 %collective-permute-start.13 = (f32[4,88,128]{2,1,0:T(8,128)S(1)}, f32[4,88,128]{2,1,0:T(8,128)S(1)}, u32[]{:S(2)}, u32[]{:S(2)}) collective-permute-start(f32[4,88,128]{2,1,0:T(8,128)S(1)} %get-tuple-element.41), channel_id=1, source_target_pairs={{0,2},{2,0},{4,6},{6,4},{1,3},{3,1},{5,7},{7,5},{8,10},{10,8},{12,... | collective-permute-start | bytes 540680 | tf_op jit(solution)/shard_map/ppermute | solution.py:29
  87.8 3.9 %collective-permute-done.14 = f32[4,88,128]{2,1,0:T(8,128)S(1)} collective-permute-done((f32[4,88,128]{2,1,0:T(8,128)S(1)}, f32[4,88,128]{2,1,0:T(8,128)S(1)}, u32[]{:S(2)}, u32[]{:S(2)}) %collective-permute-start.14) | collective-permute-done | bytes 180256 | tf_op jit(solution)/shard_map/ppermute | solution.py:29
  91.8 3.1 %collective-permute-done.15 = f32[4,88,128]{2,1,0:T(8,128)S(1)} collective-permute-done((f32[4,88,128]{2,1,0:T(8,128)S(1)}, f32[4,88,128]{2,1,0:T(8,128)S(1)}, u32[]{:S(2)}, u32[]{:S(2)}) %collective-permute-start.15) | collective-permute-done | bytes 180256 | tf_op jit(solution)/shard_map/ppermute | solution.py:29
  94.8 1.4 %collective-permute-done.13 = f32[4,88,128]{2,1,0:T(8,128)S(1)} collective-permute-done((f32[4,88,128]{2,1,0:T(8,128)S(1)}, f32[4,88,128]{2,1,0:T(8,128)S(1)}, u32[]{:S(2)}, u32[]{:S(2)}) %collective-permute-start.13) | collective-permute-done | bytes 180256 | tf_op jit(solution)/shard_map/ppermute | solution.py:29
  96.3 0.1 collective-permute-start.18
  96.3 0.1 collective-permute-start.17
  96.4 4.3 %collective-permute-start.16 = (f32[88,128]{1,0:T(8,128)S(1)}, f32[88,128]{1,0:T(8,128)S(1)}, u32[]{:S(2)}, u32[]{:S(2)}) collective-permute-start(f32[88,128]{1,0:T(8,128)S(1)} %get-tuple-element.44), channel_id=1, source_target_pairs={{0,8},{8,0},{16,24},{24,16},{1,9},{9,1},{17,25},{25,17},{2,10},{10... | collective-permute-start | bytes 135176 | tf_op jit(solution)/shard_map/ppermute | solution.py:29
  100.7 1.5 %collective-permute-done.18.refs_3_ = f32[88,128]{1,0:T(8,128)S(1)} collective-permute-done((f32[88,128]{1,0:T(8,128)S(1)}, f32[88,128]{1,0:T(8,128)S(1)}, u32[]{:S(2)}, u32[]{:S(2)}) %collective-permute-start.18) | collective-permute-done | bytes 45088 | tf_op jit(solution)/shard_map/ppermute | solution.py:29
  102.2 0.0 collective-permute-done.17.refs_2_
  102.2 0.6 collective-permute-done.16.refs_1_
  102.7 0.0 copy-done.4
  102.7 3.1 %final.1 = f32[3,16384]{1,0:T(4,128)} custom-call(s32[12]{0:T(128)S(1)} %copy-done.4, f32[12,3,128]{2,1,0:T(4,128)S(1)} %pad_maximum_fusion.1.near, f32[27,16384]{1,0:T(8,128)S(1)} %copy-done.1, f32[88,128]{1,0:T(8,128)S(1)} %get-tuple-element.45.refs_0_, f32[88,128]{1,0:T(8,128)S(1)} %collective-permute-done.16.refs_1_, ...), custom_call_target="tpu_custom_call" | custom-call | tf_op jit(solution)/shard_map/final/pallas_call | solution.py:544
  (12 shorter events, 0.1 us)
Async XLA Ops:
  0.0 15.9 %copy-start = (bf16[12,3,3,128,128]{4,3,2,1,0:T(8,128)(2,1)S(1)}, bf16[12,3,3,128,128]{4,3,2,1,0:T(8,128)(2,1)}, u32[]{:S(2)}) copy-start(bf16[12,3,3,128,128]{4,3,2,1,0:T(8,128)(2,1)} %param.14) | copy-start | bytes 10616836
  5.2 12.0 %collective-permute-start.2 = (f32[88,128]{1,0:T(8,128)}, f32[88,128]{1,0:T(8,128)}, u32[]{:S(2)}, u32[]{:S(2)}) collective-permute-start(f32[88,128]{1,0:T(8,128)} %spread.1), channel_id=1, source_target_pairs={{0,24},{8,16},{16,8},{24,0},{1,25},{9,17},{17,9},{25,1},{2,26},{10... | collective-permute-start | bytes 135176 | tf_op jit(solution)/shard_map/ppermute | solution.py:29
  10.3 6.9 %collective-permute-start.1 = (f32[88,128]{1,0:T(8,128)}, f32[88,128]{1,0:T(8,128)}, u32[]{:S(2)}, u32[]{:S(2)}) collective-permute-start(f32[88,128]{1,0:T(8,128)} %spread.1), channel_id=1, source_target_pairs={{0,16},{8,24},{16,0},{24,8},{1,17},{9,25},{17,1},{25,9},{2,18},{10... | collective-permute-start | bytes 135176 | tf_op jit(solution)/shard_map/ppermute | solution.py:29
  10.3 6.9 %collective-permute-start = (f32[88,128]{1,0:T(8,128)}, f32[88,128]{1,0:T(8,128)}, u32[]{:S(2)}, u32[]{:S(2)}) collective-permute-start(f32[88,128]{1,0:T(8,128)} %spread.1), channel_id=1, source_target_pairs={{0,8},{8,0},{16,24},{24,16},{1,9},{9,1},{17,25},{25,17},{2,10},{10... | collective-permute-start | bytes 135176 | tf_op jit(solution)/shard_map/ppermute | solution.py:29
  15.8 0.7 copy-start.6
  15.9 1.4 %copy-start.5 = (f32[88,128]{1,0:T(8,128)S(1)}, f32[88,128]{1,0:T(8,128)}, u32[]{:S(2)}) copy-start(f32[88,128]{1,0:T(8,128)} %spread.1) | copy-start | bytes 135172
  18.7 6.0 %collective-permute-start.3 = (f32[4,88,128]{2,1,0:T(8,128)}, f32[4,88,128]{2,1,0:T(8,128)}, u32[]{:S(2)}, u32[]{:S(2)}) collective-permute-start(f32[4,88,128]{2,1,0:T(8,128)} %pad_maximum_fusion.refs_0_), channel_id=1, source_target_pairs={{0,2},{2,0},{4,6},{6,4},{1,3},{3,1},{5,7},{7,5},{8,10},{10,8},{12,... | collective-permute-start | bytes 540680 | tf_op jit(solution)/shard_map/ppermute | solution.py:29
  20.5 7.4 %collective-permute-start.4 = (f32[4,88,128]{2,1,0:T(8,128)}, f32[4,88,128]{2,1,0:T(8,128)}, u32[]{:S(2)}, u32[]{:S(2)}) collective-permute-start(f32[4,88,128]{2,1,0:T(8,128)} %pad_maximum_fusion.refs_0_), channel_id=1, source_target_pairs={{0,1},{1,0},{2,3},{3,2},{4,5},{5,4},{6,7},{7,6},{8,9},{9,8},{10,11... | collective-permute-start | bytes 540680 | tf_op jit(solution)/shard_map/ppermute | solution.py:29
  24.8 3.1 %collective-permute-start.5 = (f32[4,88,128]{2,1,0:T(8,128)}, f32[4,88,128]{2,1,0:T(8,128)}, u32[]{:S(2)}, u32[]{:S(2)}) collective-permute-start(f32[4,88,128]{2,1,0:T(8,128)} %collective-permute-done.3.refs_1_), channel_id=1, source_target_pairs={{0,1},{1,0},{2,3},{3,2},{4,5},{5,4},{6,7},{7,6},{8,9},{9,8},{10,11... | collective-permute-start | bytes 540680 | tf_op jit(solution)/shard_map/ppermute | solution.py:29
  24.8 11.2 %collective-permute-start.7 = (f32[4,88,128]{2,1,0:T(8,128)}, f32[4,88,128]{2,1,0:T(8,128)}, u32[]{:S(2)}, u32[]{:S(2)}) collective-permute-start(f32[4,88,128]{2,1,0:T(8,128)} %pad_maximum_fusion.refs_0_), channel_id=1, source_target_pairs={{0,6},{2,4},{4,2},{6,0},{1,7},{3,5},{5,3},{7,1},{8,14},{10,12},{12... | collective-permute-start | bytes 540680 | tf_op jit(solution)/shard_map/ppermute | solution.py:29
  27.2 9.6 %collective-permute-start.6 = (f32[4,88,128]{2,1,0:T(8,128)}, f32[4,88,128]{2,1,0:T(8,128)}, u32[]{:S(2)}, u32[]{:S(2)}) collective-permute-start(f32[4,88,128]{2,1,0:T(8,128)} %pad_maximum_fusion.refs_0_), channel_id=1, source_target_pairs={{0,4},{2,6},{4,0},{6,2},{1,5},{3,7},{5,1},{7,3},{8,12},{10,14},{12... | collective-permute-start | bytes 540680 | tf_op jit(solution)/shard_map/ppermute | solution.py:29
  37.6 5.9 %collective-permute-start.10 = (f32[4,3,128]{2,1,0:T(4,128)S(1)}, f32[4,3,128]{2,1,0:T(4,128)S(1)}, u32[]{:S(2)}, u32[]{:S(2)}) collective-permute-start(f32[4,3,128]{2,1,0:T(4,128)S(1)} %get-tuple-element.46), channel_id=1, source_target_pairs={{0,28},{4,0},{8,4},{12,8},{16,12},{20,16},{24,20},{28,24},{1,29},{... | collective-permute-start | bytes 18440 | tf_op jit(solution)/shard_map/ppermute | solution.py:38
  42.1 6.3 %collective-permute-start.11 = (f32[4,3,128]{2,1,0:T(4,128)S(1)}, f32[4,3,128]{2,1,0:T(4,128)S(1)}, u32[]{:S(2)}, u32[]{:S(2)}) collective-permute-start(f32[4,3,128]{2,1,0:T(4,128)S(1)} %get-tuple-element.47), channel_id=1, source_target_pairs={{0,4},{4,8},{8,12},{12,16},{16,20},{20,24},{24,28},{28,0},{1,5},{5... | collective-permute-start | bytes 18440 | tf_op jit(solution)/shard_map/ppermute | solution.py:38
  42.8 5.7 %collective-permute-start.8 = (f32[4,88,128]{2,1,0:T(8,128)}, f32[4,88,128]{2,1,0:T(8,128)S(1)}, u32[]{:S(2)}, u32[]{:S(2)}) collective-permute-start(f32[4,88,128]{2,1,0:T(8,128)} %collective-permute-done.6.refs_0_), channel_id=1, source_target_pairs={{0,1},{1,0},{2,3},{3,2},{4,5},{5,4},{6,7},{7,6},{8,9},{9,8},{10,11... | collective-permute-start | bytes 540680 | tf_op jit(solution)/shard_map/ppermute | solution.py:29
  42.8 5.7 %collective-permute-start.9 = (f32[4,88,128]{2,1,0:T(8,128)}, f32[4,88,128]{2,1,0:T(8,128)S(1)}, u32[]{:S(2)}, u32[]{:S(2)}) collective-permute-start(f32[4,88,128]{2,1,0:T(8,128)} %collective-permute-done.7.refs_1_), channel_id=1, source_target_pairs={{0,1},{1,0},{2,3},{3,2},{4,5},{5,4},{6,7},{7,6},{8,9},{9,8},{10,11... | collective-permute-start | bytes 540680 | tf_op jit(solution)/shard_map/ppermute | solution.py:29
  48.5 8.1 %copy-start.2 = (bf16[2,2,256,256]{3,2,1,0:T(8,128)(2,1)S(1)}, bf16[2,2,256,256]{3,2,1,0:T(8,128)(2,1)}, u32[]{:S(2)}) copy-start(bf16[2,2,256,256]{3,2,1,0:T(8,128)(2,1)} %constant.53.clone.refs_1_) | copy-start | bytes 1572868
  48.5 8.1 %copy-start.3 = (bf16[2,2,256,256]{3,2,1,0:T(8,128)(2,1)S(1)}, bf16[2,2,256,256]{3,2,1,0:T(8,128)(2,1)}, u32[]{:S(2)}) copy-start(bf16[2,2,256,256]{3,2,1,0:T(8,128)(2,1)} %constant.52.clone.refs_0_) | copy-start | bytes 1572868
  81.9 20.9 %copy-start.1 = (f32[27,16384]{1,0:T(8,128)S(1)}, f32[27,16384]{1,0:T(8,128)}, u32[]{:S(2)}) copy-start(f32[27,16384]{1,0:T(8,128)} %weights.3) | copy-start | bytes 5308420
  81.9 20.9 %copy-start.4 = (s32[12]{0:T(128)S(1)}, s32[12]{0:T(128)}, u32[]{:S(2)}) copy-start(s32[12]{0:T(128)} %landing.1) | copy-start | bytes 148
  81.9 2.3 %collective-permute-start.12 = (f32[2,2,4,88,128]{4,3,2,1,0:T(8,128)S(1)}, f32[2,2,4,88,128]{4,3,2,1,0:T(8,128)S(1)}, u32[]{:S(2)}, u32[]{:S(2)}) collective-permute-start(f32[2,2,4,88,128]{4,3,2,1,0:T(8,128)S(1)} %get-tuple-element.38), channel_id=1, source_target_pairs={{0,1},{1,0},{2,3},{3,2},{4,5},{5,4},{6,7},{7,6},{8,9},{9,8},{10,11... | collective-permute-start | bytes 2162696 | tf_op jit(solution)/shard_map/ppermute | solution.py:29
  84.3 7.5 %collective-permute-start.14 = (f32[4,88,128]{2,1,0:T(8,128)S(1)}, f32[4,88,128]{2,1,0:T(8,128)S(1)}, u32[]{:S(2)}, u32[]{:S(2)}) collective-permute-start(f32[4,88,128]{2,1,0:T(8,128)S(1)} %get-tuple-element.39), channel_id=1, source_target_pairs={{0,4},{2,6},{4,0},{6,2},{1,5},{3,7},{5,1},{7,3},{8,12},{10,14},{12... | collective-permute-start | bytes 540680 | tf_op jit(solution)/shard_map/ppermute | solution.py:29
  84.4 10.5 %collective-permute-start.15 = (f32[4,88,128]{2,1,0:T(8,128)S(1)}, f32[4,88,128]{2,1,0:T(8,128)S(1)}, u32[]{:S(2)}, u32[]{:S(2)}) collective-permute-start(f32[4,88,128]{2,1,0:T(8,128)S(1)} %get-tuple-element.40), channel_id=1, source_target_pairs={{0,6},{2,4},{4,2},{6,0},{1,7},{3,5},{5,3},{7,1},{8,14},{10,12},{12... | collective-permute-start | bytes 540680 | tf_op jit(solution)/shard_map/ppermute | solution.py:29
  86.3 9.9 %collective-permute-start.13 = (f32[4,88,128]{2,1,0:T(8,128)S(1)}, f32[4,88,128]{2,1,0:T(8,128)S(1)}, u32[]{:S(2)}, u32[]{:S(2)}) collective-permute-start(f32[4,88,128]{2,1,0:T(8,128)S(1)} %get-tuple-element.41), channel_id=1, source_target_pairs={{0,2},{2,0},{4,6},{6,4},{1,3},{3,1},{5,7},{7,5},{8,10},{10,8},{12,... | collective-permute-start | bytes 540680 | tf_op jit(solution)/shard_map/ppermute | solution.py:29
  96.3 5.9 %collective-permute-start.18 = (f32[88,128]{1,0:T(8,128)S(1)}, f32[88,128]{1,0:T(8,128)S(1)}, u32[]{:S(2)}, u32[]{:S(2)}) collective-permute-start(f32[88,128]{1,0:T(8,128)S(1)} %get-tuple-element.42), channel_id=1, source_target_pairs={{0,24},{8,16},{16,8},{24,0},{1,25},{9,17},{17,9},{25,1},{2,26},{10... | collective-permute-start | bytes 135176 | tf_op jit(solution)/shard_map/ppermute | solution.py:29
  96.3 5.8 %collective-permute-start.17 = (f32[88,128]{1,0:T(8,128)S(1)}, f32[88,128]{1,0:T(8,128)S(1)}, u32[]{:S(2)}, u32[]{:S(2)}) collective-permute-start(f32[88,128]{1,0:T(8,128)S(1)} %get-tuple-element.43), channel_id=1, source_target_pairs={{0,16},{8,24},{16,0},{24,8},{1,17},{9,25},{17,1},{25,9},{2,18},{10... | collective-permute-start | bytes 135176 | tf_op jit(solution)/shard_map/ppermute | solution.py:29
  96.4 6.3 %collective-permute-start.16 = (f32[88,128]{1,0:T(8,128)S(1)}, f32[88,128]{1,0:T(8,128)S(1)}, u32[]{:S(2)}, u32[]{:S(2)}) collective-permute-start(f32[88,128]{1,0:T(8,128)S(1)} %get-tuple-element.44), channel_id=1, source_target_pairs={{0,8},{8,0},{16,24},{24,16},{1,9},{9,1},{17,25},{25,17},{2,10},{10... | collective-permute-start | bytes 135176 | tf_op jit(solution)/shard_map/ppermute | solution.py:29
